TPU v7x, 32 devices: a whole 2x2x4 slice. The times are simulated.
32 devices in a mesh: dp: 4 (over y, x), seq: 2 (over core), mp: 4 (over z).
Axes of the slice: x: 2, y: 2, z: 4, core: 2. Of those that a mesh axis runs over, the one named last changes fastest.
Arguments:
- node_feats: bfloat16 [8, 512, 1024], P(('dp', 'seq'), 'mp'), may hold values from -6 to 6
- coords: bfloat16 [8, 3, 512], P(('dp', 'seq'), None, 'mp'), may hold values from -36 to 36
- neighbours: int32 [8, 512, 48], P(('dp', 'seq'), 'mp'), may hold values from 0 to 511, as said below
- counts: int32 [8], P(('dp', 'seq')), may hold values from 256 to 512, as said below
- w_near: bfloat16 [1024, 1024], replicated, may hold values from -0.1875 to 0.1875
- w_rbf: bfloat16 [16, 1024], replicated, may hold values from -3.59375 to 3.59375
- gen_gain: float32 [1024], replicated, may hold values from 0.1 to 1.9
- w_logit: bfloat16 [1024, 33], replicated, may hold values from -0.59765625 to 0.59765625
- embed_table: bfloat16 [33, 2560], replicated, may hold values from -6 to 6
- trunk_gain: float32 [2560], replicated, may hold values from 0.1 to 1.9
- w_up: bfloat16 [2560, 5120], P('seq', 'mp'), may hold values from -0.125 to 0.125
- w_down: bfloat16 [5120, 2560], P('mp', 'seq'), may hold values from -0.078125 to 0.078125
Outputs:
- trunk_out: bfloat16 [8, 512, 2560], P(('dp', 'seq'), 'mp')
Inputs may be any that keep to these rules, and one draw needn't show every extreme that they name: `neighbours`: each index lies in the residue's own block of 128 residues or in the block just before or after it; the 48 indices of a residue are distinct. Residues of a backbone at positions counts[b] and beyond are padding.
All inputs are finite; a program needn't handle non-finite values.
Results may differ from a plain program's by a relative error of at most 0.013.
Values may be sent and summed in bfloat16 or wider, within the bound.
No kernel may reach another device: no remote copies, remote signals or barrier semaphores. Data moves between devices by JAX's collectives and lax.ppermute only.
A program may use at most 128 MiB of HBM per device.

v0:
```python
import math

import jax
import jax.numpy as jnp
from jax import lax
from jax.sharding import PartitionSpec as P


def from_behind(value, axis, steps):
    count = lax.axis_size(axis)
    first, last = (max(0, -steps), min(count, count - steps))
    return lax.ppermute(value, axis, [(source, source + steps) for source in range(first, last)])


def layer_norm(values, gain_vec):
    centred = values - jnp.mean(values, axis=-1, keepdims=True)
    spread = jnp.mean(centred * centred, axis=-1, keepdims=True)
    return centred * lax.rsqrt(spread + 1e-05) * gain_vec


def radial_basis(distance, bins):
    centres = 2.0 + 20.0 / (bins - 1) * jnp.arange(bins, dtype=jnp.float32)
    scaled = (distance[..., None] - centres) / 1.25
    return jnp.exp(-scaled * scaled).astype(jnp.bfloat16)


def on_device(
    node_feats,
    coords,
    neighbours,
    counts,
    w_near,
    w_rbf,
    gen_gain,
    w_logit,
    embed_table,
    trunk_gain,
    w_up,
    w_down,
):
    backbones, residues, feature_dim = node_feats.shape
    neighbour_count = neighbours.shape[2]
    bins = w_rbf.shape[0]
    vocab_size, embed_dim = embed_table.shape
    block_index = lax.axis_index("mp")
    own_start = block_index * residues
    outgoing = (
        jnp.dot(
            node_feats.reshape(backbones * residues, feature_dim),
            w_near,
            preferred_element_type=jnp.float32,
        )
        .astype(jnp.bfloat16)
        .reshape(backbones, residues, feature_dim)
    )
    row_blocks = []
    coord_blocks = []
    for offset in (1, 0, -1):
        if offset == 0:
            got_rows, got_coords = (outgoing, coords)
        else:
            got_rows, got_coords = from_behind((outgoing, coords), "mp", offset)
        row_blocks.append(got_rows)
        coord_blocks.append(got_coords)
    near_window = jnp.concatenate(row_blocks, axis=1)
    coord_window = jnp.concatenate(coord_blocks, axis=2)
    window_first = (block_index - 1) * residues
    local_links = neighbours - window_first
    step_rows = math.gcd(residues, 32)
    step_count = residues // step_rows

    def one_backbone(bundle):
        near_rows, position_xyz, link_rows, residue_count = bundle
        own_xyz = position_xyz[:, residues : 2 * residues].astype(jnp.float32)
        own_blocks = jnp.moveaxis(own_xyz.reshape(3, step_count, step_rows), 1, 0)

        def one_block(pair):
            link_block, own_block = pair
            flat_links = link_block.reshape(-1)
            picked = jnp.take(near_rows, flat_links, axis=0, mode="clip")
            other_xyz = (
                jnp.take(position_xyz, flat_links, axis=1, mode="clip")
                .astype(jnp.float32)
                .reshape(3, step_rows, neighbour_count)
            )
            offsets_xyz = own_block[:, :, None] - other_xyz
            distance = jnp.sqrt(jnp.sum(offsets_xyz * offsets_xyz, axis=0))
            radial = radial_basis(distance, bins).reshape(step_rows * neighbour_count, bins)
            preact = jnp.dot(radial, w_rbf, preferred_element_type=jnp.float32) + picked.astype(
                jnp.float32
            )
            edge_act = jax.nn.gelu(preact, approximate=False)
            keep_mask = (flat_links + window_first < residue_count).astype(jnp.float32)
            return (
                jnp.sum(
                    (edge_act * keep_mask[:, None]).reshape(
                        step_rows, neighbour_count, feature_dim
                    ),
                    axis=1,
                )
                / 30.0
            )

        pieces = lax.map(
            one_block, (link_rows.reshape(step_count, step_rows, neighbour_count), own_blocks)
        )
        return pieces.reshape(residues, feature_dim)

    message = lax.map(one_backbone, (near_window, coord_window, local_links, counts))
    mixed_rows = layer_norm(node_feats.astype(jnp.float32) + message, gen_gain).astype(jnp.bfloat16)
    logits = jnp.dot(
        mixed_rows.reshape(-1, feature_dim), w_logit, preferred_element_type=jnp.float32
    )
    bounded = 8.0 * jnp.tanh(logits / 8.0)
    exponent = jnp.exp(bounded)
    probability = (exponent / jnp.sum(exponent, axis=-1, keepdims=True)).astype(jnp.bfloat16)
    valid_rows = (
        (own_start + jnp.arange(residues, dtype=jnp.int32))[None, :] < counts[:, None]
    ).astype(jnp.float32)
    soft_embed = (
        jnp.dot(probability, embed_table, preferred_element_type=jnp.float32).reshape(
            backbones, residues, embed_dim
        )
        * valid_rows[:, :, None]
    ).astype(jnp.bfloat16)
    padded_width = max(128, vocab_size)
    prob_major = jnp.swapaxes(probability.reshape(backbones, residues, vocab_size), 0, 1)
    prob_padded = jnp.pad(prob_major, ((0, 0), (0, 0), (0, padded_width - vocab_size)))
    all_probs = lax.all_gather(prob_padded, "mp", axis=0, tiled=True)
    table_padded = jnp.pad(embed_table, ((0, padded_width - vocab_size), (0, 0)))
    whole_rows = all_probs.shape[0]
    row_valid = (jnp.arange(whole_rows, dtype=jnp.int32)[:, None] < counts[None, :]).astype(
        jnp.float32
    )
    all_soft = (
        jnp.dot(
            all_probs.reshape(-1, padded_width), table_padded, preferred_element_type=jnp.float32
        ).reshape(whole_rows, backbones, embed_dim)
        * row_valid[:, :, None]
    ).astype(jnp.bfloat16)
    normed = layer_norm(all_soft.astype(jnp.float32), trunk_gain).astype(jnp.bfloat16)
    group_rows = normed.shape[0]
    trunk_rows = normed.reshape(-1, embed_dim)
    hidden_dim = w_up.shape[1]
    up_total = jnp.dot(
        trunk_rows,
        lax.all_gather(w_up, "seq", axis=0, tiled=True),
        preferred_element_type=jnp.float32,
    )
    inner_act = jax.nn.gelu(up_total, approximate=False).astype(jnp.bfloat16)
    down_full = lax.all_gather(w_down, "seq", axis=1, tiled=True)
    inner_blocks = inner_act.reshape(group_rows, backbones, hidden_dim)
    summed = lax.psum_scatter(
        jnp.dot(inner_blocks.reshape(-1, hidden_dim), down_full, preferred_element_type=jnp.float32)
        .reshape(residues * lax.axis_size("mp"), backbones, embed_dim)
        .astype(jnp.bfloat16),
        "mp",
        scatter_dimension=0,
        tiled=True,
    ).astype(jnp.float32)
    return (soft_embed.astype(jnp.float32) + jnp.swapaxes(summed, 0, 1)).astype(jnp.bfloat16)


def solution(mesh):
    placed = (
        P(("dp", "seq"), "mp", None),
        P(("dp", "seq"), None, "mp"),
        P(("dp", "seq"), "mp", None),
        P(("dp", "seq")),
        P(),
        P(),
        P(),
        P(),
        P(),
        P(),
        P("seq", "mp"),
        P("mp", "seq"),
    )
    return jax.shard_map(
        on_device,
        mesh=mesh,
        in_specs=placed,
        out_specs=P(("dp", "seq"), "mp", None),
        check_vma=False,
    )
```

profile of v0, /device:TPU:0, one launch (start us, length us, event | category | flops | bytes accessed | tf_op | source)
XLA Modules:
  0.0 267.1 jit_solution(9965270231793718681)
XLA Ops:
  8.6 4.9 %collective-permute-start.2 = (bf16[1,128,1024]{2,1,0:T(8,128)(2,1)S(1)}, bf16[1,128,1024]{2,1,0:T(8,128)(2,1)S(1)}, u32[]{:S(2)}, u32[]{:S(2)}) collective-permute-start(bf16[1,128,1024]{2,1,0:T(8,128)(2,1)S(1)} %fusion.78), channel_id=1, source_target_pairs={{0,1},{1,2},{2,3},{4,5},{5,6},{6,7},{8,9},{9,10},{10,11},{12,13},{... | collective-permute-start | bytes 786440 | tf_op jit(solution)/shard_map/ppermute | solution.py:12
  14.8 4.5 %collective-permute-start = (bf16[1,3,128]{2,1,0:T(4,128)(2,1)S(1)}, bf16[1,3,128]{2,1,0:T(4,128)(2,1)S(1)}, u32[]{:S(2)}, u32[]{:S(2)}) collective-permute-start(bf16[1,3,128]{2,1,0:T(4,128)(2,1)S(1)} %copy-done.7), channel_id=1, source_target_pairs={{0,1},{1,2},{2,3},{4,5},{5,6},{6,7},{8,9},{9,10},{10,11},{12,13},{... | collective-permute-start | bytes 2312 | tf_op jit(solution)/shard_map/ppermute | solution.py:12
  22.1 2.7 %collective-permute-done.1 = bf16[1,3,128]{2,1,0:T(4,128)(2,1)S(1)} collective-permute-done((bf16[1,3,128]{2,1,0:T(4,128)(2,1)S(1)}, bf16[1,3,128]{2,1,0:T(4,128)(2,1)S(1)}, u32[]{:S(2)}, u32[]{:S(2)}) %collective-permute-start.1) | collective-permute-done | bytes 800 | tf_op jit(solution)/shard_map/ppermute | solution.py:12
  27.0 139.7 %while.17 = (s32[]{:T(128)}, f32[4,32,1024]{2,1,0:T(8,128)}, f32[4,3,32]{2,1,0:T(4,128)S(1)}, s32[4,32,48]{2,1,0:T(8,128)S(1)}, bf16[3,384]{0,1:T(8,128)(2,1)S(1...) while((s32[]{:T(128)}, f32[4,32,1024]{2,1,0:T(8,128)}, ...), condition=%wide.region_3.4_spmd, body=%wide.region_0.3_spmd.sunk | while | flops 157432864 | bytes 22757020 | solution.py:104
  27.8 3.2 %gather_fusion.1 = bf16[1536,3]{1,0:T(8,128)(2,1)S(1)} fusion(bf16[3,384]{0,1:T(8,128)(2,1)S(1)} %get-tuple-element.206, s32[2048]{0:T(1024)S(1)} %pad_clamp_fusion.2), kind=kCustom, calls=%fused_computation.clone.1 | custom fusion | bytes 24576 | tf_op jit(solution)/shard_map/while/body/eval_jaxpr/while/body/eval_jaxpr/jit(_take)/gather | solution.py:82
  33.6 5.8 %gather_fusion = bf16[1536,1024]{1,0:T(8,128)(2,1)} fusion(bf16[384,1024]{1,0:T(8,128)(2,1)S(1)} %get-tuple-element.208, s32[2048]{0:T(1024)S(1)} %pad_clamp_fusion.2), kind=kCustom, calls=%fused_computation.1.clone.1 | custom fusion | bytes 6297600 | tf_op jit(solution)/shard_map/while/body/eval_jaxpr/while/body/eval_jaxpr/jit(_take)/gather | solution.py:80
  39.5 18.1 %fusion.138 = f32[1536,1024]{1,0:T(8,128)} fusion(bf16[1536,1024]{1,0:T(8,128)(2,1)} %gather_fusion, bf16[16,1024]{1,0:T(8,128)(2,1)S(1)} %copy-done.8, f32[1536]{0:T(1024)S(1)} %reshape.218, f32[16]{0:T(128)S(1)} %multiply_add_fusion.2, f32[1536]{0:T(1024)S(1)} %sqrt.13), kind=kOutput, calls=%fused_computation.5.clone.1 | convolution fusion | flops 155836416 | bytes 9482304 | tf_op jit(solution)/shard_map/while/body/eval_jaxpr/while/body/eval_jaxpr/dot_general | solution.py:89
  57.6 3.7 %reduce_sum.77 = f32[32,1024]{1,0:T(8,128)S(1)} reduce(f32[32,48,1024]{2,1,0:T(8,128)} %bitcast.67, f32[]{:T(128)} %constant.42.clone.3..sunk), dimensions={1}, to_apply=%region_2.2 | reduce | flops 1540096 | bytes 6422532 | tf_op jit(solution)/shard_map/while/body/eval_jaxpr/while/body/eval_jaxpr/reduce_sum | solution.py:95
  62.8 3.2 %gather_fusion.1 = bf16[1536,3]{1,0:T(8,128)(2,1)S(1)} fusion(bf16[3,384]{0,1:T(8,128)(2,1)S(1)} %get-tuple-element.206, s32[2048]{0:T(1024)S(1)} %pad_clamp_fusion.2), kind=kCustom, calls=%fused_computation.clone.1 | custom fusion | bytes 24576 | tf_op jit(solution)/shard_map/while/body/eval_jaxpr/while/body/eval_jaxpr/jit(_take)/gather | solution.py:82
  68.5 5.8 %gather_fusion = bf16[1536,1024]{1,0:T(8,128)(2,1)} fusion(bf16[384,1024]{1,0:T(8,128)(2,1)S(1)} %get-tuple-element.208, s32[2048]{0:T(1024)S(1)} %pad_clamp_fusion.2), kind=kCustom, calls=%fused_computation.1.clone.1 | custom fusion | bytes 6297600 | tf_op jit(solution)/shard_map/while/body/eval_jaxpr/while/body/eval_jaxpr/jit(_take)/gather | solution.py:80
  74.5 18.0 %fusion.138 = f32[1536,1024]{1,0:T(8,128)} fusion(bf16[1536,1024]{1,0:T(8,128)(2,1)} %gather_fusion, bf16[16,1024]{1,0:T(8,128)(2,1)S(1)} %copy-done.8, f32[1536]{0:T(1024)S(1)} %reshape.218, f32[16]{0:T(128)S(1)} %multiply_add_fusion.2, f32[1536]{0:T(1024)S(1)} %sqrt.13), kind=kOutput, calls=%fused_computation.5.clone.1 | convolution fusion | flops 155836416 | bytes 9482304 | tf_op jit(solution)/shard_map/while/body/eval_jaxpr/while/body/eval_jaxpr/dot_general | solution.py:89
  92.5 3.7 %reduce_sum.77 = f32[32,1024]{1,0:T(8,128)S(1)} reduce(f32[32,48,1024]{2,1,0:T(8,128)} %bitcast.67, f32[]{:T(128)} %constant.42.clone.3..sunk), dimensions={1}, to_apply=%region_2.2 | reduce | flops 1540096 | bytes 6422532 | tf_op jit(solution)/shard_map/while/body/eval_jaxpr/while/body/eval_jaxpr/reduce_sum | solution.py:95
  97.7 3.2 %gather_fusion.1 = bf16[1536,3]{1,0:T(8,128)(2,1)S(1)} fusion(bf16[3,384]{0,1:T(8,128)(2,1)S(1)} %get-tuple-element.206, s32[2048]{0:T(1024)S(1)} %pad_clamp_fusion.2), kind=kCustom, calls=%fused_computation.clone.1 | custom fusion | bytes 24576 | tf_op jit(solution)/shard_map/while/body/eval_jaxpr/while/body/eval_jaxpr/jit(_take)/gather | solution.py:82
  103.4 5.8 %gather_fusion = bf16[1536,1024]{1,0:T(8,128)(2,1)} fusion(bf16[384,1024]{1,0:T(8,128)(2,1)S(1)} %get-tuple-element.208, s32[2048]{0:T(1024)S(1)} %pad_clamp_fusion.2), kind=kCustom, calls=%fused_computation.1.clone.1 | custom fusion | bytes 6297600 | tf_op jit(solution)/shard_map/while/body/eval_jaxpr/while/body/eval_jaxpr/jit(_take)/gather | solution.py:80
  109.4 18.0 %fusion.138 = f32[1536,1024]{1,0:T(8,128)} fusion(bf16[1536,1024]{1,0:T(8,128)(2,1)} %gather_fusion, bf16[16,1024]{1,0:T(8,128)(2,1)S(1)} %copy-done.8, f32[1536]{0:T(1024)S(1)} %reshape.218, f32[16]{0:T(128)S(1)} %multiply_add_fusion.2, f32[1536]{0:T(1024)S(1)} %sqrt.13), kind=kOutput, calls=%fused_computation.5.clone.1 | convolution fusion | flops 155836416 | bytes 9482304 | tf_op jit(solution)/shard_map/while/body/eval_jaxpr/while/body/eval_jaxpr/dot_general | solution.py:89
  127.4 3.7 %reduce_sum.77 = f32[32,1024]{1,0:T(8,128)S(1)} reduce(f32[32,48,1024]{2,1,0:T(8,128)} %bitcast.67, f32[]{:T(128)} %constant.42.clone.3..sunk), dimensions={1}, to_apply=%region_2.2 | reduce | flops 1540096 | bytes 6422532 | tf_op jit(solution)/shard_map/while/body/eval_jaxpr/while/body/eval_jaxpr/reduce_sum | solution.py:95
  132.5 3.2 %gather_fusion.1 = bf16[1536,3]{1,0:T(8,128)(2,1)S(1)} fusion(bf16[3,384]{0,1:T(8,128)(2,1)S(1)} %get-tuple-element.206, s32[2048]{0:T(1024)S(1)} %pad_clamp_fusion.2), kind=kCustom, calls=%fused_computation.clone.1 | custom fusion | bytes 24576 | tf_op jit(solution)/shard_map/while/body/eval_jaxpr/while/body/eval_jaxpr/jit(_take)/gather | solution.py:82
  138.3 5.8 %gather_fusion = bf16[1536,1024]{1,0:T(8,128)(2,1)} fusion(bf16[384,1024]{1,0:T(8,128)(2,1)S(1)} %get-tuple-element.208, s32[2048]{0:T(1024)S(1)} %pad_clamp_fusion.2), kind=kCustom, calls=%fused_computation.1.clone.1 | custom fusion | bytes 6297600 | tf_op jit(solution)/shard_map/while/body/eval_jaxpr/while/body/eval_jaxpr/jit(_take)/gather | solution.py:80
  144.3 18.0 %fusion.138 = f32[1536,1024]{1,0:T(8,128)} fusion(bf16[1536,1024]{1,0:T(8,128)(2,1)} %gather_fusion, bf16[16,1024]{1,0:T(8,128)(2,1)S(1)} %copy-done.8, f32[1536]{0:T(1024)S(1)} %reshape.218, f32[16]{0:T(128)S(1)} %multiply_add_fusion.2, f32[1536]{0:T(1024)S(1)} %sqrt.13), kind=kOutput, calls=%fused_computation.5.clone.1 | convolution fusion | flops 155836416 | bytes 9482304 | tf_op jit(solution)/shard_map/while/body/eval_jaxpr/while/body/eval_jaxpr/dot_general | solution.py:89
  162.3 3.7 %reduce_sum.77 = f32[32,1024]{1,0:T(8,128)S(1)} reduce(f32[32,48,1024]{2,1,0:T(8,128)} %bitcast.67, f32[]{:T(128)} %constant.42.clone.3..sunk), dimensions={1}, to_apply=%region_2.2 | reduce | flops 1540096 | bytes 6422532 | tf_op jit(solution)/shard_map/while/body/eval_jaxpr/while/body/eval_jaxpr/reduce_sum | solution.py:95
  170.3 13.4 %all_gather.9 = bf16[512,1,128]{0,2,1:T(8,128)(2,1)S(1)} all-gather(bf16[128,1,128]{0,2,1:T(8,128)(2,1)S(1)} %pad.8), channel_id=1, replica_groups=mesh['dp'=4,'seq'=2,'mp'=4] {'mp'}, dimensions={0}, use_global_device_ids=true | all-gather | bytes 163840 | tf_op jit(solution)/shard_map/all_gather | solution.py:129
  188.0 19.4 %fusion.23 = bf16[512,1,2560]{2,0,1:T(8,128)(2,1)} fusion(bf16[1280,2560]{1,0:T(8,128)(2,1)} %all-gather.5.cloned.1.call-done, bf16[2560,1280]{1,0:T(8,128)(2,1)} %all-gather.3.cloned.1.call-done, bf16[512,2560]{1,0:T(8,128)(2,1)} %copy-done.1, f32[2560]{0:T(1024)S(1)} %copy-done.9, f32[512]{0:T(512)S(1)} %add_rsqrt_fusion, f32[512]{0:T(512)S(1)} %broadcast_multiply_fusion), kind=kOutput, calls=%fused_computation.46 | convolution fusion | flops 6761349120 | bytes 18364416 | tf_op jit(solution)/shard_map/dot_general | solution.py:154
  207.5 50.8 %reduce-scatter.2.cloned.1.call-done = bf16[128,1,2560]{2,0,1:T(8,128)(2,1)} async-done(((bf16[512,1,2560]{2,0,1:T(8,128)(2,1)}), bf16[128,1,2560]{2,0,1:T(8,128)(2,1)}) %reduce-scatter.2.cloned.1.call-update) | async-done | bytes 655376 | tf_op jit(solution)/shard_map/reduce_scatter | solution.py:153
  258.2 2.3 fusion.28
  (110 shorter events, 31.5 us)
Async XLA Ops:
  6.5 1.6 copy-start
  6.5 1.6 copy-start.2
  6.5 8.3 %copy-start.7 = (bf16[1,3,128]{2,1,0:T(4,128)(2,1)S(1)}, bf16[1,3,128]{2,1,0:T(4,128)(2,1)}, u32[]{:S(2)}) copy-start(bf16[1,3,128]{2,1,0:T(4,128)(2,1)} %param.15) | copy-start | bytes 2308
  6.5 181.4 %all-gather.3.cloned.1.call-start = ((), (), s32[]{:S(2)}) async-start(), calls=%async_computation.1 | async-start | bytes 9830400 | tf_op jit(solution)/shard_map/all_gather | solution.py:147
  7.3 14.2 %copy-start.6 = (s32[1,128,48]{1,2,0:T(8,128)S(1)}, s32[1,128,48]{1,2,0:T(8,128)}, u32[]{:S(2)}) copy-start(s32[1,128,48]{1,2,0:T(8,128)} %param.16) | copy-start | bytes 73732
  7.3 180.7 %all-gather.5.cloned.1.call-start = ((), (), s32[]{:S(2)}) async-start(), calls=%async_computation.2 | async-start | bytes 9830400 | tf_op jit(solution)/shard_map/all_gather | solution.py:151
  8.6 16.6 %collective-permute-start.2 = (bf16[1,128,1024]{2,1,0:T(8,128)(2,1)S(1)}, bf16[1,128,1024]{2,1,0:T(8,128)(2,1)S(1)}, u32[]{:S(2)}, u32[]{:S(2)}) collective-permute-start(bf16[1,128,1024]{2,1,0:T(8,128)(2,1)S(1)} %fusion.78), channel_id=1, source_target_pairs={{0,1},{1,2},{2,3},{4,5},{5,6},{6,7},{8,9},{9,10},{10,11},{12,13},{... | collective-permute-start | bytes 786440 | tf_op jit(solution)/shard_map/ppermute | solution.py:12
  13.5 12.4 %collective-permute-start.3 = (bf16[1,128,1024]{2,1,0:T(8,128)(2,1)S(1)}, bf16[1,128,1024]{2,1,0:T(8,128)(2,1)}, u32[]{:S(2)}, u32[]{:S(2)}) collective-permute-start(bf16[1,128,1024]{2,1,0:T(8,128)(2,1)S(1)} %fusion.78), channel_id=1, source_target_pairs={{1,0},{2,1},{3,2},{5,4},{6,5},{7,6},{9,8},{10,9},{11,10},{13,12},{... | collective-permute-start | bytes 786440 | tf_op jit(solution)/shard_map/ppermute | solution.py:12
  14.8 7.3 %collective-permute-start = (bf16[1,3,128]{2,1,0:T(4,128)(2,1)S(1)}, bf16[1,3,128]{2,1,0:T(4,128)(2,1)S(1)}, u32[]{:S(2)}, u32[]{:S(2)}) collective-permute-start(bf16[1,3,128]{2,1,0:T(4,128)(2,1)S(1)} %copy-done.7), channel_id=1, source_target_pairs={{0,1},{1,2},{2,3},{4,5},{5,6},{6,7},{8,9},{9,10},{10,11},{12,13},{... | collective-permute-start | bytes 2312 | tf_op jit(solution)/shard_map/ppermute | solution.py:12
  19.4 5.5 %collective-permute-start.1 = (bf16[1,3,128]{2,1,0:T(4,128)(2,1)S(1)}, bf16[1,3,128]{2,1,0:T(4,128)(2,1)S(1)}, u32[]{:S(2)}, u32[]{:S(2)}) collective-permute-start(bf16[1,3,128]{2,1,0:T(4,128)(2,1)S(1)} %copy-done.7), channel_id=1, source_target_pairs={{1,0},{2,1},{3,2},{5,4},{6,5},{7,6},{9,8},{10,9},{11,10},{13,12},{... | collective-permute-start | bytes 2312 | tf_op jit(solution)/shard_map/ppermute | solution.py:12
  20.7 237.5 %reduce-scatter.2.cloned.1.call-start = ((), (), s32[]{:S(2)}) async-start(), calls=%async_computation.3 | async-start | bytes 3276800 | tf_op jit(solution)/shard_map/reduce_scatter | solution.py:153
  25.2 0.7 copy-start.3
  27.0 142.3 %copy-start.5 = (bf16[1024,33]{0,1:T(8,128)(2,1)S(1)}, bf16[1024,33]{0,1:T(8,128)(2,1)}, u32[]{:S(2)}) copy-start(bf16[1024,33]{0,1:T(8,128)(2,1)} %param.21) | copy-start | bytes 202756
  33.6 5.9 %copy-start.8 = (bf16[16,1024]{1,0:T(8,128)(2,1)S(1)}, bf16[16,1024]{1,0:T(8,128)(2,1)}, u32[]{:S(2)}) copy-start(bf16[16,1024]{1,0:T(8,128)(2,1)} %get-tuple-element.207) | copy-start | bytes 98308 | tf_op jit(solution)/shard_map/while/body/eval_jaxpr/while
  68.5 5.9 %copy-start.8 = (bf16[16,1024]{1,0:T(8,128)(2,1)S(1)}, bf16[16,1024]{1,0:T(8,128)(2,1)}, u32[]{:S(2)}) copy-start(bf16[16,1024]{1,0:T(8,128)(2,1)} %get-tuple-element.207) | copy-start | bytes 98308 | tf_op jit(solution)/shard_map/while/body/eval_jaxpr/while
  103.4 5.9 %copy-start.8 = (bf16[16,1024]{1,0:T(8,128)(2,1)S(1)}, bf16[16,1024]{1,0:T(8,128)(2,1)}, u32[]{:S(2)}) copy-start(bf16[16,1024]{1,0:T(8,128)(2,1)} %get-tuple-element.207) | copy-start | bytes 98308 | tf_op jit(solution)/shard_map/while/body/eval_jaxpr/while
  138.3 5.9 %copy-start.8 = (bf16[16,1024]{1,0:T(8,128)(2,1)S(1)}, bf16[16,1024]{1,0:T(8,128)(2,1)}, u32[]{:S(2)}) copy-start(bf16[16,1024]{1,0:T(8,128)(2,1)} %get-tuple-element.207) | copy-start | bytes 98308 | tf_op jit(solution)/shard_map/while/body/eval_jaxpr/while
  183.7 4.3 %copy-start.9 = (f32[2560]{0:T(1024)S(1)}, f32[2560]{0:T(1024)}, u32[]{:S(2)}) copy-start(f32[2560]{0:T(1024)} %param.23) | copy-start | bytes 30724
  185.6 1.5 copy-start.1
  187.9 70.3 %copy-start.4 = (bf16[33,2560]{1,0:T(8,128)(2,1)S(1)}, bf16[33,2560]{1,0:T(8,128)(2,1)}, u32[]{:S(2)}) copy-start(bf16[33,2560]{1,0:T(8,128)(2,1)} %param.22) | copy-start | bytes 506884
Sparse Core Ops, SparseCore 0:
  8.9 19.8 all-gather.2
  30.3 18.3 all-gather.4
  207.6 50.6 reduce-scatter.1
where the time goes:
time: 268 us; the launch traced here: 267 us
  matrix products  97.2 us (36%)
  waiting for transfers between devices  54.3 us (20%)
  local copies, waits for them, and re-layouts  40.9 us (15%)
  other arithmetic  34.9 us (13%)
  between operations  14 us (5%)
  blocking collectives  13.4 us (5%)
  starting transfers between devices  12.2 us (5%)
    dot_general x4, matrix products, one_block(): jnp.dot(radial, w_rbf, preferred_element_type=jnp.float32)  72.2 us
    reduce_scatter x1, waiting for transfers between devices, on_device(): lax.psum_scatter(jnp.dot(inner_blocks.reshape(-1, hidden_dim), down_full,...  50.8 us
    gather x4, local copies, waits for them, and re-layouts, one_block(): picked = jnp.take(near_rows, flat_links, axis=0, mode='clip')  23.4 us
    dot_general x1, matrix products, on_device(): jnp.dot(inner_blocks.reshape(-1, hidden_dim), down_full, preferred_elemen...  19.4 us
    reduce_sum x4, other arithmetic, one_block(): jnp.sum((edge_act * keep_mask[:, None]).reshape(step_rows, neighbour_coun...  14.9 us
    all_gather x1, blocking collectives, on_device(): all_probs = lax.all_gather(prob_padded, 'mp', axis=0, tiled=True)  13.4 us
    gather x4, local copies, waits for them, and re-layouts, one_block(): jnp.take(position_xyz, flat_links, axis=1, mode='clip').astype(jnp.float32)  12.8 us
    ppermute x4, starting transfers between devices, from_behind(): lax.ppermute(value, axis, [(source, source + steps) for source in range(f...  12.1 us
  transfers between devices with their start and end apart: 7, of which 2 were waited for; matrix products, arithmetic and copies ran while one was open for 56% of the time, Pallas kernels for 0%

commit v1 on v0

v1 whole, which is shorter than its diff:
```python
import functools

import jax
import jax.numpy as jnp
from jax import lax
from jax.experimental import pallas as pl
from jax.experimental.pallas import tpu as pltpu
from jax.sharding import PartitionSpec as P

F32 = jnp.float32
BF16 = jnp.bfloat16
LANES = 128
COORD_ROWS = 16


def swap(value, axis, step):
    count = lax.axis_size(axis)
    return lax.ppermute(value, axis, [(i, i ^ step) for i in range(count)])


def high_low(value):
    high = value.astype(BF16)
    low = (value - high.astype(F32)).astype(BF16)
    return high, low


def message_kernel(
    rows_at_once,
    vocab_size,
    own_ref,
    side_ref,
    other_ref,
    link_ref,
    scalar_ref,
    w_near_ref,
    w_rbf_ref,
    gain_ref,
    w_logit_ref,
    table_ref,
    soft_ref,
    coded_ref,
    window_ref,
    xyz_ref,
    message_ref,
):
    residues, neighbour_count = link_ref.shape
    feature_dim = w_near_ref.shape[0]
    bins = w_rbf_ref.shape[0]
    window = 3 * residues
    blocks = (own_ref, side_ref, other_ref)
    for slot, ref in enumerate(blocks):
        near = jnp.dot(ref[0:residues, :], w_near_ref[...], preferred_element_type=F32)
        window_ref[slot * residues : (slot + 1) * residues, :] = near.astype(BF16)
    window_ref[window : window + bins, :] = w_rbf_ref[...]
    window_ref[window + bins :, :] = jnp.zeros(
        (window_ref.shape[0] - window - bins, feature_dim), BF16
    )
    positions = [
        ref[residues : residues + COORD_ROWS, 0:residues].astype(F32) for ref in blocks
    ]
    xyz_ref[...] = jnp.transpose(
        jnp.concatenate([positions[0], jnp.zeros((LANES - COORD_ROWS, residues), F32)], axis=0)
    )
    block_index = scalar_ref[0]
    residue_count = scalar_ref[1]
    lane = lax.broadcasted_iota(jnp.int32, (rows_at_once, LANES), 1)
    centres = 2.0 + (20.0 / (bins - 1)) * lane.astype(F32)
    padding = jnp.zeros((rows_at_once, LANES - neighbour_count), jnp.int32)

    def one_chunk(step, carry):
        first = pl.multiple_of(step * rows_at_once, rows_at_once)
        links = jnp.concatenate([link_ref[pl.ds(first, rows_at_once), :], padding], axis=1)
        keep = (links < residue_count) & (lane < neighbour_count)
        within = jnp.bitwise_and(links, residues - 1)
        block_of = lax.shift_right_logical(links, residues.bit_length() - 1)
        side_block = jnp.bitwise_xor(block_index, 1)
        slot_of = jnp.where(
            block_of == block_index, 0, jnp.where(block_of == side_block, 1, 2)
        )
        own_xyz = xyz_ref[pl.ds(first, rows_at_once), :]
        squared = None
        for slot in range(3):
            total = None
            for axis in range(3):
                offset = own_xyz[:, axis : axis + 1] - positions[slot][axis : axis + 1, :]
                total = offset * offset if total is None else total + offset * offset
            picked = jnp.take_along_axis(total, within, axis=1)
            squared = picked if squared is None else jnp.where(slot_of == slot, picked, squared)
        distance = jnp.where(keep, jnp.sqrt(squared), 1e6)
        place = jnp.where(keep, within + slot_of * residues, -1)
        rows = []
        for k in range(neighbour_count):
            place_k = jnp.broadcast_to(place[:, k : k + 1], (rows_at_once, LANES))
            parts = [
                jnp.where(place_k == lane + slot * residues, 1.0, 0.0).astype(BF16)
                for slot in range(3)
            ]
            distance_k = jnp.broadcast_to(distance[:, k : k + 1], (rows_at_once, LANES))
            scaled = (distance_k - centres) * (1.0 / 1.25)
            radial = jnp.where(lane < bins, jnp.exp(-scaled * scaled), 0.0)
            parts.append(radial.astype(BF16))
            rows.append(jnp.concatenate(parts, axis=1))
        selector = jnp.concatenate(rows, axis=0)
        width = 256
        for column in range(feature_dim // width):
            cols = slice(column * width, (column + 1) * width)
            preact = jnp.dot(selector, window_ref[:, cols], preferred_element_type=F32)
            doubled = preact * (1.0 + lax.erf(preact * (0.5**0.5)))
            message_ref[pl.ds(first, rows_at_once), cols] = jnp.sum(
                doubled.reshape(neighbour_count, rows_at_once, width), axis=0
            ) * (0.5 / 30.0)
        return carry

    lax.fori_loop(0, residues // rows_at_once, one_chunk, 0)

    values = own_ref[0:residues, :].astype(F32) + message_ref[...]
    centred = values - jnp.mean(values, axis=1, keepdims=True)
    spread = jnp.mean(centred * centred, axis=1, keepdims=True)
    mixed = (centred * lax.rsqrt(spread + 1e-5) * gain_ref[...]).astype(BF16)
    logits = jnp.dot(mixed, w_logit_ref[...], preferred_element_type=F32)
    bounded = 8.0 * jnp.tanh(logits * 0.125)
    token = lax.broadcasted_iota(jnp.int32, logits.shape, 1)
    exponent = jnp.where(token < vocab_size, jnp.exp(bounded), 0.0)
    probability = (exponent / jnp.sum(exponent, axis=1, keepdims=True)).astype(BF16)
    residue = block_index * residues + lax.broadcasted_iota(jnp.int32, (residues, 1), 0)
    valid = (residue < residue_count).astype(F32)
    soft = (
        jnp.dot(probability, table_ref[...], preferred_element_type=F32) * valid
    ).astype(BF16)
    soft_ref[...] = soft
    soft_wide = soft.astype(F32)
    soft_centred = soft_wide - jnp.mean(soft_wide, axis=1, keepdims=True)
    soft_spread = jnp.mean(soft_centred * soft_centred, axis=1, keepdims=True)
    coded = probability.astype(F32) * (lax.rsqrt(soft_spread + 1e-5) * valid)
    high, low = high_low(coded)
    half = LANES // 2
    coded_ref[...] = jnp.concatenate([high[:, :half], low[:, :half]], axis=1)


def messages(own, side, other, links, scalars, w_near, w_rbf, gen_gain, w_logit, table, vocab):
    residues = links.shape[0]
    feature_dim = w_near.shape[0]
    embed_dim = table.shape[1]
    bins = w_rbf.shape[0]
    depth = -(-(3 * residues + bins) // 256) * 256
    in_vmem = pl.BlockSpec(memory_space=pltpu.VMEM)
    return pl.pallas_call(
        functools.partial(message_kernel, min(32, residues), vocab),
        out_shape=(
            jax.ShapeDtypeStruct((residues, embed_dim), BF16),
            jax.ShapeDtypeStruct((residues, LANES), BF16),
        ),
        in_specs=[in_vmem] * 4 + [pl.BlockSpec(memory_space=pltpu.SMEM)] + [in_vmem] * 5,
        out_specs=(in_vmem, in_vmem),
        scratch_shapes=[
            pltpu.VMEM((depth, feature_dim), BF16),
            pltpu.VMEM((residues, LANES), F32),
            pltpu.VMEM((residues, feature_dim), F32),
        ],
        compiler_params=pltpu.CompilerParams(vmem_limit_bytes=40 << 20),
        cost_estimate=pl.CostEstimate(
            flops=12_000_000_000, bytes_accessed=6_000_000, transcendentals=7_000_000
        ),
        name="messages",
    )(own, side, other, links, scalars, w_near, w_rbf, gen_gain, w_logit, table)


def on_device(
    node_feats,
    coords,
    neighbours,
    counts,
    w_near,
    w_rbf,
    gen_gain,
    w_logit,
    embed_table,
    trunk_gain,
    w_up,
    w_down,
):
    backbones, residues, feature_dim = node_feats.shape
    assert backbones == 1 and lax.axis_size("mp") == 4
    vocab_size, embed_dim = embed_table.shape
    half = LANES // 2
    seq_count = lax.axis_size("seq")
    seq_index = lax.axis_index("seq")
    block_index = lax.axis_index("mp")

    xyz = jnp.pad(coords[0], ((0, COORD_ROWS - 3), (0, feature_dim - residues)))
    own = jnp.concatenate([node_feats[0], xyz], axis=0)
    side = swap(own, "mp", 1)
    other = lax.ppermute(own, "mp", [(1, 2), (2, 1)])

    table_wide = embed_table.astype(F32)
    table_centred = table_wide - jnp.mean(table_wide, axis=1, keepdims=True)
    table_scaled = jnp.pad(
        (table_centred * trunk_gain).astype(BF16), ((0, half - vocab_size), (0, 0))
    )
    table_part = lax.dynamic_slice_in_dim(
        table_scaled, seq_index * w_up.shape[0], w_up.shape[0], 1
    )
    token_up = jnp.dot(table_part, w_up, preferred_element_type=F32)
    if seq_count == 2:
        token_up = token_up + swap(token_up, "seq", 1)
        down_parts = [w_down, swap(w_down, "seq", 1)]
    else:
        token_up = lax.psum(token_up, "seq")
        down_parts = [lax.all_gather(w_down, "seq", axis=1, tiled=True)]
    up_high, up_low = high_low(token_up)
    up_stack = jnp.concatenate([up_high, up_high, up_low, up_low], axis=0)

    scalars = jnp.stack([block_index.astype(jnp.int32), counts[0]])
    soft, coded = messages(
        own,
        side,
        other,
        neighbours[0],
        scalars,
        w_near,
        w_rbf,
        gen_gain[None, :],
        jnp.pad(w_logit, ((0, 0), (0, LANES - vocab_size))),
        jnp.pad(embed_table, ((0, LANES - vocab_size), (0, 0))),
        vocab_size,
    )

    coded_rows = [coded] + [swap(coded, "mp", step) for step in (1, 2, 3)]

    def inner_of(rows):
        wide = jnp.concatenate([rows, rows], axis=1)
        total = jnp.dot(wide, up_stack, preferred_element_type=F32)
        return jax.nn.gelu(total, approximate=False).astype(BF16)

    inner = [inner_of(rows) for rows in coded_rows]

    def product(step, part):
        return jnp.dot(inner[step], part, preferred_element_type=F32)

    inward = [(0, 1), (3, 2)]
    middle = [(1, 2), (2, 1)]
    outward = [(1, 0), (2, 3)]
    sums = []
    for part in down_parts:
        far_edge = lax.ppermute(product(3, part).astype(BF16), "mp", inward)
        far_near = lax.ppermute(product(2, part).astype(BF16), "mp", inward)
        to_inner = lax.ppermute(product(1, part).astype(BF16), "mp", inward)
        crossing_edge = lax.ppermute(
            (product(2, part) + far_edge.astype(F32)).astype(BF16), "mp", middle
        )
        crossing_near = lax.ppermute(
            (product(3, part) + far_near.astype(F32)).astype(BF16), "mp", middle
        )
        to_edge = lax.ppermute(
            (product(1, part) + crossing_edge.astype(F32)).astype(BF16), "mp", outward
        )
        sums.append(
            product(0, part)
            + to_inner.astype(F32)
            + crossing_near.astype(F32)
            + to_edge.astype(F32)
        )
    if seq_count == 2:
        first = seq_index == 0
        total = jnp.concatenate(
            [jnp.where(first, sums[0], sums[1]), jnp.where(first, sums[1], sums[0])], axis=1
        )
    else:
        total = sums[0]
    return (soft.astype(F32) + total).astype(BF16)[None]


def solution(mesh):
    placed = (
        P(("dp", "seq"), "mp", None),
        P(("dp", "seq"), None, "mp"),
        P(("dp", "seq"), "mp", None),
        P(("dp", "seq")),
        P(),
        P(),
        P(),
        P(),
        P(),
        P(),
        P("seq", "mp"),
        P("mp", "seq"),
    )
    return jax.shard_map(
        on_device,
        mesh=mesh,
        in_specs=placed,
        out_specs=P(("dp", "seq"), "mp", None),
        check_vma=False,
    )
```

time: 268 us -> 113 us (0.42)
  matrix products: 97.2 us -> 28.2 us
  waiting for transfers between devices: 54.3 us -> 13.1 us
  local copies, waits for them, and re-layouts: 40.9 us -> 9.39 us
  starting transfers between devices: 12.2 us -> 41.5 us
  other arithmetic: 34.9 us -> 6.36 us
  blocking collectives: 13.4 us -> 0 us
  between operations: 14 us -> 1 us
  Pallas kernels: 0 us -> 12.7 us
    dot_general x9 -> x13, matrix products: 97.2 us -> 28.2 us  [the longest x8 20.6 us: product(): return jnp.dot(inner[step], part, preferred_element_type=F32)]
    reduce_scatter x1 -> x0, waiting for transfers between devices: 50.8 us -> none  [on_device(): lax.psum_scatter(jnp.dot(inner_blocks.reshape(-1, hidden_dim), down_full,...]
    gather x8 -> x0, local copies, waits for them, and re-layouts: 36.2 us -> none  [the longest x4 23.4 us: one_block(): picked = jnp.take(near_rows, flat_links, axis=0, mode='clip')]
    ppermute x4 -> x19, starting transfers between devices: 12.1 us -> 41.5 us  [the longest x2 14.1 us: on_device(): to_inner = lax.ppermute(product(1, part).astype(BF16), 'mp', inward)]
    reduce_sum x11 -> x1, other arithmetic: 23.9 us -> 1.06 us  [on_device(): table_centred = table_wide - jnp.mean(table_wide, axis=1, keepdims=True)]
    all_gather x1 -> x0, blocking collectives: 13.4 us -> none  [on_device(): all_probs = lax.all_gather(prob_padded, 'mp', axis=0, tiled=True)]
    pallas_call x0 -> x1, Pallas kernels: none -> 12.7 us  [messages(): pl.pallas_call(functools.partial(message_kernel, min(32, residues), vocab...]
    ppermute x4 -> x19, waiting for transfers between devices: 2.72 us -> 13.1 us  [the longest x2 4.43 us: on_device(): far_edge = lax.ppermute(product(3, part).astype(BF16), 'mp', inward)]
  transfers between devices with their start and end apart: 7 -> 19, of which waited for: 2 -> 4; matrix products, arithmetic and copies ran while one was open for 56% -> 30% of each run, Pallas kernels for 0% -> 11%
where the time goes in v1:
time: 113 us; the launch traced here: 112 us
  starting transfers between devices  41.5 us (37%)
  matrix products  28.2 us (25%)
  waiting for transfers between devices  13.1 us (12%)
  Pallas kernels  12.7 us (11%)
  local copies, waits for them, and re-layouts  9.39 us (8%)
  other arithmetic  6.36 us (6%)
    dot_general x8, matrix products, product(): return jnp.dot(inner[step], part, preferred_element_type=F32)  20.6 us
    ppermute x2, starting transfers between devices, on_device(): to_inner = lax.ppermute(product(1, part).astype(BF16), 'mp', inward)  14.1 us
    pallas_call x1, Pallas kernels, messages(): pl.pallas_call(functools.partial(message_kernel, min(32, residues), vocab...  12.7 us
    ppermute x6, starting transfers between devices, swap(): return lax.ppermute(value, axis, [(i, i ^ step) for i in range(count)])  9.59 us
    unnamed x16, local copies, waits for them, and re-layouts  7.51 us
    dot_general x4, matrix products, inner_of(): total = jnp.dot(wide, up_stack, preferred_element_type=F32)  6.16 us
    ppermute x2, starting transfers between devices, on_device(): far_edge = lax.ppermute(product(3, part).astype(BF16), 'mp', inward)  5.71 us
    ppermute x2, starting transfers between devices, on_device(): far_near = lax.ppermute(product(2, part).astype(BF16), 'mp', inward)  5.44 us
  transfers between devices with their start and end apart: 19, of which 4 were waited for; matrix products, arithmetic and copies ran while one was open for 30% of the time, Pallas kernels for 11%

profile of v1, /device:TPU:0, one launch (start us, length us, event | category | flops | bytes accessed | tf_op | source)
XLA Modules:
  0.0 112.3 jit_solution(10168216805874000475)
XLA Ops:
  0.0 1.9 %fusion.47.own_ref = bf16[144,1024]{1,0:T(8,128)(2,1)} fusion(bf16[3,128]{1,0:T(4,128)(2,1)} %bitcast.27, bf16[128,1024]{1,0:T(8,128)(2,1)} %bitcast.26), kind=kLoop, calls=%fused_computation.100 | loop fusion | flops 884736 | bytes 557824 | tf_op jit(solution)/shard_map/concatenate | solution.py:191
  1.9 3.0 %collective-permute-start = (bf16[144,1024]{1,0:T(8,128)(2,1)}, bf16[144,1024]{1,0:T(8,128)(2,1)}, u32[]{:S(2)}, u32[]{:S(2)}) collective-permute-start(bf16[144,1024]{1,0:T(8,128)(2,1)} %fusion.47.own_ref), channel_id=1, source_target_pairs={{0,1},{1,0},{2,3},{3,2},{4,5},{5,4},{6,7},{7,6},{8,9},{9,8},{10,11... | collective-permute-start | bytes 884744 | tf_op jit(solution)/shard_map/ppermute | solution.py:18
  11.9 1.8 %copy.14 = bf16[1024,33]{1,0:T(8,128)(2,1)} copy(bf16[1024,33]{0,1:T(8,128)(2,1)} %param.19) | data formatting | bytes 135168 | tf_op args[7]
  18.2 1.6 %copy-done.3 = bf16[1024,1024]{1,0:T(8,128)(2,1)S(1)} copy-done((bf16[1024,1024]{1,0:T(8,128)(2,1)S(1)}, bf16[1024,1024]{1,0:T(8,128)(2,1)}, u32[]{:S(2)}) %copy-start.3) | copy-done | bytes 2097176
  20.5 12.7 %messages.1 = (bf16[128,2560]{1,0:T(8,128)(2,1)S(1)}, bf16[128,128]{1,0:T(8,128)(2,1)S(1)}) custom-call(bf16[144,1024]{1,0:T(8,128)(2,1)} %fusion.47.own_ref, bf16[144,1024]{1,0:T(8,128)(2,1)} %collective-permute-done.side_ref, bf16[144,1024]{1,0:T(8,128)(2,1)} %collective-permute-done.1.other_ref, s32[128,48]{1,0:T(8,128)S(1)} %bitcast.24, ...), custom_call_target="tpu_custom_call" | custom-call | flops 12000000000 | bytes 6000000 | tf_op jit(solution)/shard_map/messages/pallas_call | solution.py:147
  33.3 3.1 %collective-permute-start.6 = (bf16[128,128]{1,0:T(8,128)(2,1)S(1)}, bf16[128,128]{1,0:T(8,128)(2,1)S(1)}, u32[]{:S(2)}, u32[]{:S(2)}) collective-permute-start(bf16[128,128]{1,0:T(8,128)(2,1)S(1)} %get-tuple-element.8), channel_id=1, source_target_pairs={{0,2},{1,3},{2,0},{3,1},{4,6},{5,7},{6,4},{7,5},{8,10},{9,11},{10,... | collective-permute-start | bytes 98312 | tf_op jit(solution)/shard_map/ppermute | solution.py:18
  36.4 2.9 %collective-permute-start.5 = (bf16[128,128]{1,0:T(8,128)(2,1)S(1)}, bf16[128,128]{1,0:T(8,128)(2,1)S(1)}, u32[]{:S(2)}, u32[]{:S(2)}) collective-permute-start(bf16[128,128]{1,0:T(8,128)(2,1)S(1)} %get-tuple-element.8), channel_id=1, source_target_pairs={{0,3},{1,2},{2,1},{3,0},{4,7},{5,6},{6,5},{7,4},{8,11},{9,10},{10,... | collective-permute-start | bytes 98312 | tf_op jit(solution)/shard_map/ppermute | solution.py:18
  42.0 1.5 %fusion.14 = bf16[128,1280]{1,0:T(8,128)(2,1)S(1)} fusion(bf16[128,128]{1,0:T(8,128)(2,1)S(1)} %collective-permute-done.6, bf16[64,1280]{1,0:T(8,128)(2,1)S(1)} %get-tuple-element.20, bf16[64,1280]{1,0:T(8,128)(2,1)S(1)} %get-tuple-element.19), kind=kOutput, calls=%fused_computation.20 | convolution fusion | flops 97288192 | bytes 688128 | tf_op jit(solution)/shard_map/dot_general | solution.py:232
  43.5 2.6 %fusion.82 = (bf16[128,1280]{1,0:T(8,128)(2,1)S(1)}, f32[128,1280]{1,0:T(8,128)S(1)}) fusion(bf16[128,1280]{1,0:T(8,128)(2,1)S(1)} %fusion.14, bf16[1280,1280]{1,0:T(8,128)(2,1)} %param.23), kind=kOutput, calls=%fused_computation.130 | convolution fusion | flops 419594240 | bytes 4587520 | tf_op jit(solution)/shard_map/dot_general | solution.py:238
  46.1 4.1 %collective-permute-start.7 = (bf16[128,1280]{1,0:T(8,128)(2,1)S(1)}, bf16[128,1280]{1,0:T(8,128)(2,1)S(1)}, u32[]{:S(2)}, u32[]{:S(2)}) collective-permute-start(bf16[128,1280]{1,0:T(8,128)(2,1)S(1)} %get-tuple-element.23), channel_id=1, source_target_pairs={{0,1},{3,2},{4,5},{7,6},{8,9},{11,10},{12,13},{15,14},{16,17},{19,... | collective-permute-start | bytes 983048 | tf_op jit(solution)/shard_map/ppermute | solution.py:246
  50.2 1.5 %fusion.8 = bf16[128,1280]{1,0:T(8,128)(2,1)S(1)} fusion(bf16[128,128]{1,0:T(8,128)(2,1)S(1)} %collective-permute-done.3, bf16[64,1280]{1,0:T(8,128)(2,1)S(1)} %get-tuple-element.20, bf16[64,1280]{1,0:T(8,128)(2,1)S(1)} %get-tuple-element.19), kind=kOutput, calls=%fused_computation.14 | convolution fusion | flops 97288192 | bytes 688128 | tf_op jit(solution)/shard_map/dot_general | solution.py:232
  51.8 2.5 %fusion.84 = f32[128,1280]{1,0:T(8,128)S(1)} fusion(bf16[128,1280]{1,0:T(8,128)(2,1)S(1)} %fusion.8, bf16[1280,1280]{1,0:T(8,128)(2,1)} %param.23), kind=kOutput, calls=%fused_computation.132 | convolution fusion | flops 419430400 | bytes 4259840 | tf_op jit(solution)/shard_map/dot_general | solution.py:238
  55.9 2.6 %fusion.81 = (bf16[128,1280]{1,0:T(8,128)(2,1)S(1)}, f32[128,1280]{1,0:T(8,128)S(1)}) fusion(bf16[128,1280]{1,0:T(8,128)(2,1)S(1)} %fusion.14, bf16[1280,1280]{1,0:T(8,128)(2,1)} %collective-permute-done.12), kind=kOutput, calls=%fused_computation.129 | convolution fusion | flops 419594240 | bytes 4587520 | tf_op jit(solution)/shard_map/dot_general | solution.py:238
  59.8 2.6 %add_convert_fusion.5 = (bf16[128,1280]{1,0:T(8,128)(2,1)S(1)}, bf16[128,1280]{1,0:T(8,128)(2,1)S(1)}) fusion(bf16[128,1280]{1,0:T(8,128)(2,1)S(1)} %collective-permute-done.7, bf16[128,1280]{1,0:T(8,128)(2,1)S(1)} %fusion.11, bf16[1280,1280]{1,0:T(8,128)(2,1)} %param.23), kind=kOutput, calls=%fused_computation.29 | convolution fusion | flops 420085760 | bytes 4587520 | tf_op jit(solution)/shard_map/dot_general | solution.py:238
  64.4 3.5 %collective-permute-done.14 = bf16[128,1280]{1,0:T(8,128)(2,1)S(1)} collective-permute-done((bf16[128,1280]{1,0:T(8,128)(2,1)S(1)}, bf16[128,1280]{1,0:T(8,128)(2,1)S(1)}, u32[]{:S(2)}, u32[]{:S(2)}) %collective-permute-start.14) | collective-permute-done | bytes 327712 | tf_op jit(solution)/shard_map/ppermute | solution.py:246
  67.9 2.6 %add_convert_fusion.2 = (bf16[128,1280]{1,0:T(8,128)(2,1)S(1)}, bf16[128,1280]{1,0:T(8,128)(2,1)S(1)}) fusion(bf16[128,1280]{1,0:T(8,128)(2,1)S(1)} %collective-permute-done.14, bf16[128,1280]{1,0:T(8,128)(2,1)S(1)} %fusion.11, bf16[1280,1280]{1,0:T(8,128)(2,1)} %collective-permute-done.12), kind=kOutput, calls=%fused_computation.25 | convolution fusion | flops 420085760 | bytes 4587520 | tf_op jit(solution)/shard_map/dot_general | solution.py:238
  70.5 4.4 %collective-permute-start.16 = (bf16[128,1280]{1,0:T(8,128)(2,1)S(1)}, bf16[128,1280]{1,0:T(8,128)(2,1)S(1)}, u32[]{:S(2)}, u32[]{:S(2)}) collective-permute-start(bf16[128,1280]{1,0:T(8,128)(2,1)S(1)} %get-tuple-element.18), channel_id=1, source_target_pairs={{0,1},{3,2},{4,5},{7,6},{8,9},{11,10},{12,13},{15,14},{16,17},{19,... | collective-permute-start | bytes 983048 | tf_op jit(solution)/shard_map/ppermute | solution.py:245
  75.7 4.4 %collective-permute-done.16 = bf16[128,1280]{1,0:T(8,128)(2,1)S(1)} collective-permute-done((bf16[128,1280]{1,0:T(8,128)(2,1)S(1)}, bf16[128,1280]{1,0:T(8,128)(2,1)S(1)}, u32[]{:S(2)}, u32[]{:S(2)}) %collective-permute-start.16) | collective-permute-done | bytes 327712 | tf_op jit(solution)/shard_map/ppermute | solution.py:245
  82.2 9.2 %collective-permute-start.4 = (bf16[128,1280]{1,0:T(8,128)(2,1)S(1)}, bf16[128,1280]{1,0:T(8,128)(2,1)S(1)}, u32[]{:S(2)}, u32[]{:S(2)}) collective-permute-start(bf16[128,1280]{1,0:T(8,128)(2,1)S(1)} %get-tuple-element.11), channel_id=1, source_target_pairs={{0,1},{3,2},{4,5},{7,6},{8,9},{11,10},{12,13},{15,14},{16,17},{19,... | collective-permute-start | bytes 983048 | tf_op jit(solution)/shard_map/ppermute | solution.py:247
  92.1 2.5 %fusion.80 = (bf16[128,1280]{1,0:T(8,128)(2,1)S(1)}, bf16[128,1280]{1,0:T(8,128)(2,1)S(1)}) fusion(bf16[128,1280]{1,0:T(8,128)(2,1)S(1)} %collective-permute-done.17, bf16[128,1280]{1,0:T(8,128)(2,1)S(1)} %fusion.8, bf16[1280,1280]{1,0:T(8,128)(2,1)} %collective-permute-done.12), kind=kOutput, calls=%fused_computation.128 | convolution fusion | flops 420085760 | bytes 4587520 | tf_op jit(solution)/shard_map/dot_general | solution.py:238
  94.7 4.9 %collective-permute-start.13 = (bf16[128,1280]{1,0:T(8,128)(2,1)S(1)}, bf16[128,1280]{1,0:T(8,128)(2,1)S(1)}, u32[]{:S(2)}, u32[]{:S(2)}) collective-permute-start(bf16[128,1280]{1,0:T(8,128)(2,1)S(1)} %get-tuple-element.15), channel_id=1, source_target_pairs={{0,1},{3,2},{4,5},{7,6},{8,9},{11,10},{12,13},{15,14},{16,17},{19,... | collective-permute-start | bytes 983048 | tf_op jit(solution)/shard_map/ppermute | solution.py:247
  100.9 2.5 %fusion.83 = f32[128,1280]{1,0:T(8,128)S(1)} fusion(bf16[128,1280]{1,0:T(8,128)(2,1)S(1)} %fusion.5, bf16[1280,1280]{1,0:T(8,128)(2,1)} %param.23), kind=kOutput, calls=%fused_computation.131 | convolution fusion | flops 419430400 | bytes 4259840 | tf_op jit(solution)/shard_map/dot_general | solution.py:238
  104.2 4.4 %collective-permute-done.18 = bf16[128,1280]{1,0:T(8,128)(2,1)S(1)} collective-permute-done((bf16[128,1280]{1,0:T(8,128)(2,1)S(1)}, bf16[128,1280]{1,0:T(8,128)(2,1)S(1)}, u32[]{:S(2)}, u32[]{:S(2)}) %collective-permute-start.18) | collective-permute-done | bytes 327712 | tf_op jit(solution)/shard_map/ppermute | solution.py:254
  108.6 2.7 %broadcast_select_fusion.1 = (f32[128,1280]{1,0:T(8,128)S(1)}, f32[128,1280]{1,0:T(8,128)S(1)}) fusion(pred[]{:T(512)S(6)} %eq.3, bf16[128,1280]{1,0:T(8,128)(2,1)S(1)} %collective-permute-done.11, bf16[128,1280]{1,0:T(8,128)(2,1)S(1)} %collective-permute-done.8, f32[128,1280]{1,0:T(8,128)S(1)} %fusion.83, ...), kind=kOutput, calls=%fused_computation.99 | convolution fusion | flops 421724160 | bytes 7536641 | tf_op jit(solution)/shard_map/dot_general | solution.py:238
  (56 shorter events, 25.6 us)
Async XLA Ops:
  0.0 8.4 %copy-start = (bf16[1280,1280]{1,0:T(8,128)(2,1)S(1)}, bf16[1280,1280]{1,0:T(8,128)(2,1)}, u32[]{:S(2)}) copy-start(bf16[1280,1280]{1,0:T(8,128)(2,1)} %param.22) | copy-start | bytes 9830404
  1.9 14.4 %collective-permute-start = (bf16[144,1024]{1,0:T(8,128)(2,1)}, bf16[144,1024]{1,0:T(8,128)(2,1)}, u32[]{:S(2)}, u32[]{:S(2)}) collective-permute-start(bf16[144,1024]{1,0:T(8,128)(2,1)} %fusion.47.own_ref), channel_id=1, source_target_pairs={{0,1},{1,0},{2,3},{3,2},{4,5},{5,4},{6,7},{7,6},{8,9},{9,8},{10,11... | collective-permute-start | bytes 884744 | tf_op jit(solution)/shard_map/ppermute | solution.py:18
  4.9 11.4 %collective-permute-start.1 = (bf16[144,1024]{1,0:T(8,128)(2,1)}, bf16[144,1024]{1,0:T(8,128)(2,1)}, u32[]{:S(2)}, u32[]{:S(2)}) collective-permute-start(bf16[144,1024]{1,0:T(8,128)(2,1)} %fusion.47.own_ref), channel_id=1, source_target_pairs={{1,2},{2,1},{5,6},{6,5},{9,10},{10,9},{13,14},{14,13},{17,18},{18,... | collective-permute-start | bytes 884744 | tf_op jit(solution)/shard_map/ppermute | solution.py:193
  8.4 2.6 %copy-start.6 = (bf16[33,2560]{1,0:T(8,128)(2,1)S(1)}, bf16[33,2560]{1,0:T(8,128)(2,1)}, u32[]{:S(2)}) copy-start(bf16[33,2560]{1,0:T(8,128)(2,1)} %param.20) | copy-start | bytes 506884
  9.9 6.4 %copy-start.5 = (f32[1024]{0:T(1024)S(1)}, f32[1024]{0:T(1024)}, u32[]{:S(2)}) copy-start(f32[1024]{0:T(1024)} %param.18) | copy-start | bytes 12292
  9.9 29.4 %collective-permute-start.2 = (f32[64,1280]{1,0:T(8,128)}, f32[64,1280]{1,0:T(8,128)}, u32[]{:S(2)}, u32[]{:S(2)}) collective-permute-start(f32[64,1280]{1,0:T(8,128)} %fusion.48), channel_id=1, source_target_pairs={{0,4},{4,0},{1,5},{5,1},{2,6},{6,2},{3,7},{7,3},{8,12},{12,8},{9,1... | collective-permute-start | bytes 983048 | tf_op jit(solution)/shard_map/ppermute | solution.py:18
  9.9 46.0 %collective-permute-start.12 = (bf16[1280,1280]{1,0:T(8,128)(2,1)}, bf16[1280,1280]{1,0:T(8,128)(2,1)}, u32[]{:S(2)}, u32[]{:S(2)}) collective-permute-start(bf16[1280,1280]{1,0:T(8,128)(2,1)} %param.23), channel_id=1, source_target_pairs={{0,4},{4,0},{1,5},{5,1},{2,6},{6,2},{3,7},{7,3},{8,12},{12,8},{9,1... | collective-permute-start | bytes 9830408 | tf_op jit(solution)/shard_map/ppermute | solution.py:18
  16.2 1.1 copy-start.1
  18.2 1.6 %copy-start.3 = (bf16[1024,1024]{1,0:T(8,128)(2,1)S(1)}, bf16[1024,1024]{1,0:T(8,128)(2,1)}, u32[]{:S(2)}) copy-start(bf16[1024,1024]{1,0:T(8,128)(2,1)} %w_near_ref.1) | copy-start | bytes 6291460
  33.3 8.7 %collective-permute-start.6 = (bf16[128,128]{1,0:T(8,128)(2,1)S(1)}, bf16[128,128]{1,0:T(8,128)(2,1)S(1)}, u32[]{:S(2)}, u32[]{:S(2)}) collective-permute-start(bf16[128,128]{1,0:T(8,128)(2,1)S(1)} %get-tuple-element.8), channel_id=1, source_target_pairs={{0,2},{1,3},{2,0},{3,1},{4,6},{5,7},{6,4},{7,5},{8,10},{9,11},{10,... | collective-permute-start | bytes 98312 | tf_op jit(solution)/shard_map/ppermute | solution.py:18
  36.4 17.9 %collective-permute-start.5 = (bf16[128,128]{1,0:T(8,128)(2,1)S(1)}, bf16[128,128]{1,0:T(8,128)(2,1)S(1)}, u32[]{:S(2)}, u32[]{:S(2)}) collective-permute-start(bf16[128,128]{1,0:T(8,128)(2,1)S(1)} %get-tuple-element.8), channel_id=1, source_target_pairs={{0,3},{1,2},{2,1},{3,0},{4,7},{5,6},{6,5},{7,4},{8,11},{9,10},{10,... | collective-permute-start | bytes 98312 | tf_op jit(solution)/shard_map/ppermute | solution.py:18
  39.3 10.9 %collective-permute-start.3 = (bf16[128,128]{1,0:T(8,128)(2,1)S(1)}, bf16[128,128]{1,0:T(8,128)(2,1)S(1)}, u32[]{:S(2)}, u32[]{:S(2)}) collective-permute-start(bf16[128,128]{1,0:T(8,128)(2,1)S(1)} %get-tuple-element.8), channel_id=1, source_target_pairs={{0,1},{1,0},{2,3},{3,2},{4,5},{5,4},{6,7},{7,6},{8,9},{9,8},{10,11... | collective-permute-start | bytes 98312 | tf_op jit(solution)/shard_map/ppermute | solution.py:18
  46.1 13.7 %collective-permute-start.7 = (bf16[128,1280]{1,0:T(8,128)(2,1)S(1)}, bf16[128,1280]{1,0:T(8,128)(2,1)S(1)}, u32[]{:S(2)}, u32[]{:S(2)}) collective-permute-start(bf16[128,1280]{1,0:T(8,128)(2,1)S(1)} %get-tuple-element.23), channel_id=1, source_target_pairs={{0,1},{3,2},{4,5},{7,6},{8,9},{11,10},{12,13},{15,14},{16,17},{19,... | collective-permute-start | bytes 983048 | tf_op jit(solution)/shard_map/ppermute | solution.py:246
  58.5 9.4 %collective-permute-start.14 = (bf16[128,1280]{1,0:T(8,128)(2,1)S(1)}, bf16[128,1280]{1,0:T(8,128)(2,1)S(1)}, u32[]{:S(2)}, u32[]{:S(2)}) collective-permute-start(bf16[128,1280]{1,0:T(8,128)(2,1)S(1)} %get-tuple-element.21), channel_id=1, source_target_pairs={{0,1},{3,2},{4,5},{7,6},{8,9},{11,10},{12,13},{15,14},{16,17},{19,... | collective-permute-start | bytes 983048 | tf_op jit(solution)/shard_map/ppermute | solution.py:246
  62.4 12.5 %collective-permute-start.9 = (bf16[128,1280]{1,0:T(8,128)(2,1)S(1)}, bf16[128,1280]{1,0:T(8,128)(2,1)S(1)}, u32[]{:S(2)}, u32[]{:S(2)}) collective-permute-start(bf16[128,1280]{1,0:T(8,128)(2,1)S(1)} %get-tuple-element.14), channel_id=1, source_target_pairs={{0,1},{3,2},{4,5},{7,6},{8,9},{11,10},{12,13},{15,14},{16,17},{19,... | collective-permute-start | bytes 983048 | tf_op jit(solution)/shard_map/ppermute | solution.py:245
  63.7 35.9 %collective-permute-start.8 = (bf16[128,1280]{1,0:T(8,128)(2,1)S(1)}, bf16[128,1280]{1,0:T(8,128)(2,1)S(1)}, u32[]{:S(2)}, u32[]{:S(2)}) collective-permute-start(bf16[128,1280]{1,0:T(8,128)(2,1)S(1)} %get-tuple-element.13), channel_id=1, source_target_pairs={{1,2},{2,1},{5,6},{6,5},{9,10},{10,9},{13,14},{14,13},{17,18},{18,... | collective-permute-start | bytes 983048 | tf_op jit(solution)/shard_map/ppermute | solution.py:251
  70.5 9.6 %collective-permute-start.16 = (bf16[128,1280]{1,0:T(8,128)(2,1)S(1)}, bf16[128,1280]{1,0:T(8,128)(2,1)S(1)}, u32[]{:S(2)}, u32[]{:S(2)}) collective-permute-start(bf16[128,1280]{1,0:T(8,128)(2,1)S(1)} %get-tuple-element.18), channel_id=1, source_target_pairs={{0,1},{3,2},{4,5},{7,6},{8,9},{11,10},{12,13},{15,14},{16,17},{19,... | collective-permute-start | bytes 983048 | tf_op jit(solution)/shard_map/ppermute | solution.py:245
  75.0 5.9 %collective-permute-start.10 = (bf16[128,1280]{1,0:T(8,128)(2,1)S(1)}, bf16[128,1280]{1,0:T(8,128)(2,1)S(1)}, u32[]{:S(2)}, u32[]{:S(2)}) collective-permute-start(bf16[128,1280]{1,0:T(8,128)(2,1)S(1)} %add_convert_fusion.4), channel_id=1, source_target_pairs={{1,2},{2,1},{5,6},{6,5},{9,10},{10,9},{13,14},{14,13},{17,18},{18,... | collective-permute-start | bytes 983048 | tf_op jit(solution)/shard_map/ppermute | solution.py:248
  80.2 12.0 %collective-permute-start.17 = (bf16[128,1280]{1,0:T(8,128)(2,1)S(1)}, bf16[128,1280]{1,0:T(8,128)(2,1)S(1)}, u32[]{:S(2)}, u32[]{:S(2)}) collective-permute-start(bf16[128,1280]{1,0:T(8,128)(2,1)S(1)} %add_convert_fusion.1), channel_id=1, source_target_pairs={{1,2},{2,1},{5,6},{6,5},{9,10},{10,9},{13,14},{14,13},{17,18},{18,... | collective-permute-start | bytes 983048 | tf_op jit(solution)/shard_map/ppermute | solution.py:248
  80.9 22.5 %collective-permute-start.11 = (bf16[128,1280]{1,0:T(8,128)(2,1)S(1)}, bf16[128,1280]{1,0:T(8,128)(2,1)S(1)}, u32[]{:S(2)}, u32[]{:S(2)}) collective-permute-start(bf16[128,1280]{1,0:T(8,128)(2,1)S(1)} %get-tuple-element.12), channel_id=1, source_target_pairs={{1,0},{2,3},{5,4},{6,7},{9,8},{10,11},{13,12},{14,15},{17,16},{18,... | collective-permute-start | bytes 983048 | tf_op jit(solution)/shard_map/ppermute | solution.py:254
  82.2 21.2 %collective-permute-start.4 = (bf16[128,1280]{1,0:T(8,128)(2,1)S(1)}, bf16[128,1280]{1,0:T(8,128)(2,1)S(1)}, u32[]{:S(2)}, u32[]{:S(2)}) collective-permute-start(bf16[128,1280]{1,0:T(8,128)(2,1)S(1)} %get-tuple-element.11), channel_id=1, source_target_pairs={{0,1},{3,2},{4,5},{7,6},{8,9},{11,10},{12,13},{15,14},{16,17},{19,... | collective-permute-start | bytes 983048 | tf_op jit(solution)/shard_map/ppermute | solution.py:247
  91.4 12.1 %collective-permute-start.15 = (bf16[128,1280]{1,0:T(8,128)(2,1)S(1)}, bf16[128,1280]{1,0:T(8,128)(2,1)S(1)}, u32[]{:S(2)}, u32[]{:S(2)}) collective-permute-start(bf16[128,1280]{1,0:T(8,128)(2,1)S(1)} %get-tuple-element.17), channel_id=1, source_target_pairs={{1,2},{2,1},{5,6},{6,5},{9,10},{10,9},{13,14},{14,13},{17,18},{18,... | collective-permute-start | bytes 983048 | tf_op jit(solution)/shard_map/ppermute | solution.py:251
  94.7 9.5 %collective-permute-start.13 = (bf16[128,1280]{1,0:T(8,128)(2,1)S(1)}, bf16[128,1280]{1,0:T(8,128)(2,1)S(1)}, u32[]{:S(2)}, u32[]{:S(2)}) collective-permute-start(bf16[128,1280]{1,0:T(8,128)(2,1)S(1)} %get-tuple-element.15), channel_id=1, source_target_pairs={{0,1},{3,2},{4,5},{7,6},{8,9},{11,10},{12,13},{15,14},{16,17},{19,... | collective-permute-start | bytes 983048 | tf_op jit(solution)/shard_map/ppermute | solution.py:247
  99.6 9.0 %collective-permute-start.18 = (bf16[128,1280]{1,0:T(8,128)(2,1)S(1)}, bf16[128,1280]{1,0:T(8,128)(2,1)S(1)}, u32[]{:S(2)}, u32[]{:S(2)}) collective-permute-start(bf16[128,1280]{1,0:T(8,128)(2,1)S(1)} %get-tuple-element.16), channel_id=1, source_target_pairs={{1,0},{2,3},{5,4},{6,7},{9,8},{10,11},{13,12},{14,15},{17,16},{18,... | collective-permute-start | bytes 983048 | tf_op jit(solution)/shard_map/ppermute | solution.py:254
  (2 other events, 1.6 us)

commit v2 on v1

v2 whole, which is shorter than its diff:
```python
import functools

import jax
import jax.numpy as jnp
from jax import lax
from jax.experimental import pallas as pl
from jax.experimental.pallas import tpu as pltpu
from jax.sharding import PartitionSpec as P

F32 = jnp.float32
BF16 = jnp.bfloat16
LANES = 128
COORD_ROWS = 16


def swap(value, axis, step):
    count = lax.axis_size(axis)
    return lax.ppermute(value, axis, [(i, i ^ step) for i in range(count)])


def high_low(value):
    high = value.astype(BF16)
    low = (value - high.astype(F32)).astype(BF16)
    return high, low


def in_hbm(*arrays):
    return [pltpu.with_memory_space_constraint(array, pltpu.HBM) for array in arrays]


def near_kernel(feats_ref, xyz_ref, w_near_ref, out_ref, feats, xyz, weights, arrived):
    residues = feats.shape[0]
    parts, height, depth = weights.shape
    copies = [
        pltpu.make_async_copy(feats_ref, feats, arrived.at[parts]),
        pltpu.make_async_copy(xyz_ref, xyz, arrived.at[parts + 1]),
    ] + [
        pltpu.make_async_copy(
            w_near_ref.at[part * height : (part + 1) * height, :],
            weights.at[part],
            arrived.at[part],
        )
        for part in range(parts)
    ]
    for copy in copies:
        copy.start()
    out_ref[residues:, :] = jnp.zeros((COORD_ROWS, depth), BF16)
    copies[0].wait()
    copies[1].wait()
    out_ref[residues : residues + 3, 0:residues] = xyz[...]
    near = None
    for part in range(parts):
        copies[2 + part].wait()
        term = jnp.dot(
            feats[:, part * height : (part + 1) * height],
            weights[part],
            preferred_element_type=F32,
        )
        near = term if near is None else near + term
    out_ref[0:residues, :] = near.astype(BF16)


def near_rows(feats, xyz, w_near):
    residues, depth = feats.shape
    parts = 4
    return pl.pallas_call(
        near_kernel,
        out_shape=jax.ShapeDtypeStruct((residues + COORD_ROWS, depth), BF16),
        in_specs=[pl.BlockSpec(memory_space=pltpu.HBM)] * 3,
        out_specs=pl.BlockSpec(memory_space=pltpu.VMEM),
        scratch_shapes=[
            pltpu.VMEM(feats.shape, BF16),
            pltpu.VMEM(xyz.shape, BF16),
            pltpu.VMEM((parts, depth // parts, depth), BF16),
            pltpu.SemaphoreType.DMA((parts + 2,)),
        ],
        name="near_rows",
    )(*in_hbm(feats, xyz, w_near))


def message_kernel(
    rows_at_once,
    first_row,
    with_tokens,
    *refs,
):
    if with_tokens:
        (token_gain_ref, w_up_ref), refs = refs[9:11], refs[:9] + refs[11:]
        (token_ref,), refs = refs[12:13], refs[:12] + refs[13:]
        (token_gain_buf, w_up_buf, scaled_ref), refs = refs[-3:], refs[:-3]
    message_body(
        rows_at_once,
        first_row,
        (token_gain_ref, w_up_ref, token_ref, token_gain_buf, w_up_buf, scaled_ref)
        if with_tokens
        else None,
        *refs,
    )


def message_body(
    rows_at_once,
    first_row,
    tokens,
    own_ref,
    side_ref,
    other_ref,
    feats_ref,
    link_ref,
    w_rbf_ref,
    gain_ref,
    w_logit_ref,
    table_ref,
    scalar_ref,
    soft_ref,
    coded_ref,
    window_ref,
    position_ref,
    feats_buf,
    link_buf,
    gain_buf,
    w_logit_buf,
    table_buf,
    place_ref,
    xyz_ref,
    message_ref,
    soft_buf,
    arrived,
):
    neighbour_count, residues = link_ref.shape
    bins, feature_dim = w_rbf_ref.shape
    vocab_size = table_ref.shape[0]
    window = 3 * residues
    early = []
    for slot, ref in enumerate((own_ref, side_ref, other_ref)):
        early.append(
            (ref.at[0:residues, :], window_ref.at[slot * residues : (slot + 1) * residues, :])
        )
        early.append(
            (ref.at[residues : residues + COORD_ROWS, 0:residues], position_ref.at[slot])
        )
    early.append((w_rbf_ref, window_ref.at[window : window + bins, :]))
    early.append((link_ref, link_buf))
    late = [
        (feats_ref, feats_buf),
        (gain_ref, gain_buf),
        (w_logit_ref, w_logit_buf),
        (table_ref, table_buf),
    ]
    if tokens:
        token_gain_ref, w_up_ref, token_ref, token_gain_buf, w_up_buf, scaled_ref = tokens
        late += [(token_gain_ref, token_gain_buf), (w_up_ref, w_up_buf)]
    copies = [
        pltpu.make_async_copy(source, target, arrived.at[place])
        for place, (source, target) in enumerate(early + late)
    ]
    for copy in copies:
        copy.start()
    window_ref[window + bins :, :] = jnp.zeros(
        (window_ref.shape[0] - window - bins, feature_dim), BF16
    )
    for copy in copies[: len(early)]:
        copy.wait()

    block_index = scalar_ref[0]
    residue_count = scalar_ref[1]
    positions = [position_ref[slot].astype(F32) for slot in range(3)]
    xyz_ref[...] = jnp.transpose(
        jnp.concatenate([positions[0], jnp.zeros((LANES - COORD_ROWS, residues), F32)], axis=0)
    )
    place_ref[...] = jnp.transpose(
        jnp.concatenate(
            [link_buf[...], jnp.zeros((LANES - neighbour_count, residues), jnp.int32)], axis=0
        )
    )
    lane = lax.broadcasted_iota(jnp.int32, (rows_at_once, LANES), 1)
    centres = 2.0 + (20.0 / (bins - 1)) * lane.astype(F32)

    def one_chunk(step, carry):
        begin = pl.multiple_of(step * rows_at_once, rows_at_once)
        first = first_row + begin
        links = place_ref[pl.ds(first, rows_at_once), :]
        keep = (links < residue_count) & (lane < neighbour_count)
        within = jnp.bitwise_and(links, residues - 1)
        block_of = lax.shift_right_logical(links, residues.bit_length() - 1)
        side_block = jnp.bitwise_xor(block_index, 1)
        slot_of = jnp.where(
            block_of == block_index, 0, jnp.where(block_of == side_block, 1, 2)
        )
        own_xyz = xyz_ref[pl.ds(first, rows_at_once), :]
        squared = None
        for slot in range(3):
            total = None
            for axis in range(3):
                offset = own_xyz[:, axis : axis + 1] - positions[slot][axis : axis + 1, :]
                total = offset * offset if total is None else total + offset * offset
            picked = jnp.take_along_axis(total, within, axis=1)
            squared = picked if squared is None else jnp.where(slot_of == slot, picked, squared)
        distance = jnp.where(keep, jnp.sqrt(squared), 1e6)
        place = jnp.where(keep, within + slot_of * residues, -1)
        rows = []
        for k in range(neighbour_count):
            place_k = jnp.broadcast_to(place[:, k : k + 1], (rows_at_once, LANES))
            parts = [
                jnp.where(place_k == lane + slot * residues, 1.0, 0.0).astype(BF16)
                for slot in range(3)
            ]
            distance_k = jnp.broadcast_to(distance[:, k : k + 1], (rows_at_once, LANES))
            scaled = (distance_k - centres) * (1.0 / 1.25)
            radial = jnp.where(lane < bins, jnp.exp(-scaled * scaled), 0.0)
            parts.append(radial.astype(BF16))
            rows.append(jnp.concatenate(parts, axis=1))
        selector = jnp.concatenate(rows, axis=0)
        width = 256
        for column in range(feature_dim // width):
            cols = slice(column * width, (column + 1) * width)
            preact = jnp.dot(selector, window_ref[:, cols], preferred_element_type=F32)
            doubled = preact * (1.0 + lax.erf(preact * (0.5**0.5)))
            message_ref[pl.ds(begin, rows_at_once), cols] = jnp.sum(
                doubled.reshape(neighbour_count, rows_at_once, width), axis=0
            ) * (0.5 / 30.0)
        return carry

    count = message_ref.shape[0]
    lax.fori_loop(0, count // rows_at_once, one_chunk, 0)

    for copy in copies[len(early) :]:
        copy.wait()
    values = feats_buf[first_row : first_row + count, :].astype(F32) + message_ref[...]
    centred = values - jnp.mean(values, axis=1, keepdims=True)
    spread = jnp.mean(centred * centred, axis=1, keepdims=True)
    mixed = (centred * lax.rsqrt(spread + 1e-5) * gain_buf[...]).astype(BF16)
    half = LANES // 2
    w_logit = jnp.concatenate(
        [w_logit_buf[...].astype(F32), jnp.zeros((LANES - vocab_size, feature_dim), F32)], axis=0
    ).astype(BF16)
    logits = lax.dot_general(
        mixed, w_logit, (((1,), (1,)), ((), ())), preferred_element_type=F32
    )
    bounded = 8.0 * jnp.tanh(logits * 0.125)
    token = lax.broadcasted_iota(jnp.int32, logits.shape, 1)
    exponent = jnp.where(token < vocab_size, jnp.exp(bounded), 0.0)
    probability = (exponent / jnp.sum(exponent, axis=1, keepdims=True)).astype(BF16)
    residue = (
        block_index * residues + first_row + lax.broadcasted_iota(jnp.int32, (count, 1), 0)
    )
    valid = (residue < residue_count).astype(F32)
    table = jnp.concatenate(
        [
            table_buf[...].astype(F32),
            jnp.zeros((LANES - vocab_size, table_buf.shape[1]), F32),
        ],
        axis=0,
    ).astype(BF16)
    soft = (jnp.dot(probability, table, preferred_element_type=F32) * valid).astype(BF16)
    soft_buf[...] = soft
    leaving = pltpu.make_async_copy(soft_buf, soft_ref, arrived.at[len(copies)])
    leaving.start()
    soft_wide = soft.astype(F32)
    soft_centred = soft_wide - jnp.mean(soft_wide, axis=1, keepdims=True)
    soft_spread = jnp.mean(soft_centred * soft_centred, axis=1, keepdims=True)
    coded = probability.astype(F32) * (lax.rsqrt(soft_spread + 1e-5) * valid)
    high, low = high_low(coded)
    coded_ref[...] = jnp.concatenate([high[:, :half], low[:, :half]], axis=1)
    if tokens:
        wide = table.astype(F32)[:half]
        wide = wide - jnp.mean(wide, axis=1, keepdims=True)
        scaled_ref[...] = (wide * token_gain_buf[...]).astype(BF16)
        depth = w_up_buf.shape[0]
        part = scaled_ref[:, pl.ds(pl.multiple_of(scalar_ref[2] * depth, LANES), depth)]
        token_ref[...] = jnp.dot(part, w_up_buf[...], preferred_element_type=F32)
    leaving.wait()


def messages(own, side, other, feats, links, w_rbf, gain, w_logit, table, scalars, rows, tokens):
    residues, feature_dim = feats.shape
    embed_dim = table.shape[1]
    bins = w_rbf.shape[0]
    depth = -(-(3 * residues + bins) // 256) * 256
    count = rows[1] - rows[0]
    in_vmem = pl.BlockSpec(memory_space=pltpu.VMEM)
    in_hbm_spec = pl.BlockSpec(memory_space=pltpu.HBM)
    arrays = [own, side, other, feats, links, w_rbf, gain, w_logit, table, *tokens]
    out_shape = [pltpu.HBM((count, embed_dim), BF16), jax.ShapeDtypeStruct((count, LANES), BF16)]
    scratch = [
        pltpu.VMEM((depth, feature_dim), BF16),
        pltpu.VMEM((3, COORD_ROWS, residues), BF16),
        pltpu.VMEM(feats.shape, BF16),
        pltpu.VMEM(links.shape, jnp.int32),
        pltpu.VMEM(gain.shape, F32),
        pltpu.VMEM(w_logit.shape, BF16),
        pltpu.VMEM(table.shape, BF16),
        pltpu.VMEM((residues, LANES), jnp.int32),
        pltpu.VMEM((residues, LANES), F32),
        pltpu.VMEM((count, feature_dim), F32),
        pltpu.VMEM((count, embed_dim), BF16),
        pltpu.SemaphoreType.DMA((16,)),
    ]
    if tokens:
        token_gain, w_up = tokens
        out_shape.append(jax.ShapeDtypeStruct((LANES // 2, w_up.shape[1]), F32))
        scratch += [
            pltpu.VMEM(token_gain.shape, F32),
            pltpu.VMEM(w_up.shape, BF16),
            pltpu.VMEM((LANES // 2, embed_dim), BF16),
        ]
    return pl.pallas_call(
        functools.partial(message_kernel, min(32, count), rows[0], bool(tokens)),
        out_shape=out_shape,
        in_specs=[in_hbm_spec] * len(arrays) + [pl.BlockSpec(memory_space=pltpu.SMEM)],
        out_specs=[in_hbm_spec] + [in_vmem] * (len(out_shape) - 1),
        scratch_shapes=scratch,
        compiler_params=pltpu.CompilerParams(vmem_limit_bytes=20 << 20),
        cost_estimate=pl.CostEstimate(
            flops=100_000_000 * count, bytes_accessed=5_000_000, transcendentals=50_000 * count
        ),
        name="messages",
    )(*in_hbm(*arrays), scalars)


def gelu_rows(rows, up):
    total = jnp.dot(rows, jnp.concatenate([up, up], axis=0), preferred_element_type=F32)
    return (0.5 * total * (1.0 + lax.erf(total * (0.5**0.5)))).astype(BF16)


def trunk_kernel(columns, targets, *refs):
    coded, up_ref = refs[:4], refs[4]
    weights = refs[5 : 5 + len(columns)]
    outs = refs[5 + len(columns) : -5]
    buffer, inner, results, arrived, left = refs[-5:]
    chunk = buffer.shape[2]
    copies = [
        pltpu.make_async_copy(
            ref.at[:, first : first + chunk], buffer.at[place], arrived.at[place]
        )
        for place, (ref, first) in enumerate(zip(weights, columns))
    ]
    for copy in copies:
        copy.start()
    rows = coded[0].shape[0]
    for place, ref in enumerate(coded):
        inner[place * rows : (place + 1) * rows, :] = gelu_rows(ref[...], up_ref[...])
    leaving = []
    for place, copy in enumerate(copies):
        copy.wait()
        value = jnp.dot(inner[...], buffer[place], preferred_element_type=F32)
        results[place] = value.astype(BF16)
        for number, (start, stop) in enumerate(targets):
            leaving.append(
                pltpu.make_async_copy(
                    results.at[place, start:stop, :],
                    outs[number].at[:, place * chunk : (place + 1) * chunk],
                    left.at[len(leaving)],
                )
            )
            leaving[-1].start()
    for copy in leaving:
        copy.wait()


def trunk(coded, up, pieces, targets, chunk):
    rows, hidden = coded[0].shape[0], up.shape[1]
    in_vmem = pl.BlockSpec(memory_space=pltpu.VMEM)
    hbm_spec = pl.BlockSpec(memory_space=pltpu.HBM)
    return pl.pallas_call(
        functools.partial(trunk_kernel, [column for _, column in pieces], targets),
        out_shape=[
            pltpu.HBM((stop - start, len(pieces) * chunk), BF16) for start, stop in targets
        ],
        in_specs=[in_vmem] * 5 + [hbm_spec] * len(pieces),
        out_specs=[hbm_spec] * len(targets),
        scratch_shapes=[
            pltpu.VMEM((len(pieces), hidden, chunk), BF16),
            pltpu.VMEM((4 * rows, hidden), BF16),
            pltpu.VMEM((len(pieces), 4 * rows, chunk), BF16),
            pltpu.SemaphoreType.DMA((len(pieces),)),
            pltpu.SemaphoreType.DMA((len(pieces) * len(targets),)),
        ],
        compiler_params=pltpu.CompilerParams(vmem_limit_bytes=16 << 20),
        cost_estimate=pl.CostEstimate(
            flops=8 * rows * len(pieces) * hidden * chunk,
            bytes_accessed=2 * hidden * chunk * len(pieces),
            transcendentals=4 * rows * hidden,
        ),
        name="trunk",
    )(*coded, up, *in_hbm(*[array for array, _ in pieces]))


def rounded_sum(left, right):
    return (left.astype(F32) + right.astype(F32)).astype(BF16)


def on_device(
    node_feats,
    coords,
    neighbours,
    counts,
    w_near,
    w_rbf,
    gen_gain,
    w_logit,
    embed_table,
    trunk_gain,
    w_up,
    w_down,
):
    backbones, residues, feature_dim = node_feats.shape
    assert backbones == 1 and lax.axis_size("mp") == 4
    vocab_size, embed_dim = embed_table.shape
    half = LANES // 2
    seq_count = lax.axis_size("seq")
    seq_index = lax.axis_index("seq")
    block_index = lax.axis_index("mp")

    own = near_rows(node_feats[0], coords[0], w_near)
    side = swap(own, "mp", 1)
    other = lax.ppermute(own, "mp", [(1, 2), (2, 1)])

    scalars = jnp.stack([block_index.astype(jnp.int32), counts[0], seq_index.astype(jnp.int32)])

    def some_messages(first, last, tokens):
        return messages(
            own,
            side,
            other,
            node_feats[0],
            neighbours[0].T,
            w_rbf,
            gen_gain[None, :],
            w_logit.T,
            embed_table,
            scalars,
            (first, last),
            tokens,
        )

    if seq_count == 2 and w_up.shape[0] % LANES == 0:
        soft_a, coded_a, token_up = some_messages(
            0, residues // 2, (trunk_gain[None, :], w_up)
        )
        token_up = (token_up + swap(token_up, "seq", 1)).astype(BF16)
        whole = [w_down, swap(w_down, "seq", 1)]
    else:
        soft_a, coded_a = some_messages(0, residues // 2, ())
        table_wide = embed_table.astype(F32)
        table_centred = table_wide - jnp.mean(table_wide, axis=1, keepdims=True)
        table_scaled = jnp.pad(
            (table_centred * trunk_gain).astype(BF16), ((0, half - vocab_size), (0, 0))
        )
        table_part = lax.dynamic_slice_in_dim(
            table_scaled, seq_index * w_up.shape[0], w_up.shape[0], 1
        )
        token_up = lax.psum(
            jnp.dot(table_part, w_up, preferred_element_type=F32), "seq"
        ).astype(BF16)
        whole = [lax.all_gather(w_down, "seq", axis=1, tiled=True)]
    soft_b, coded_b = some_messages(residues // 2, residues, ())
    soft = jnp.concatenate([soft_a, soft_b], axis=0)
    chunk = embed_dim // 4
    pieces = [(part, first) for part in whole for first in range(0, part.shape[1], chunk)]

    part_rows = residues // 2
    inward = [(0, 1), (3, 2)]
    crossing = [(1, 2), (2, 1)]
    skipping = [(1, 3), (2, 0)]
    sums = []
    order = ()
    for coded in (coded_a, coded_b):
        coded_rows = [swap(coded, "mp", step) for step in (3, 2, 1)] + [coded]
        coded_rows, order = lax.optimization_barrier((coded_rows, order))
        far, near, held = trunk(
            coded_rows,
            token_up,
            pieces,
            [
                (0, 2 * part_rows),
                (2 * part_rows, 3 * part_rows),
                (3 * part_rows, 4 * part_rows),
            ],
            chunk,
        )
        arrived = lax.ppermute(far, "mp", inward)
        arrived, near = lax.optimization_barrier((arrived, near))
        swapped = swap(near, "mp", 1)
        across = rounded_sum(far[:part_rows], arrived[part_rows:])
        beyond = rounded_sum(far[part_rows:], arrived[:part_rows])
        order = (across, beyond)
        across = lax.ppermute(across, "mp", crossing)
        beyond = lax.ppermute(beyond, "mp", skipping)
        sums.append(
            held.astype(F32)
            + swapped.astype(F32)
            + across.astype(F32)
            + beyond.astype(F32)
        )
    total = jnp.concatenate(sums, axis=0)
    if len(whole) == 2:
        middle = embed_dim // 2
        turned = jnp.concatenate([total[:, middle:], total[:, :middle]], axis=1)
        total = jnp.where(seq_index == 0, total, turned)
    return (soft.astype(F32) + total).astype(BF16)[None]


def solution(mesh):
    placed = (
        P(("dp", "seq"), "mp", None),
        P(("dp", "seq"), None, "mp"),
        P(("dp", "seq"), "mp", None),
        P(("dp", "seq")),
        P(),
        P(),
        P(),
        P(),
        P(),
        P(),
        P("seq", "mp"),
        P("mp", "seq"),
    )
    return jax.shard_map(
        on_device,
        mesh=mesh,
        in_specs=placed,
        out_specs=P(("dp", "seq"), "mp", None),
        check_vma=False,
    )
```

time: 113 us -> 101 us (0.89)
  matrix products: 28.2 us -> 0 us
  waiting for transfers between devices: 13.1 us -> 30.3 us
  Pallas kernels: 12.7 us -> 29.5 us
  starting transfers between devices: 41.5 us -> 33.9 us
  local copies, waits for them, and re-layouts: 9.39 us -> 3.26 us
  other arithmetic: 6.36 us -> 2.87 us
    dot_general x13 -> x0, matrix products: 28.2 us -> none  [the longest x8 20.6 us: product(): return jnp.dot(inner[step], part, preferred_element_type=F32)]
    ppermute x12 -> x6, starting transfers between devices: 30.6 us -> 8.4 us  [the longest x2 4.32 us: on_device(): arrived = lax.ppermute(far, 'mp', inward)]
    pallas_call x1 -> x5, Pallas kernels: 12.7 us -> 29.5 us  [the longest x2 16.1 us: messages(): pl.pallas_call(functools.partial(message_kernel, min(32, count), rows[0],...]
    ppermute x6 -> x11, starting transfers between devices: 9.59 us -> 24.1 us  [swap(): return lax.ppermute(value, axis, [(i, i ^ step) for i in range(count)])]
    ppermute x6 -> x11, waiting for transfers between devices: 0.02 us -> 13.6 us  [swap(): return lax.ppermute(value, axis, [(i, i ^ step) for i in range(count)])]
    unnamed x16 -> x18, local copies, waits for them, and re-layouts: 7.51 us -> 2.66 us
    ppermute x12 -> x6, waiting for transfers between devices: 13.1 us -> 16.8 us  [the longest x2 9.11 us: on_device(): arrived = lax.ppermute(far, 'mp', inward)]
    pad x2 -> x0, local copies, waits for them, and re-layouts: 1.89 us -> none  [the longest x1 1 us: on_device(): jnp.pad(w_logit, ((0, 0), (0, LANES - vocab_size)))]
  transfers between devices with their start and end apart: 19 -> 18, of which waited for: 4 -> 9; matrix products, arithmetic and copies ran while one was open for 30% -> 2% of each run, Pallas kernels for 11% -> 19%
where the time goes in v2:
time: 101 us
  starting transfers between devices  33.9 us (34%)
  waiting for transfers between devices  30.3 us (30%)
  Pallas kernels  29.5 us (29%)
  local copies, waits for them, and re-layouts  3.26 us (3%)
  other arithmetic  2.87 us (3%)
    ppermute x11, starting transfers between devices, swap(): return lax.ppermute(value, axis, [(i, i ^ step) for i in range(count)])  24.1 us
    pallas_call x2, Pallas kernels, messages(): pl.pallas_call(functools.partial(message_kernel, min(32, count), rows[0],...  16.1 us
    ppermute x11, waiting for transfers between devices, swap(): return lax.ppermute(value, axis, [(i, i ^ step) for i in range(count)])  13.6 us
    pallas_call x2, Pallas kernels, trunk(): pl.pallas_call(functools.partial(trunk_kernel, [column for _, column in p...  10.7 us
    ppermute x2, waiting for transfers between devices, on_device(): arrived = lax.ppermute(far, 'mp', inward)  9.11 us
    ppermute x2, waiting for transfers between devices, on_device(): beyond = lax.ppermute(beyond, 'mp', skipping)  7.64 us
    ppermute x2, starting transfers between devices, on_device(): arrived = lax.ppermute(far, 'mp', inward)  4.32 us
    unnamed x18, local copies, waits for them, and re-layouts  2.66 us
  transfers between devices with their start and end apart: 18, of which 9 were waited for; matrix products, arithmetic and copies ran while one was open for 2% of the time, Pallas kernels for 19%

profile of v2, /device:TPU:0, one launch (start us, length us, event | category | flops | bytes accessed | tf_op | source)
XLA Modules:
  0.0 100.8 jit_solution(5144278314432140878)
XLA Ops:
  0.5 2.6 %near_rows.1.refs_0_ = bf16[144,1024]{1,0:T(8,128)(2,1)} custom-call(bf16[128,1024]{1,0:T(8,128)(2,1)} %bitcast.21, bf16[3,128]{1,0:T(4,128)(2,1)} %bitcast.24, bf16[1024,1024]{1,0:T(8,128)(2,1)} %w_near_ref.1), custom_call_target="tpu_custom_call" | custom-call | tf_op jit(solution)/shard_map/near_rows/pallas_call | solution.py:66
  3.1 1.4 %collective-permute-start.1 = (bf16[144,1024]{1,0:T(8,128)(2,1)}, bf16[144,1024]{1,0:T(8,128)(2,1)}, u32[]{:S(2)}, u32[]{:S(2)}) collective-permute-start(bf16[144,1024]{1,0:T(8,128)(2,1)} %near_rows.1.refs_0_), channel_id=1, source_target_pairs={{1,2},{2,1},{5,6},{6,5},{9,10},{10,9},{13,14},{14,13},{17,18},{18,... | collective-permute-start | bytes 884744 | tf_op jit(solution)/shard_map/ppermute | solution.py:417
  4.5 4.7 %collective-permute-start = (bf16[144,1024]{1,0:T(8,128)(2,1)}, bf16[144,1024]{1,0:T(8,128)(2,1)}, u32[]{:S(2)}, u32[]{:S(2)}) collective-permute-start(bf16[144,1024]{1,0:T(8,128)(2,1)} %near_rows.1.refs_0_), channel_id=1, source_target_pairs={{0,1},{1,0},{2,3},{3,2},{4,5},{5,4},{6,7},{7,6},{8,9},{9,8},{10,11... | collective-permute-start | bytes 884744 | tf_op jit(solution)/shard_map/ppermute | solution.py:18
  10.6 6.4 %collective-permute-done.refs_1_ = bf16[144,1024]{1,0:T(8,128)(2,1)} collective-permute-done((bf16[144,1024]{1,0:T(8,128)(2,1)}, bf16[144,1024]{1,0:T(8,128)(2,1)}, u32[]{:S(2)}, u32[]{:S(2)}) %collective-permute-start) | collective-permute-done | bytes 294944 | tf_op jit(solution)/shard_map/ppermute | solution.py:18
  16.9 8.1 %messages.2 = (bf16[64,2560]{1,0:T(8,128)(2,1)}, bf16[64,128]{1,0:T(8,128)(2,1)S(1)}, f32[64,1280]{1,0:T(8,128)S(1)}) custom-call(bf16[144,1024]{1,0:T(8,128)(2,1)} %near_rows.1.refs_0_, bf16[144,1024]{1,0:T(8,128)(2,1)} %collective-permute-done.refs_1_, bf16[144,1024]{1,0:T(8,128)(2,1)} %collective-permute-done.1.refs_2_, bf16[128,1024]{1,0:T(8,128)(2,1)} %bitcast.22, ...), custom_call_target="tpu_custom_call" | custom-call | flops 6400000000 | bytes 5000000 | tf_op jit(solution)/shard_map/messages/pallas_call | solution.py:307
  25.1 1.8 %collective-permute-start.4 = (bf16[64,128]{1,0:T(8,128)(2,1)S(1)}, bf16[64,128]{1,0:T(8,128)(2,1)S(1)}, u32[]{:S(2)}, u32[]{:S(2)}) collective-permute-start(bf16[64,128]{1,0:T(8,128)(2,1)S(1)} %get-tuple-element.34.refs_3_), channel_id=1, source_target_pairs={{0,1},{1,0},{2,3},{3,2},{4,5},{5,4},{6,7},{7,6},{8,9},{9,8},{10,11... | collective-permute-start | bytes 49160 | tf_op jit(solution)/shard_map/ppermute | solution.py:18
  27.6 2.0 %collective-permute-start.2 = (bf16[64,128]{1,0:T(8,128)(2,1)S(1)}, bf16[64,128]{1,0:T(8,128)(2,1)S(1)}, u32[]{:S(2)}, u32[]{:S(2)}) collective-permute-start(bf16[64,128]{1,0:T(8,128)(2,1)S(1)} %get-tuple-element.34.refs_3_), channel_id=1, source_target_pairs={{0,3},{1,2},{2,1},{3,0},{4,7},{5,6},{6,5},{7,4},{8,11},{9,10},{10,... | collective-permute-start | bytes 49160 | tf_op jit(solution)/shard_map/ppermute | solution.py:18
  29.6 2.0 %collective-permute-done.3.refs_1_ = bf16[64,128]{1,0:T(8,128)(2,1)S(1)} collective-permute-done((bf16[64,128]{1,0:T(8,128)(2,1)S(1)}, bf16[64,128]{1,0:T(8,128)(2,1)S(1)}, u32[]{:S(2)}, u32[]{:S(2)}) %collective-permute-start.3) | collective-permute-done | bytes 16416 | tf_op jit(solution)/shard_map/ppermute | solution.py:18
  31.6 1.6 %collective-permute-done.2.refs_0_ = bf16[64,128]{1,0:T(8,128)(2,1)S(1)} collective-permute-done((bf16[64,128]{1,0:T(8,128)(2,1)S(1)}, bf16[64,128]{1,0:T(8,128)(2,1)S(1)}, u32[]{:S(2)}, u32[]{:S(2)}) %collective-permute-start.2) | collective-permute-done | bytes 16416 | tf_op jit(solution)/shard_map/ppermute | solution.py:18
  33.2 1.7 %copy-done = bf16[1280,1280]{1,0:T(8,128)(2,1)} copy-done((bf16[1280,1280]{1,0:T(8,128)(2,1)}, bf16[1280,1280]{1,0:T(8,128)(2,1)S(1)}, u32[]{:S(2)}) %copy-start) | copy-done | bytes 3276824
  34.9 5.4 %trunk.2 = (bf16[128,2560]{1,0:T(8,128)(2,1)}, bf16[64,2560]{1,0:T(8,128)(2,1)}, bf16[64,2560]{1,0:T(8,128)(2,1)}) custom-call(bf16[64,128]{1,0:T(8,128)(2,1)S(1)} %collective-permute-done.2.refs_0_, bf16[64,128]{1,0:T(8,128)(2,1)S(1)} %collective-permute-done.3.refs_1_, bf16[64,128]{1,0:T(8,128)(2,1)S(1)} %collective-permute-done.4.refs_2_, ...), custom_call_target="tpu_custom_call" | custom-call | flops 1677721600 | bytes 6553600 | tf_op jit(solution)/shard_map/trunk/pallas_call | solution.py:365
  40.3 1.8 %collective-permute-start.7 = (bf16[128,2560]{1,0:T(8,128)(2,1)}, bf16[128,2560]{1,0:T(8,128)(2,1)S(1)}, u32[]{:S(2)}, u32[]{:S(2)}) collective-permute-start(bf16[128,2560]{1,0:T(8,128)(2,1)} %get-tuple-element.37), channel_id=1, source_target_pairs={{0,1},{3,2},{4,5},{7,6},{8,9},{11,10},{12,13},{15,14},{16,17},{19,... | collective-permute-start | bytes 1966088 | tf_op jit(solution)/shard_map/ppermute | solution.py:482
  42.2 8.0 %messages.3 = (bf16[64,2560]{1,0:T(8,128)(2,1)}, bf16[64,128]{1,0:T(8,128)(2,1)S(1)}) custom-call(bf16[144,1024]{1,0:T(8,128)(2,1)} %near_rows.1.refs_0_, bf16[144,1024]{1,0:T(8,128)(2,1)} %collective-permute-done.refs_1_, bf16[144,1024]{1,0:T(8,128)(2,1)} %collective-permute-done.1.refs_2_, bf16[128,1024]{1,0:T(8,128)(2,1)} %bitcast.23, ...), custom_call_target="tpu_custom_call" | custom-call | flops 6400000000 | bytes 5000000 | tf_op jit(solution)/shard_map/messages/pallas_call | solution.py:307
  50.2 2.9 %collective-permute-start.12 = (bf16[64,128]{1,0:T(8,128)(2,1)S(1)}, bf16[64,128]{1,0:T(8,128)(2,1)S(1)}, u32[]{:S(2)}, u32[]{:S(2)}) collective-permute-start(bf16[64,128]{1,0:T(8,128)(2,1)S(1)} %get-tuple-element.45.refs_3_), channel_id=1, source_target_pairs={{0,2},{1,3},{2,0},{3,1},{4,6},{5,7},{6,4},{7,5},{8,10},{9,11},{10,... | collective-permute-start | bytes 49160 | tf_op jit(solution)/shard_map/ppermute | solution.py:18
  53.1 1.5 %collective-permute-start.11 = (bf16[64,128]{1,0:T(8,128)(2,1)S(1)}, bf16[64,128]{1,0:T(8,128)(2,1)S(1)}, u32[]{:S(2)}, u32[]{:S(2)}) collective-permute-start(bf16[64,128]{1,0:T(8,128)(2,1)S(1)} %get-tuple-element.45.refs_3_), channel_id=1, source_target_pairs={{0,3},{1,2},{2,1},{3,0},{4,7},{5,6},{6,5},{7,4},{8,11},{9,10},{10,... | collective-permute-start | bytes 49160 | tf_op jit(solution)/shard_map/ppermute | solution.py:18
  56.1 2.8 %collective-permute-done.11.refs_0_ = bf16[64,128]{1,0:T(8,128)(2,1)S(1)} collective-permute-done((bf16[64,128]{1,0:T(8,128)(2,1)S(1)}, bf16[64,128]{1,0:T(8,128)(2,1)S(1)}, u32[]{:S(2)}, u32[]{:S(2)}) %collective-permute-start.11) | collective-permute-done | bytes 16416 | tf_op jit(solution)/shard_map/ppermute | solution.py:18
  58.9 5.4 %trunk.3 = (bf16[128,2560]{1,0:T(8,128)(2,1)}, bf16[64,2560]{1,0:T(8,128)(2,1)}, bf16[64,2560]{1,0:T(8,128)(2,1)}) custom-call(bf16[64,128]{1,0:T(8,128)(2,1)S(1)} %collective-permute-done.11.refs_0_, bf16[64,128]{1,0:T(8,128)(2,1)S(1)} %collective-permute-done.12.refs_1_, bf16[64,128]{1,0:T(8,128)(2,1)S(1)} %collective-permute-done.13.refs_2_, ...), custom_call_target="tpu_custom_call" | custom-call | flops 1677721600 | bytes 6553600 | tf_op jit(solution)/shard_map/trunk/pallas_call | solution.py:365
  64.3 2.5 %collective-permute-start.14 = (bf16[128,2560]{1,0:T(8,128)(2,1)}, bf16[128,2560]{1,0:T(8,128)(2,1)S(1)}, u32[]{:S(2)}, u32[]{:S(2)}) collective-permute-start(bf16[128,2560]{1,0:T(8,128)(2,1)} %get-tuple-element.47), channel_id=1, source_target_pairs={{0,1},{3,2},{4,5},{7,6},{8,9},{11,10},{12,13},{15,14},{16,17},{19,... | collective-permute-start | bytes 1966088 | tf_op jit(solution)/shard_map/ppermute | solution.py:482
  66.8 1.3 %collective-permute-start.10 = (bf16[64,2560]{1,0:T(8,128)(2,1)S(1)}, bf16[64,2560]{1,0:T(8,128)(2,1)S(1)}, u32[]{:S(2)}, u32[]{:S(2)}) collective-permute-start(bf16[64,2560]{1,0:T(8,128)(2,1)S(1)} %get-tuple-element.55), channel_id=1, source_target_pairs={{1,3},{2,0},{5,7},{6,4},{9,11},{10,8},{13,15},{14,12},{17,19},{18,... | collective-permute-start | bytes 983048 | tf_op jit(solution)/shard_map/ppermute | solution.py:489
  68.8 5.4 %collective-permute-start.8 = (bf16[64,2560]{1,0:T(8,128)(2,1)S(1)}, bf16[64,2560]{1,0:T(8,128)(2,1)S(1)}, u32[]{:S(2)}, u32[]{:S(2)}) collective-permute-start(bf16[64,2560]{1,0:T(8,128)(2,1)S(1)} %copy-done.7), channel_id=1, source_target_pairs={{0,1},{1,0},{2,3},{3,2},{4,5},{5,4},{6,7},{7,6},{8,9},{9,8},{10,11... | collective-permute-start | bytes 983048 | tf_op jit(solution)/shard_map/ppermute | solution.py:18
  74.2 7.9 %collective-permute-done.14 = bf16[128,2560]{1,0:T(8,128)(2,1)S(1)} collective-permute-done((bf16[128,2560]{1,0:T(8,128)(2,1)}, bf16[128,2560]{1,0:T(8,128)(2,1)S(1)}, u32[]{:S(2)}, u32[]{:S(2)}) %collective-permute-start.14) | collective-permute-done | bytes 655392 | tf_op jit(solution)/shard_map/ppermute | solution.py:482
  84.1 1.3 %collective-permute-start.17 = (bf16[64,2560]{1,0:T(8,128)(2,1)S(1)}, bf16[64,2560]{1,0:T(8,128)(2,1)S(1)}, u32[]{:S(2)}, u32[]{:S(2)}) collective-permute-start(bf16[64,2560]{1,0:T(8,128)(2,1)S(1)} %get-tuple-element.54), channel_id=1, source_target_pairs={{1,3},{2,0},{5,7},{6,4},{9,11},{10,8},{13,15},{14,12},{17,19},{18,... | collective-permute-start | bytes 983048 | tf_op jit(solution)/shard_map/ppermute | solution.py:489
  85.4 4.6 %collective-permute-start.15 = (bf16[64,2560]{1,0:T(8,128)(2,1)S(1)}, bf16[64,2560]{1,0:T(8,128)(2,1)S(1)}, u32[]{:S(2)}, u32[]{:S(2)}) collective-permute-start(bf16[64,2560]{1,0:T(8,128)(2,1)S(1)} %copy-done.8), channel_id=1, source_target_pairs={{0,1},{1,0},{2,3},{3,2},{4,5},{5,4},{6,7},{7,6},{8,9},{9,8},{10,11... | collective-permute-start | bytes 983048 | tf_op jit(solution)/shard_map/ppermute | solution.py:18
  90.2 7.6 %collective-permute-done.17 = bf16[64,2560]{1,0:T(8,128)(2,1)S(1)} collective-permute-done((bf16[64,2560]{1,0:T(8,128)(2,1)S(1)}, bf16[64,2560]{1,0:T(8,128)(2,1)S(1)}, u32[]{:S(2)}, u32[]{:S(2)}) %collective-permute-start.17) | collective-permute-done | bytes 327712 | tf_op jit(solution)/shard_map/ppermute | solution.py:489
  (44 shorter events, 9.3 us)
Async XLA Ops:
  0.0 33.2 %collective-permute-start.6 = (bf16[1280,1280]{1,0:T(8,128)(2,1)}, bf16[1280,1280]{1,0:T(8,128)(2,1)S(1)}, u32[]{:S(2)}, u32[]{:S(2)}) collective-permute-start(bf16[1280,1280]{1,0:T(8,128)(2,1)} %refs_6_.3), channel_id=1, source_target_pairs={{0,4},{4,0},{1,5},{5,1},{2,6},{6,2},{3,7},{7,3},{8,12},{12,8},{9,1... | collective-permute-start | bytes 9830408 | tf_op jit(solution)/shard_map/ppermute | solution.py:18
  0.5 9.4 %copy-start.6 = (f32[2560]{0:T(1024)S(1)}, f32[2560]{0:T(1024)}, u32[]{:S(2)}) copy-start(f32[2560]{0:T(1024)} %param.21) | copy-start | bytes 30724
  3.1 7.5 %collective-permute-start.1 = (bf16[144,1024]{1,0:T(8,128)(2,1)}, bf16[144,1024]{1,0:T(8,128)(2,1)}, u32[]{:S(2)}, u32[]{:S(2)}) collective-permute-start(bf16[144,1024]{1,0:T(8,128)(2,1)} %near_rows.1.refs_0_), channel_id=1, source_target_pairs={{1,2},{2,1},{5,6},{6,5},{9,10},{10,9},{13,14},{14,13},{17,18},{18,... | collective-permute-start | bytes 884744 | tf_op jit(solution)/shard_map/ppermute | solution.py:417
  4.5 12.5 %collective-permute-start = (bf16[144,1024]{1,0:T(8,128)(2,1)}, bf16[144,1024]{1,0:T(8,128)(2,1)}, u32[]{:S(2)}, u32[]{:S(2)}) collective-permute-start(bf16[144,1024]{1,0:T(8,128)(2,1)} %near_rows.1.refs_0_), channel_id=1, source_target_pairs={{0,1},{1,0},{2,3},{3,2},{4,5},{5,4},{6,7},{7,6},{8,9},{9,8},{10,11... | collective-permute-start | bytes 884744 | tf_op jit(solution)/shard_map/ppermute | solution.py:18
  25.1 8.1 %collective-permute-start.5 = (f32[64,1280]{1,0:T(8,128)S(1)}, f32[64,1280]{1,0:T(8,128)S(1)}, u32[]{:S(2)}, u32[]{:S(2)}) collective-permute-start(f32[64,1280]{1,0:T(8,128)S(1)} %get-tuple-element.35), channel_id=1, source_target_pairs={{0,4},{4,0},{1,5},{5,1},{2,6},{6,2},{3,7},{7,3},{8,12},{12,8},{9,1... | collective-permute-start | bytes 983048 | tf_op jit(solution)/shard_map/ppermute | solution.py:18
  25.1 4.5 %collective-permute-start.4 = (bf16[64,128]{1,0:T(8,128)(2,1)S(1)}, bf16[64,128]{1,0:T(8,128)(2,1)S(1)}, u32[]{:S(2)}, u32[]{:S(2)}) collective-permute-start(bf16[64,128]{1,0:T(8,128)(2,1)S(1)} %get-tuple-element.34.refs_3_), channel_id=1, source_target_pairs={{0,1},{1,0},{2,3},{3,2},{4,5},{5,4},{6,7},{7,6},{8,9},{9,8},{10,11... | collective-permute-start | bytes 49160 | tf_op jit(solution)/shard_map/ppermute | solution.py:18
  26.9 4.6 %collective-permute-start.3 = (bf16[64,128]{1,0:T(8,128)(2,1)S(1)}, bf16[64,128]{1,0:T(8,128)(2,1)S(1)}, u32[]{:S(2)}, u32[]{:S(2)}) collective-permute-start(bf16[64,128]{1,0:T(8,128)(2,1)S(1)} %get-tuple-element.34.refs_3_), channel_id=1, source_target_pairs={{0,2},{1,3},{2,0},{3,1},{4,6},{5,7},{6,4},{7,5},{8,10},{9,11},{10,... | collective-permute-start | bytes 49160 | tf_op jit(solution)/shard_map/ppermute | solution.py:18
  27.6 5.5 %collective-permute-start.2 = (bf16[64,128]{1,0:T(8,128)(2,1)S(1)}, bf16[64,128]{1,0:T(8,128)(2,1)S(1)}, u32[]{:S(2)}, u32[]{:S(2)}) collective-permute-start(bf16[64,128]{1,0:T(8,128)(2,1)S(1)} %get-tuple-element.34.refs_3_), channel_id=1, source_target_pairs={{0,3},{1,2},{2,1},{3,0},{4,7},{5,6},{6,5},{7,4},{8,11},{9,10},{10,... | collective-permute-start | bytes 49160 | tf_op jit(solution)/shard_map/ppermute | solution.py:18
  40.3 15.5 %copy-start.1 = (bf16[128,2560]{1,0:T(8,128)(2,1)S(1)}, bf16[128,2560]{1,0:T(8,128)(2,1)}, u32[]{:S(2)}) copy-start(bf16[128,2560]{1,0:T(8,128)(2,1)} %get-tuple-element.37) | copy-start | bytes 1966084
  40.3 15.5 %collective-permute-start.7 = (bf16[128,2560]{1,0:T(8,128)(2,1)}, bf16[128,2560]{1,0:T(8,128)(2,1)S(1)}, u32[]{:S(2)}, u32[]{:S(2)}) collective-permute-start(bf16[128,2560]{1,0:T(8,128)(2,1)} %get-tuple-element.37), channel_id=1, source_target_pairs={{0,1},{3,2},{4,5},{7,6},{8,9},{11,10},{12,13},{15,14},{16,17},{19,... | collective-permute-start | bytes 1966088 | tf_op jit(solution)/shard_map/ppermute | solution.py:482
  50.2 5.8 %collective-permute-start.13 = (bf16[64,128]{1,0:T(8,128)(2,1)S(1)}, bf16[64,128]{1,0:T(8,128)(2,1)S(1)}, u32[]{:S(2)}, u32[]{:S(2)}) collective-permute-start(bf16[64,128]{1,0:T(8,128)(2,1)S(1)} %get-tuple-element.45.refs_3_), channel_id=1, source_target_pairs={{0,1},{1,0},{2,3},{3,2},{4,5},{5,4},{6,7},{7,6},{8,9},{9,8},{10,11... | collective-permute-start | bytes 49160 | tf_op jit(solution)/shard_map/ppermute | solution.py:18
  50.2 5.8 %collective-permute-start.12 = (bf16[64,128]{1,0:T(8,128)(2,1)S(1)}, bf16[64,128]{1,0:T(8,128)(2,1)S(1)}, u32[]{:S(2)}, u32[]{:S(2)}) collective-permute-start(bf16[64,128]{1,0:T(8,128)(2,1)S(1)} %get-tuple-element.45.refs_3_), channel_id=1, source_target_pairs={{0,2},{1,3},{2,0},{3,1},{4,6},{5,7},{6,4},{7,5},{8,10},{9,11},{10,... | collective-permute-start | bytes 49160 | tf_op jit(solution)/shard_map/ppermute | solution.py:18
  53.1 5.8 %collective-permute-start.11 = (bf16[64,128]{1,0:T(8,128)(2,1)S(1)}, bf16[64,128]{1,0:T(8,128)(2,1)S(1)}, u32[]{:S(2)}, u32[]{:S(2)}) collective-permute-start(bf16[64,128]{1,0:T(8,128)(2,1)S(1)} %get-tuple-element.45.refs_3_), channel_id=1, source_target_pairs={{0,3},{1,2},{2,1},{3,0},{4,7},{5,6},{6,5},{7,4},{8,11},{9,10},{10,... | collective-permute-start | bytes 49160 | tf_op jit(solution)/shard_map/ppermute | solution.py:18
  58.9 9.9 %copy-start.7 = (bf16[64,2560]{1,0:T(8,128)(2,1)S(1)}, bf16[64,2560]{1,0:T(8,128)(2,1)}, u32[]{:S(2)}) copy-start(bf16[64,2560]{1,0:T(8,128)(2,1)} %get-tuple-element.39) | copy-start | bytes 983044
  64.2 21.2 %copy-start.8 = (bf16[64,2560]{1,0:T(8,128)(2,1)S(1)}, bf16[64,2560]{1,0:T(8,128)(2,1)}, u32[]{:S(2)}) copy-start(bf16[64,2560]{1,0:T(8,128)(2,1)} %get-tuple-element.49) | copy-start | bytes 983044
  64.3 25.8 %copy-start.4 = (bf16[64,2560]{1,0:T(8,128)(2,1)S(1)}, bf16[64,2560]{1,0:T(8,128)(2,1)}, u32[]{:S(2)}) copy-start(bf16[64,2560]{1,0:T(8,128)(2,1)} %get-tuple-element.36) | copy-start | bytes 983044
  64.3 17.8 %collective-permute-start.14 = (bf16[128,2560]{1,0:T(8,128)(2,1)}, bf16[128,2560]{1,0:T(8,128)(2,1)S(1)}, u32[]{:S(2)}, u32[]{:S(2)}) collective-permute-start(bf16[128,2560]{1,0:T(8,128)(2,1)} %get-tuple-element.47), channel_id=1, source_target_pairs={{0,1},{3,2},{4,5},{7,6},{8,9},{11,10},{12,13},{15,14},{16,17},{19,... | collective-permute-start | bytes 1966088 | tf_op jit(solution)/shard_map/ppermute | solution.py:482
  66.8 18.7 %collective-permute-start.10 = (bf16[64,2560]{1,0:T(8,128)(2,1)S(1)}, bf16[64,2560]{1,0:T(8,128)(2,1)S(1)}, u32[]{:S(2)}, u32[]{:S(2)}) collective-permute-start(bf16[64,2560]{1,0:T(8,128)(2,1)S(1)} %get-tuple-element.55), channel_id=1, source_target_pairs={{1,3},{2,0},{5,7},{6,4},{9,11},{10,8},{13,15},{14,12},{17,19},{18,... | collective-permute-start | bytes 983048 | tf_op jit(solution)/shard_map/ppermute | solution.py:489
  68.1 22.0 %collective-permute-start.9 = (bf16[64,2560]{1,0:T(8,128)(2,1)S(1)}, bf16[64,2560]{1,0:T(8,128)(2,1)S(1)}, u32[]{:S(2)}, u32[]{:S(2)}) collective-permute-start(bf16[64,2560]{1,0:T(8,128)(2,1)S(1)} %get-tuple-element.56), channel_id=1, source_target_pairs={{1,2},{2,1},{5,6},{6,5},{9,10},{10,9},{13,14},{14,13},{17,18},{18,... | collective-permute-start | bytes 983048 | tf_op jit(solution)/shard_map/ppermute | solution.py:488
  68.8 21.3 %collective-permute-start.8 = (bf16[64,2560]{1,0:T(8,128)(2,1)S(1)}, bf16[64,2560]{1,0:T(8,128)(2,1)S(1)}, u32[]{:S(2)}, u32[]{:S(2)}) collective-permute-start(bf16[64,2560]{1,0:T(8,128)(2,1)S(1)} %copy-done.7), channel_id=1, source_target_pairs={{0,1},{1,0},{2,3},{3,2},{4,5},{5,4},{6,7},{7,6},{8,9},{9,8},{10,11... | collective-permute-start | bytes 983048 | tf_op jit(solution)/shard_map/ppermute | solution.py:18
  83.3 15.3 %copy-start.5 = (bf16[64,2560]{1,0:T(8,128)(2,1)S(1)}, bf16[64,2560]{1,0:T(8,128)(2,1)}, u32[]{:S(2)}) copy-start(bf16[64,2560]{1,0:T(8,128)(2,1)} %get-tuple-element.46) | copy-start | bytes 983044
  83.3 6.9 %collective-permute-start.16 = (bf16[64,2560]{1,0:T(8,128)(2,1)S(1)}, bf16[64,2560]{1,0:T(8,128)(2,1)S(1)}, u32[]{:S(2)}, u32[]{:S(2)}) collective-permute-start(bf16[64,2560]{1,0:T(8,128)(2,1)S(1)} %get-tuple-element.53), channel_id=1, source_target_pairs={{1,2},{2,1},{5,6},{6,5},{9,10},{10,9},{13,14},{14,13},{17,18},{18,... | collective-permute-start | bytes 983048 | tf_op jit(solution)/shard_map/ppermute | solution.py:488
  84.1 13.7 %collective-permute-start.17 = (bf16[64,2560]{1,0:T(8,128)(2,1)S(1)}, bf16[64,2560]{1,0:T(8,128)(2,1)S(1)}, u32[]{:S(2)}, u32[]{:S(2)}) collective-permute-start(bf16[64,2560]{1,0:T(8,128)(2,1)S(1)} %get-tuple-element.54), channel_id=1, source_target_pairs={{1,3},{2,0},{5,7},{6,4},{9,11},{10,8},{13,15},{14,12},{17,19},{18,... | collective-permute-start | bytes 983048 | tf_op jit(solution)/shard_map/ppermute | solution.py:489
  85.4 13.1 %collective-permute-start.15 = (bf16[64,2560]{1,0:T(8,128)(2,1)S(1)}, bf16[64,2560]{1,0:T(8,128)(2,1)S(1)}, u32[]{:S(2)}, u32[]{:S(2)}) collective-permute-start(bf16[64,2560]{1,0:T(8,128)(2,1)S(1)} %copy-done.8), channel_id=1, source_target_pairs={{0,1},{1,0},{2,3},{3,2},{4,5},{5,4},{6,7},{7,6},{8,9},{9,8},{10,11... | collective-permute-start | bytes 983048 | tf_op jit(solution)/shard_map/ppermute | solution.py:18
  (3 other events, 3.7 us)

commit v3 on v2

--- a/solution.py
+++ b/solution.py
@@ -112,7 +112,7 @@
     w_logit_ref,
     table_ref,
     scalar_ref,
-    soft_ref,
+    shown_ref,
     coded_ref,
     window_ref,
     position_ref,
@@ -124,7 +124,6 @@
     place_ref,
     xyz_ref,
     message_ref,
-    soft_buf,
     arrived,
 ):
     neighbour_count, residues = link_ref.shape
@@ -176,8 +175,10 @@
     lane = lax.broadcasted_iota(jnp.int32, (rows_at_once, LANES), 1)
     centres = 2.0 + (20.0 / (bins - 1)) * lane.astype(F32)
 
-    def one_chunk(step, carry):
-        begin = pl.multiple_of(step * rows_at_once, rows_at_once)
+    lane_short = lane.astype(jnp.int16)
+    one, zero = jnp.ones((), BF16), jnp.zeros((), BF16)
+    count = message_ref.shape[0]
+    for begin in range(0, count, rows_at_once):
         first = first_row + begin
         links = place_ref[pl.ds(first, rows_at_once), :]
         keep = (links < residue_count) & (lane < neighbour_count)
@@ -201,8 +202,9 @@
         rows = []
         for k in range(neighbour_count):
             place_k = jnp.broadcast_to(place[:, k : k + 1], (rows_at_once, LANES))
+            place_k = place_k.astype(jnp.int16)
             parts = [
-                jnp.where(place_k == lane + slot * residues, 1.0, 0.0).astype(BF16)
+                jnp.where(place_k == lane_short + jnp.int16(slot * residues), one, zero)
                 for slot in range(3)
             ]
             distance_k = jnp.broadcast_to(distance[:, k : k + 1], (rows_at_once, LANES))
@@ -219,10 +221,6 @@
             message_ref[pl.ds(begin, rows_at_once), cols] = jnp.sum(
                 doubled.reshape(neighbour_count, rows_at_once, width), axis=0
             ) * (0.5 / 30.0)
-        return carry
-
-    count = message_ref.shape[0]
-    lax.fori_loop(0, count // rows_at_once, one_chunk, 0)
 
     for copy in copies[len(early) :]:
         copy.wait()
@@ -253,9 +251,7 @@
         axis=0,
     ).astype(BF16)
     soft = (jnp.dot(probability, table, preferred_element_type=F32) * valid).astype(BF16)
-    soft_buf[...] = soft
-    leaving = pltpu.make_async_copy(soft_buf, soft_ref, arrived.at[len(copies)])
-    leaving.start()
+    shown_ref[...] = (probability.astype(F32) * valid).astype(BF16)
     soft_wide = soft.astype(F32)
     soft_centred = soft_wide - jnp.mean(soft_wide, axis=1, keepdims=True)
     soft_spread = jnp.mean(soft_centred * soft_centred, axis=1, keepdims=True)
@@ -269,7 +265,6 @@
         depth = w_up_buf.shape[0]
         part = scaled_ref[:, pl.ds(pl.multiple_of(scalar_ref[2] * depth, LANES), depth)]
         token_ref[...] = jnp.dot(part, w_up_buf[...], preferred_element_type=F32)
-    leaving.wait()
 
 
 def messages(own, side, other, feats, links, w_rbf, gain, w_logit, table, scalars, rows, tokens):
@@ -281,7 +276,7 @@
     in_vmem = pl.BlockSpec(memory_space=pltpu.VMEM)
     in_hbm_spec = pl.BlockSpec(memory_space=pltpu.HBM)
     arrays = [own, side, other, feats, links, w_rbf, gain, w_logit, table, *tokens]
-    out_shape = [pltpu.HBM((count, embed_dim), BF16), jax.ShapeDtypeStruct((count, LANES), BF16)]
+    out_shape = [jax.ShapeDtypeStruct((count, LANES), BF16)] * 2
     scratch = [
         pltpu.VMEM((depth, feature_dim), BF16),
         pltpu.VMEM((3, COORD_ROWS, residues), BF16),
@@ -293,7 +288,6 @@
         pltpu.VMEM((residues, LANES), jnp.int32),
         pltpu.VMEM((residues, LANES), F32),
         pltpu.VMEM((count, feature_dim), F32),
-        pltpu.VMEM((count, embed_dim), BF16),
         pltpu.SemaphoreType.DMA((16,)),
     ]
     if tokens:
@@ -308,7 +302,7 @@
         functools.partial(message_kernel, min(32, count), rows[0], bool(tokens)),
         out_shape=out_shape,
         in_specs=[in_hbm_spec] * len(arrays) + [pl.BlockSpec(memory_space=pltpu.SMEM)],
-        out_specs=[in_hbm_spec] + [in_vmem] * (len(out_shape) - 1),
+        out_specs=[in_vmem] * len(out_shape),
         scratch_shapes=scratch,
         compiler_params=pltpu.CompilerParams(vmem_limit_bytes=20 << 20),
         cost_estimate=pl.CostEstimate(
@@ -323,10 +317,16 @@
     return (0.5 * total * (1.0 + lax.erf(total * (0.5**0.5)))).astype(BF16)
 
 
-def trunk_kernel(columns, targets, *refs):
-    coded, up_ref = refs[:4], refs[4]
-    weights = refs[5 : 5 + len(columns)]
-    outs = refs[5 + len(columns) : -5]
+def trunk_kernel(blocks, columns, targets, table_columns, *refs):
+    coded, up_ref, refs = refs[:blocks], refs[blocks], refs[blocks + 1 :]
+    weights, refs = refs[: len(columns)], refs[len(columns) :]
+    if table_columns:
+        shown_ref, turn_ref, table_ref, refs = refs[0], refs[1], refs[2], refs[3:]
+        refs, (table_raw, table_buf, base_buf, extra) = refs[:-4], refs[-4:]
+        base_ref, refs = refs[0], refs[1:]
+        fetching = pltpu.make_async_copy(table_ref, table_raw, extra.at[0])
+        fetching.start()
+    outs = refs[:-5]
     buffer, inner, results, arrived, left = refs[-5:]
     chunk = buffer.shape[2]
     copies = [
@@ -344,6 +344,24 @@
     for place, copy in enumerate(copies):
         copy.wait()
         value = jnp.dot(inner[...], buffer[place], preferred_element_type=F32)
+        if table_columns:
+            if place == 0:
+                fetching.wait()
+                filler = (table_buf.shape[0] - table_raw.shape[0], table_raw.shape[1])
+                table_buf[...] = jnp.concatenate(
+                    [table_raw[...].astype(F32), jnp.zeros(filler, F32)], axis=0
+                ).astype(BF16)
+            half_width = table_buf.shape[1] // 2
+            first = pl.multiple_of(
+                lax.rem(turn_ref[0] * half_width + table_columns[place], 2 * half_width), LANES
+            )
+            soft = jnp.dot(
+                shown_ref[...], table_buf[:, pl.ds(first, chunk)], preferred_element_type=F32
+            )
+            base_buf[:, place * chunk : (place + 1) * chunk] = value[
+                (blocks - 1) * rows :
+            ].astype(BF16).astype(F32) + soft.astype(BF16).astype(F32)
+            value = value[: (blocks - 1) * rows]
         results[place] = value.astype(BF16)
         for number, (start, stop) in enumerate(targets):
             leaving.append(
@@ -354,36 +372,62 @@
                 )
             )
             leaving[-1].start()
+    if table_columns:
+        leaving.append(pltpu.make_async_copy(base_buf, base_ref, extra.at[1]))
+        leaving[-1].start()
     for copy in leaving:
         copy.wait()
 
 
-def trunk(coded, up, pieces, targets, chunk):
+def trunk(coded, up, pieces, targets, chunk, shown=None, turn=None, table=None):
+    with_base = table is not None
+    kept = len(coded) - with_base
     rows, hidden = coded[0].shape[0], up.shape[1]
     in_vmem = pl.BlockSpec(memory_space=pltpu.VMEM)
     hbm_spec = pl.BlockSpec(memory_space=pltpu.HBM)
     return pl.pallas_call(
-        functools.partial(trunk_kernel, [column for _, column in pieces], targets),
-        out_shape=[
-            pltpu.HBM((stop - start, len(pieces) * chunk), BF16) for start, stop in targets
-        ],
-        in_specs=[in_vmem] * 5 + [hbm_spec] * len(pieces),
-        out_specs=[hbm_spec] * len(targets),
+        functools.partial(
+            trunk_kernel,
+            len(coded),
+            [column for _, column in pieces],
+            targets,
+            [place * chunk for place in range(len(pieces))] if with_base else (),
+        ),
+        out_shape=[pltpu.HBM((rows, len(pieces) * chunk), F32)] * with_base
+        + [pltpu.HBM((stop - start, len(pieces) * chunk), BF16) for start, stop in targets],
+        in_specs=[in_vmem] * (len(coded) + 1) + [pl.BlockSpec(memory_space=pl.ANY)] * len(pieces)
+        + [in_vmem, pl.BlockSpec(memory_space=pltpu.SMEM), hbm_spec] * with_base,
+        out_specs=[hbm_spec] * (with_base + len(targets)),
         scratch_shapes=[
             pltpu.VMEM((len(pieces), hidden, chunk), BF16),
-            pltpu.VMEM((4 * rows, hidden), BF16),
-            pltpu.VMEM((len(pieces), 4 * rows, chunk), BF16),
+            pltpu.VMEM((len(coded) * rows, hidden), BF16),
+            pltpu.VMEM((len(pieces), kept * rows, chunk), BF16),
             pltpu.SemaphoreType.DMA((len(pieces),)),
             pltpu.SemaphoreType.DMA((len(pieces) * len(targets),)),
-        ],
+        ]
+        + (
+            [
+                pltpu.VMEM(table.shape, BF16),
+                pltpu.VMEM((LANES, table.shape[1]), BF16),
+                pltpu.VMEM((rows, len(pieces) * chunk), F32),
+                pltpu.SemaphoreType.DMA((2,)),
+            ]
+            if with_base
+            else []
+        ),
         compiler_params=pltpu.CompilerParams(vmem_limit_bytes=16 << 20),
         cost_estimate=pl.CostEstimate(
-            flops=8 * rows * len(pieces) * hidden * chunk,
+            flops=2 * len(coded) * rows * len(pieces) * hidden * chunk,
             bytes_accessed=2 * hidden * chunk * len(pieces),
-            transcendentals=4 * rows * hidden,
+            transcendentals=len(coded) * rows * hidden,
         ),
         name="trunk",
-    )(*coded, up, *in_hbm(*[array for array, _ in pieces]))
+    )(
+        *coded,
+        up,
+        *[array for array, _ in pieces],
+        *((shown, turn, in_hbm(table)[0]) if with_base else ()),
+    )
 
 
 def rounded_sum(left, right):
@@ -418,30 +462,25 @@
 
     scalars = jnp.stack([block_index.astype(jnp.int32), counts[0], seq_index.astype(jnp.int32)])
 
-    def some_messages(first, last, tokens):
-        return messages(
-            own,
-            side,
-            other,
-            node_feats[0],
-            neighbours[0].T,
-            w_rbf,
-            gen_gain[None, :],
-            w_logit.T,
-            embed_table,
-            scalars,
-            (first, last),
-            tokens,
-        )
-
-    if seq_count == 2 and w_up.shape[0] % LANES == 0:
-        soft_a, coded_a, token_up = some_messages(
-            0, residues // 2, (trunk_gain[None, :], w_up)
-        )
-        token_up = (token_up + swap(token_up, "seq", 1)).astype(BF16)
-        whole = [w_down, swap(w_down, "seq", 1)]
+    in_kernel = seq_count == 2 and w_up.shape[0] % LANES == 0
+    shown, coded, *token_up = messages(
+        own,
+        side,
+        other,
+        node_feats[0],
+        neighbours[0].T,
+        w_rbf,
+        gen_gain[None, :],
+        w_logit.T,
+        embed_table,
+        scalars,
+        (0, residues),
+        (trunk_gain[None, :], w_up) if in_kernel else (),
+    )
+    if in_kernel:
+        token_up = (token_up[0] + swap(token_up[0], "seq", 1)).astype(BF16)
+        whole = in_hbm(w_down) + [swap(w_down, "seq", 1)]
     else:
-        soft_a, coded_a = some_messages(0, residues // 2, ())
         table_wide = embed_table.astype(F32)
         table_centred = table_wide - jnp.mean(table_wide, axis=1, keepdims=True)
         table_scaled = jnp.pad(
@@ -454,51 +493,52 @@
             jnp.dot(table_part, w_up, preferred_element_type=F32), "seq"
         ).astype(BF16)
         whole = [lax.all_gather(w_down, "seq", axis=1, tiled=True)]
-    soft_b, coded_b = some_messages(residues // 2, residues, ())
-    soft = jnp.concatenate([soft_a, soft_b], axis=0)
     chunk = embed_dim // 4
     pieces = [(part, first) for part in whole for first in range(0, part.shape[1], chunk)]
 
-    part_rows = residues // 2
     inward = [(0, 1), (3, 2)]
     crossing = [(1, 2), (2, 1)]
     skipping = [(1, 3), (2, 0)]
+    coded_3, coded_2, coded_1 = [swap(coded, "mp", step) for step in (3, 2, 1)]
+    coded_3, coded_2, coded_1, token_up = lax.optimization_barrier(
+        (coded_3, coded_2, coded_1, token_up)
+    )
+    pairs = [(0, 2 * residues)]
+    (far_a,) = trunk([coded_3, coded_2], token_up, pieces[:2], pairs, chunk)
+    coded_1, _ = lax.optimization_barrier((coded_1, far_a))
+    turn = seq_index.astype(jnp.int32) if len(whole) == 2 else jnp.zeros((), jnp.int32)
+    base, near = trunk(
+        [coded_1, coded],
+        token_up,
+        pieces,
+        [(0, residues)],
+        chunk,
+        shown,
+        turn[None],
+        embed_table,
+    )
+    coded_3, _ = lax.optimization_barrier((coded_3, near))
+    (far_b,) = trunk([coded_3, coded_2], token_up, pieces[2:], pairs, chunk)
+    arrived_a = lax.ppermute(far_a, "mp", inward)
+    to_edge = lax.ppermute(near, "mp", [(1, 0), (2, 3)])
+    arrived_b = lax.ppermute(far_b, "mp", inward)
+    arrived_a, far_a, _ = lax.optimization_barrier((arrived_a, far_a, far_b))
+    near, _ = lax.optimization_barrier((near, arrived_b))
+    to_inner = lax.ppermute(near, "mp", inward)
     sums = []
-    order = ()
-    for coded in (coded_a, coded_b):
-        coded_rows = [swap(coded, "mp", step) for step in (3, 2, 1)] + [coded]
-        coded_rows, order = lax.optimization_barrier((coded_rows, order))
-        far, near, held = trunk(
-            coded_rows,
-            token_up,
-            pieces,
-            [
-                (0, 2 * part_rows),
-                (2 * part_rows, 3 * part_rows),
-                (3 * part_rows, 4 * part_rows),
-            ],
-            chunk,
-        )
-        arrived = lax.ppermute(far, "mp", inward)
-        arrived, near = lax.optimization_barrier((arrived, near))
-        swapped = swap(near, "mp", 1)
-        across = rounded_sum(far[:part_rows], arrived[part_rows:])
-        beyond = rounded_sum(far[part_rows:], arrived[:part_rows])
-        order = (across, beyond)
+    for far, arrived in ((far_a, arrived_a), (far_b, arrived_b)):
+        across = rounded_sum(far[:residues], arrived[residues:])
+        beyond = rounded_sum(far[residues:], arrived[:residues])
         across = lax.ppermute(across, "mp", crossing)
         beyond = lax.ppermute(beyond, "mp", skipping)
-        sums.append(
-            held.astype(F32)
-            + swapped.astype(F32)
-            + across.astype(F32)
-            + beyond.astype(F32)
-        )
-    total = jnp.concatenate(sums, axis=0)
+        sums.append(across.astype(F32) + beyond.astype(F32))
+    total = base + to_edge.astype(F32) + to_inner.astype(F32)
+    total = total + jnp.concatenate(sums, axis=1)
     if len(whole) == 2:
         middle = embed_dim // 2
         turned = jnp.concatenate([total[:, middle:], total[:, :middle]], axis=1)
         total = jnp.where(seq_index == 0, total, turned)
-    return (soft.astype(F32) + total).astype(BF16)[None]
+    return total.astype(BF16)[None]
 
 
 def solution(mesh):

time: 101 us -> 92.1 us (0.912)
  starting transfers between devices: 33.9 us -> 26.1 us
  waiting for transfers between devices: 30.3 us -> 34.1 us
  Pallas kernels: 29.5 us -> 26.9 us
  local copies, waits for them, and re-layouts: 3.26 us -> 0.66 us
    ppermute x11 -> x6, starting transfers between devices: 24.1 us -> 9.72 us  [swap(): return lax.ppermute(value, axis, [(i, i ^ step) for i in range(count)])]
    ppermute x2 -> x4, starting transfers between devices: 4.32 us -> 11 us  [the longest x1 4.31 us: on_device(): to_inner = lax.ppermute(near, 'mp', inward)]
    ppermute x2, waiting for transfers between devices: 7.64 us -> 13.3 us  [on_device(): beyond = lax.ppermute(beyond, 'mp', skipping)]
    ppermute x11 -> x6, waiting for transfers between devices: 13.6 us -> 8.88 us  [swap(): return lax.ppermute(value, axis, [(i, i ^ step) for i in range(count)])]
    pallas_call x2 -> x1, Pallas kernels: 16.1 us -> 11.8 us  [messages(): pl.pallas_call(functools.partial(message_kernel, min(32, count), rows[0],...]
    ppermute x2 -> x4, waiting for transfers between devices: 9.11 us -> 11.8 us  [the longest x1 8.63 us: on_device(): arrived_b = lax.ppermute(far_b, 'mp', inward)]
    unnamed x18 -> x8, local copies, waits for them, and re-layouts: 2.66 us -> 0.02 us
    pallas_call x2 -> x3, Pallas kernels: 10.7 us -> 12.5 us  [trunk(): pl.pallas_call(functools.partial(trunk_kernel, len(coded), [column for _,...]
  transfers between devices with their start and end apart: 18 -> 15, of which waited for: 9 -> 6; matrix products, arithmetic and copies ran while one was open for 2% -> 3% of each run, Pallas kernels for 19% -> 29%
where the time goes in v3:
time: 92.1 us; the launch traced here: 91.8 us
  waiting for transfers between devices  34.1 us (37%)
  Pallas kernels  26.9 us (29%)
  starting transfers between devices  26.1 us (28%)
  other arithmetic  3.07 us (3%)
    ppermute x2, waiting for transfers between devices, on_device(): beyond = lax.ppermute(beyond, 'mp', skipping)  13.3 us
    pallas_call x3, Pallas kernels, trunk(): pl.pallas_call(functools.partial(trunk_kernel, len(coded), [column for _,...  12.5 us
    pallas_call x1, Pallas kernels, messages(): pl.pallas_call(functools.partial(message_kernel, min(32, count), rows[0],...  11.8 us
    ppermute x6, starting transfers between devices, swap(): return lax.ppermute(value, axis, [(i, i ^ step) for i in range(count)])  9.72 us
    ppermute x6, waiting for transfers between devices, swap(): return lax.ppermute(value, axis, [(i, i ^ step) for i in range(count)])  8.88 us
    ppermute x1, waiting for transfers between devices, on_device(): arrived_b = lax.ppermute(far_b, 'mp', inward)  8.63 us
    ppermute x1, starting transfers between devices, on_device(): to_inner = lax.ppermute(near, 'mp', inward)  4.31 us
    ppermute x1, starting transfers between devices, on_device(): arrived_a = lax.ppermute(far_a, 'mp', inward)  3.91 us
  transfers between devices with their start and end apart: 15, of which 6 were waited for; matrix products, arithmetic and copies ran while one was open for 3% of the time, Pallas kernels for 29%

profile of v3, /device:TPU:0, one launch (start us, length us, event | category | flops | bytes accessed | tf_op | source)
XLA Modules:
  0.0 91.8 jit_solution(2601791430958127885)
XLA Ops:
  0.5 2.6 %near_rows.1.refs_0_ = bf16[144,1024]{1,0:T(8,128)(2,1)} custom-call(bf16[128,1024]{1,0:T(8,128)(2,1)} %bitcast.11, bf16[3,128]{1,0:T(4,128)(2,1)} %bitcast.13, bf16[1024,1024]{1,0:T(8,128)(2,1)} %w_near_ref.1), custom_call_target="tpu_custom_call" | custom-call | tf_op jit(solution)/shard_map/near_rows/pallas_call | solution.py:66
  3.1 2.6 %collective-permute-start = (bf16[144,1024]{1,0:T(8,128)(2,1)}, bf16[144,1024]{1,0:T(8,128)(2,1)}, u32[]{:S(2)}, u32[]{:S(2)}) collective-permute-start(bf16[144,1024]{1,0:T(8,128)(2,1)} %near_rows.1.refs_0_), channel_id=1, source_target_pairs={{0,1},{1,0},{2,3},{3,2},{4,5},{5,4},{6,7},{7,6},{8,9},{9,8},{10,11... | collective-permute-start | bytes 884744 | tf_op jit(solution)/shard_map/ppermute | solution.py:18
  5.7 1.4 %collective-permute-start.1 = (bf16[144,1024]{1,0:T(8,128)(2,1)}, bf16[144,1024]{1,0:T(8,128)(2,1)}, u32[]{:S(2)}, u32[]{:S(2)}) collective-permute-start(bf16[144,1024]{1,0:T(8,128)(2,1)} %near_rows.1.refs_0_), channel_id=1, source_target_pairs={{1,2},{2,1},{5,6},{6,5},{9,10},{10,9},{13,14},{14,13},{17,18},{18,... | collective-permute-start | bytes 884744 | tf_op jit(solution)/shard_map/ppermute | solution.py:461
  8.4 5.3 %collective-permute-done.refs_1_ = bf16[144,1024]{1,0:T(8,128)(2,1)} collective-permute-done((bf16[144,1024]{1,0:T(8,128)(2,1)}, bf16[144,1024]{1,0:T(8,128)(2,1)}, u32[]{:S(2)}, u32[]{:S(2)}) %collective-permute-start) | collective-permute-done | bytes 294944 | tf_op jit(solution)/shard_map/ppermute | solution.py:18
  13.7 11.8 %messages.1 = (bf16[128,128]{1,0:T(8,128)(2,1)S(1)}, bf16[128,128]{1,0:T(8,128)(2,1)S(1)}, f32[64,1280]{1,0:T(8,128)S(1)}) custom-call(bf16[144,1024]{1,0:T(8,128)(2,1)} %near_rows.1.refs_0_, bf16[144,1024]{1,0:T(8,128)(2,1)} %collective-permute-done.refs_1_, bf16[144,1024]{1,0:T(8,128)(2,1)} %collective-permute-done.1.refs_2_, bf16[128,1024]{1,0:T(8,128)(2,1)} %bitcast.12, ...), custom_call_target="tpu_custom_call" | custom-call | flops 12800000000 | bytes 5000000 | tf_op jit(solution)/shard_map/messages/pallas_call | solution.py:301
  25.6 3.8 %collective-permute-start.2 = (bf16[128,128]{1,0:T(8,128)(2,1)S(1)}, bf16[128,128]{1,0:T(8,128)(2,1)S(1)}, u32[]{:S(2)}, u32[]{:S(2)}) collective-permute-start(bf16[128,128]{1,0:T(8,128)(2,1)S(1)} %get-tuple-element.19.refs_1_), channel_id=1, source_target_pairs={{0,3},{1,2},{2,1},{3,0},{4,7},{5,6},{6,5},{7,4},{8,11},{9,10},{10,... | collective-permute-start | bytes 98312 | tf_op jit(solution)/shard_map/ppermute | solution.py:18
  29.4 2.4 %collective-permute-start.3 = (bf16[128,128]{1,0:T(8,128)(2,1)S(1)}, bf16[128,128]{1,0:T(8,128)(2,1)S(1)}, u32[]{:S(2)}, u32[]{:S(2)}) collective-permute-start(bf16[128,128]{1,0:T(8,128)(2,1)S(1)} %get-tuple-element.19.refs_1_), channel_id=1, source_target_pairs={{0,2},{1,3},{2,0},{3,1},{4,6},{5,7},{6,4},{7,5},{8,10},{9,11},{10,... | collective-permute-start | bytes 98312 | tf_op jit(solution)/shard_map/ppermute | solution.py:18
  32.2 2.1 %collective-permute-done.3.refs_1_ = bf16[128,128]{1,0:T(8,128)(2,1)S(1)} collective-permute-done((bf16[128,128]{1,0:T(8,128)(2,1)S(1)}, bf16[128,128]{1,0:T(8,128)(2,1)S(1)}, u32[]{:S(2)}, u32[]{:S(2)}) %collective-permute-start.3) | collective-permute-done | bytes 32800 | tf_op jit(solution)/shard_map/ppermute | solution.py:18
  34.3 1.5 %collective-permute-done.4.refs_0_ = bf16[128,128]{1,0:T(8,128)(2,1)S(1)} collective-permute-done((bf16[128,128]{1,0:T(8,128)(2,1)S(1)}, bf16[128,128]{1,0:T(8,128)(2,1)S(1)}, u32[]{:S(2)}, u32[]{:S(2)}) %collective-permute-start.4) | collective-permute-done | bytes 32800 | tf_op jit(solution)/shard_map/ppermute | solution.py:18
  35.8 3.9 %trunk.3 = bf16[256,1280]{1,0:T(8,128)(2,1)} custom-call(bf16[128,128]{1,0:T(8,128)(2,1)S(1)} %collective-permute-done.2.refs_0_, bf16[128,128]{1,0:T(8,128)(2,1)S(1)} %collective-permute-done.3.refs_1_, bf16[64,1280]{1,0:T(8,128)(2,1)S(1)} %add_convert_fusion.4.refs_2_, bf16[1280,1280]{1,0:T(8,128)(2,1)} %refs_4_.3, bf16[1280,1280]{1,0:T(8,128)(2,1)} %refs_4_.3), custom_call_target="tpu_custom_call" | custom-call | flops 838860800 | bytes 3276800 | tf_op jit(solution)/shard_map/trunk/pallas_call | solution.py:388
  39.7 3.9 %collective-permute-start.10 = (bf16[256,1280]{1,0:T(8,128)(2,1)}, bf16[256,1280]{1,0:T(8,128)(2,1)}, u32[]{:S(2)}, u32[]{:S(2)}) collective-permute-start(bf16[256,1280]{1,0:T(8,128)(2,1)} %trunk.3), channel_id=1, source_target_pairs={{0,1},{3,2},{4,5},{7,6},{8,9},{11,10},{12,13},{15,14},{16,17},{19,... | collective-permute-start | bytes 1966088 | tf_op jit(solution)/shard_map/ppermute | solution.py:522
  43.6 5.8 %trunk.4 = (f32[128,2560]{1,0:T(8,128)}, bf16[128,2560]{1,0:T(8,128)(2,1)}) custom-call(bf16[128,128]{1,0:T(8,128)(2,1)S(1)} %collective-permute-done.4.refs_0_, bf16[128,128]{1,0:T(8,128)(2,1)S(1)} %get-tuple-element.19.refs_1_, bf16[64,1280]{1,0:T(8,128)(2,1)S(1)} %add_convert_fusion.4.refs_2_, bf16[1280,1280]{1,0:T(8,128)(2,1)} %refs_4_.3, ...), custom_call_target="tpu_custom_call" | custom-call | flops 1677721600 | bytes 6553600 | tf_op jit(solution)/shard_map/trunk/pallas_call | solution.py:388
  49.4 2.9 %trunk.5 = bf16[256,1280]{1,0:T(8,128)(2,1)} custom-call(bf16[128,128]{1,0:T(8,128)(2,1)S(1)} %collective-permute-done.2.refs_0_, bf16[128,128]{1,0:T(8,128)(2,1)S(1)} %collective-permute-done.3.refs_1_, bf16[64,1280]{1,0:T(8,128)(2,1)S(1)} %add_convert_fusion.4.refs_2_, bf16[1280,1280]{1,0:T(8,128)(2,1)S(1)} %collective-permute-done.6.refs_5_.refs_6_.refs_3_.refs_4_, ...), custom_call_target="tpu_custom_call" | custom-call | flops 838860800 | bytes 3276800 | tf_op jit(solution)/shard_map/trunk/pallas_call | solution.py:388
  52.2 1.5 %collective-permute-start.8 = (bf16[256,1280]{1,0:T(8,128)(2,1)}, bf16[256,1280]{1,0:T(8,128)(2,1)S(1)}, u32[]{:S(2)}, u32[]{:S(2)}) collective-permute-start(bf16[256,1280]{1,0:T(8,128)(2,1)} %trunk.5), channel_id=1, source_target_pairs={{0,1},{3,2},{4,5},{7,6},{8,9},{11,10},{12,13},{15,14},{16,17},{19,... | collective-permute-start | bytes 1966088 | tf_op jit(solution)/shard_map/ppermute | solution.py:524
  53.7 1.3 %collective-permute-start.7 = (bf16[128,2560]{1,0:T(8,128)(2,1)}, bf16[128,2560]{1,0:T(8,128)(2,1)S(1)}, u32[]{:S(2)}, u32[]{:S(2)}) collective-permute-start(bf16[128,2560]{1,0:T(8,128)(2,1)} %get-tuple-element.30), channel_id=1, source_target_pairs={{1,0},{2,3},{5,4},{6,7},{9,8},{10,11},{13,12},{14,15},{17,16},{18,... | collective-permute-start | bytes 1966088 | tf_op jit(solution)/shard_map/ppermute | solution.py:523
  55.0 3.2 %collective-permute-done.10 = bf16[256,1280]{1,0:T(8,128)(2,1)} collective-permute-done((bf16[256,1280]{1,0:T(8,128)(2,1)}, bf16[256,1280]{1,0:T(8,128)(2,1)}, u32[]{:S(2)}, u32[]{:S(2)}) %collective-permute-start.10) | collective-permute-done | bytes 655392 | tf_op jit(solution)/shard_map/ppermute | solution.py:522
  58.2 1.4 %add_convert_fusion.3 = (bf16[128,1280]{1,0:T(8,128)(2,1)S(1)}, bf16[128,1280]{1,0:T(8,128)(2,1)S(1)}) fusion(bf16[256,1280]{1,0:T(8,128)(2,1)} %collective-permute-done.10, bf16[256,1280]{1,0:T(8,128)(2,1)} %trunk.3), kind=kLoop, calls=%fused_computation.9 | loop fusion | flops 1310720 | bytes 1966080 | tf_op jit(solution)/shard_map/convert_element_type | solution.py:434
  59.7 0.7 collective-permute-start.11
  60.3 1.3 %collective-permute-start.12 = (bf16[128,1280]{1,0:T(8,128)(2,1)S(1)}, bf16[128,1280]{1,0:T(8,128)(2,1)S(1)}, u32[]{:S(2)}, u32[]{:S(2)}) collective-permute-start(bf16[128,1280]{1,0:T(8,128)(2,1)S(1)} %get-tuple-element.34), channel_id=1, source_target_pairs={{1,3},{2,0},{5,7},{6,4},{9,11},{10,8},{13,15},{14,12},{17,19},{18,... | collective-permute-start | bytes 983048 | tf_op jit(solution)/shard_map/ppermute | solution.py:533
  61.6 8.6 %collective-permute-done.8 = bf16[256,1280]{1,0:T(8,128)(2,1)S(1)} collective-permute-done((bf16[256,1280]{1,0:T(8,128)(2,1)}, bf16[256,1280]{1,0:T(8,128)(2,1)S(1)}, u32[]{:S(2)}, u32[]{:S(2)}) %collective-permute-start.8) | collective-permute-done | bytes 655392 | tf_op jit(solution)/shard_map/ppermute | solution.py:524
  70.3 4.3 %collective-permute-start.9 = (bf16[128,2560]{1,0:T(8,128)(2,1)S(1)}, bf16[128,2560]{1,0:T(8,128)(2,1)S(1)}, u32[]{:S(2)}, u32[]{:S(2)}) collective-permute-start(bf16[128,2560]{1,0:T(8,128)(2,1)S(1)} %copy-done.3), channel_id=1, source_target_pairs={{0,1},{3,2},{4,5},{7,6},{8,9},{11,10},{12,13},{15,14},{16,17},{19,... | collective-permute-start | bytes 1966088 | tf_op jit(solution)/shard_map/ppermute | solution.py:527
  75.5 1.4 %collective-permute-start.14 = (bf16[128,1280]{1,0:T(8,128)(2,1)S(1)}, bf16[128,1280]{1,0:T(8,128)(2,1)S(1)}, u32[]{:S(2)}, u32[]{:S(2)}) collective-permute-start(bf16[128,1280]{1,0:T(8,128)(2,1)S(1)} %get-tuple-element.36), channel_id=1, source_target_pairs={{1,3},{2,0},{5,7},{6,4},{9,11},{10,8},{13,15},{14,12},{17,19},{18,... | collective-permute-start | bytes 983048 | tf_op jit(solution)/shard_map/ppermute | solution.py:533
  77.0 13.3 %collective-permute-done.14 = bf16[128,1280]{1,0:T(8,128)(2,1)S(1)} collective-permute-done((bf16[128,1280]{1,0:T(8,128)(2,1)S(1)}, bf16[128,1280]{1,0:T(8,128)(2,1)S(1)}, u32[]{:S(2)}, u32[]{:S(2)}) %collective-permute-start.14) | collective-permute-done | bytes 327712 | tf_op jit(solution)/shard_map/ppermute | solution.py:533
  90.8 1.0 %fusion.1 = bf16[1,128,2560]{2,1,0:T(8,128)(2,1)} fusion(bf16[128,2560]{1,0:T(8,128)(2,1)S(1)} %maximum_add_fusion, bf16[128,1280]{1,0:T(8,128)(2,1)S(1)} %get-tuple-element.38, bf16[128,1280]{1,0:T(8,128)(2,1)S(1)} %get-tuple-element.37, pred[]{:T(512)S(6)} %eq.3), kind=kLoop, calls=%fused_computation.3 | loop fusion | flops 1638400 | bytes 1966081 | tf_op jit(solution)/shard_map/broadcast_in_dim | solution.py:541
  (29 shorter events, 2.8 us)
Async XLA Ops:
  0.0 43.6 %collective-permute-start.6 = (bf16[1280,1280]{1,0:T(8,128)(2,1)}, bf16[1280,1280]{1,0:T(8,128)(2,1)S(1)}, u32[]{:S(2)}, u32[]{:S(2)}) collective-permute-start(bf16[1280,1280]{1,0:T(8,128)(2,1)} %refs_4_.3), channel_id=1, source_target_pairs={{0,4},{4,0},{1,5},{5,1},{2,6},{6,2},{3,7},{7,3},{8,12},{12,8},{9,1... | collective-permute-start | bytes 9830408 | tf_op jit(solution)/shard_map/ppermute | solution.py:18
  0.5 7.3 %copy-start.2 = (f32[2560]{0:T(1024)S(1)}, f32[2560]{0:T(1024)}, u32[]{:S(2)}) copy-start(f32[2560]{0:T(1024)} %param.21) | copy-start | bytes 30724
  3.1 10.6 %collective-permute-start = (bf16[144,1024]{1,0:T(8,128)(2,1)}, bf16[144,1024]{1,0:T(8,128)(2,1)}, u32[]{:S(2)}, u32[]{:S(2)}) collective-permute-start(bf16[144,1024]{1,0:T(8,128)(2,1)} %near_rows.1.refs_0_), channel_id=1, source_target_pairs={{0,1},{1,0},{2,3},{3,2},{4,5},{5,4},{6,7},{7,6},{8,9},{9,8},{10,11... | collective-permute-start | bytes 884744 | tf_op jit(solution)/shard_map/ppermute | solution.py:18
  5.7 8.0 %collective-permute-start.1 = (bf16[144,1024]{1,0:T(8,128)(2,1)}, bf16[144,1024]{1,0:T(8,128)(2,1)}, u32[]{:S(2)}, u32[]{:S(2)}) collective-permute-start(bf16[144,1024]{1,0:T(8,128)(2,1)} %near_rows.1.refs_0_), channel_id=1, source_target_pairs={{1,2},{2,1},{5,6},{6,5},{9,10},{10,9},{13,14},{14,13},{17,18},{18,... | collective-permute-start | bytes 884744 | tf_op jit(solution)/shard_map/ppermute | solution.py:461
  25.5 6.6 %collective-permute-start.5 = (f32[64,1280]{1,0:T(8,128)S(1)}, f32[64,1280]{1,0:T(8,128)S(1)}, u32[]{:S(2)}, u32[]{:S(2)}) collective-permute-start(f32[64,1280]{1,0:T(8,128)S(1)} %get-tuple-element.20), channel_id=1, source_target_pairs={{0,4},{4,0},{1,5},{5,1},{2,6},{6,2},{3,7},{7,3},{8,12},{12,8},{9,1... | collective-permute-start | bytes 983048 | tf_op jit(solution)/shard_map/ppermute | solution.py:18
  25.6 6.6 %collective-permute-start.2 = (bf16[128,128]{1,0:T(8,128)(2,1)S(1)}, bf16[128,128]{1,0:T(8,128)(2,1)S(1)}, u32[]{:S(2)}, u32[]{:S(2)}) collective-permute-start(bf16[128,128]{1,0:T(8,128)(2,1)S(1)} %get-tuple-element.19.refs_1_), channel_id=1, source_target_pairs={{0,3},{1,2},{2,1},{3,0},{4,7},{5,6},{6,5},{7,4},{8,11},{9,10},{10,... | collective-permute-start | bytes 98312 | tf_op jit(solution)/shard_map/ppermute | solution.py:18
  29.4 4.9 %collective-permute-start.3 = (bf16[128,128]{1,0:T(8,128)(2,1)S(1)}, bf16[128,128]{1,0:T(8,128)(2,1)S(1)}, u32[]{:S(2)}, u32[]{:S(2)}) collective-permute-start(bf16[128,128]{1,0:T(8,128)(2,1)S(1)} %get-tuple-element.19.refs_1_), channel_id=1, source_target_pairs={{0,2},{1,3},{2,0},{3,1},{4,6},{5,7},{6,4},{7,5},{8,10},{9,11},{10,... | collective-permute-start | bytes 98312 | tf_op jit(solution)/shard_map/ppermute | solution.py:18
  31.9 3.9 %collective-permute-start.4 = (bf16[128,128]{1,0:T(8,128)(2,1)S(1)}, bf16[128,128]{1,0:T(8,128)(2,1)S(1)}, u32[]{:S(2)}, u32[]{:S(2)}) collective-permute-start(bf16[128,128]{1,0:T(8,128)(2,1)S(1)} %get-tuple-element.19.refs_1_), channel_id=1, source_target_pairs={{0,1},{1,0},{2,3},{3,2},{4,5},{5,4},{6,7},{7,6},{8,9},{9,8},{10,11... | collective-permute-start | bytes 98312 | tf_op jit(solution)/shard_map/ppermute | solution.py:18
  39.7 18.6 %collective-permute-start.10 = (bf16[256,1280]{1,0:T(8,128)(2,1)}, bf16[256,1280]{1,0:T(8,128)(2,1)}, u32[]{:S(2)}, u32[]{:S(2)}) collective-permute-start(bf16[256,1280]{1,0:T(8,128)(2,1)} %trunk.3), channel_id=1, source_target_pairs={{0,1},{3,2},{4,5},{7,6},{8,9},{11,10},{12,13},{15,14},{16,17},{19,... | collective-permute-start | bytes 1966088 | tf_op jit(solution)/shard_map/ppermute | solution.py:522
  52.2 18.1 %copy-start.3 = (bf16[128,2560]{1,0:T(8,128)(2,1)S(1)}, bf16[128,2560]{1,0:T(8,128)(2,1)}, u32[]{:S(2)}) copy-start(bf16[128,2560]{1,0:T(8,128)(2,1)} %get-tuple-element.30) | copy-start | bytes 1966084
  52.2 22.4 %copy-start = (bf16[256,1280]{1,0:T(8,128)(2,1)S(1)}, bf16[256,1280]{1,0:T(8,128)(2,1)}, u32[]{:S(2)}) copy-start(bf16[256,1280]{1,0:T(8,128)(2,1)} %trunk.5) | copy-start | bytes 1966084
  52.2 18.0 %collective-permute-start.8 = (bf16[256,1280]{1,0:T(8,128)(2,1)}, bf16[256,1280]{1,0:T(8,128)(2,1)S(1)}, u32[]{:S(2)}, u32[]{:S(2)}) collective-permute-start(bf16[256,1280]{1,0:T(8,128)(2,1)} %trunk.5), channel_id=1, source_target_pairs={{0,1},{3,2},{4,5},{7,6},{8,9},{11,10},{12,13},{15,14},{16,17},{19,... | collective-permute-start | bytes 1966088 | tf_op jit(solution)/shard_map/ppermute | solution.py:524
  53.7 36.7 %collective-permute-start.7 = (bf16[128,2560]{1,0:T(8,128)(2,1)}, bf16[128,2560]{1,0:T(8,128)(2,1)S(1)}, u32[]{:S(2)}, u32[]{:S(2)}) collective-permute-start(bf16[128,2560]{1,0:T(8,128)(2,1)} %get-tuple-element.30), channel_id=1, source_target_pairs={{1,0},{2,3},{5,4},{6,7},{9,8},{10,11},{13,12},{14,15},{17,16},{18,... | collective-permute-start | bytes 1966088 | tf_op jit(solution)/shard_map/ppermute | solution.py:523
  59.7 15.8 %collective-permute-start.11 = (bf16[128,1280]{1,0:T(8,128)(2,1)S(1)}, bf16[128,1280]{1,0:T(8,128)(2,1)S(1)}, u32[]{:S(2)}, u32[]{:S(2)}) collective-permute-start(bf16[128,1280]{1,0:T(8,128)(2,1)S(1)} %get-tuple-element.33), channel_id=1, source_target_pairs={{1,2},{2,1},{5,6},{6,5},{9,10},{10,9},{13,14},{14,13},{17,18},{18,... | collective-permute-start | bytes 983048 | tf_op jit(solution)/shard_map/ppermute | solution.py:532
  60.3 16.6 %collective-permute-start.12 = (bf16[128,1280]{1,0:T(8,128)(2,1)S(1)}, bf16[128,1280]{1,0:T(8,128)(2,1)S(1)}, u32[]{:S(2)}, u32[]{:S(2)}) collective-permute-start(bf16[128,1280]{1,0:T(8,128)(2,1)S(1)} %get-tuple-element.34), channel_id=1, source_target_pairs={{1,3},{2,0},{5,7},{6,4},{9,11},{10,8},{13,15},{14,12},{17,19},{18,... | collective-permute-start | bytes 983048 | tf_op jit(solution)/shard_map/ppermute | solution.py:533
  70.3 20.2 %collective-permute-start.9 = (bf16[128,2560]{1,0:T(8,128)(2,1)S(1)}, bf16[128,2560]{1,0:T(8,128)(2,1)S(1)}, u32[]{:S(2)}, u32[]{:S(2)}) collective-permute-start(bf16[128,2560]{1,0:T(8,128)(2,1)S(1)} %copy-done.3), channel_id=1, source_target_pairs={{0,1},{3,2},{4,5},{7,6},{8,9},{11,10},{12,13},{15,14},{16,17},{19,... | collective-permute-start | bytes 1966088 | tf_op jit(solution)/shard_map/ppermute | solution.py:527
  74.8 2.2 %collective-permute-start.13 = (bf16[128,1280]{1,0:T(8,128)(2,1)S(1)}, bf16[128,1280]{1,0:T(8,128)(2,1)S(1)}, u32[]{:S(2)}, u32[]{:S(2)}) collective-permute-start(bf16[128,1280]{1,0:T(8,128)(2,1)S(1)} %get-tuple-element.35), channel_id=1, source_target_pairs={{1,2},{2,1},{5,6},{6,5},{9,10},{10,9},{13,14},{14,13},{17,18},{18,... | collective-permute-start | bytes 983048 | tf_op jit(solution)/shard_map/ppermute | solution.py:532
  75.5 15.0 %copy-start.1 = (f32[128,2560]{1,0:T(8,128)S(1)}, f32[128,2560]{1,0:T(8,128)}, u32[]{:S(2)}) copy-start(f32[128,2560]{1,0:T(8,128)} %get-tuple-element.27) | copy-start | bytes 3932164
  75.5 14.9 %collective-permute-start.14 = (bf16[128,1280]{1,0:T(8,128)(2,1)S(1)}, bf16[128,1280]{1,0:T(8,128)(2,1)S(1)}, u32[]{:S(2)}, u32[]{:S(2)}) collective-permute-start(bf16[128,1280]{1,0:T(8,128)(2,1)S(1)} %get-tuple-element.36), channel_id=1, source_target_pairs={{1,3},{2,0},{5,7},{6,4},{9,11},{10,8},{13,15},{14,12},{17,19},{18,... | collective-permute-start | bytes 983048 | tf_op jit(solution)/shard_map/ppermute | solution.py:533

commit v4 on v3

--- a/solution.py
+++ b/solution.py
@@ -76,6 +76,29 @@
         ],
         name="near_rows",
     )(*in_hbm(feats, xyz, w_near))
+
+
+def token_kernel(turn_ref, table_ref, gain_ref, w_up_ref, out_ref, scaled_ref):
+    wide = table_ref[...].astype(F32)
+    wide = wide - jnp.mean(wide, axis=1, keepdims=True)
+    scaled = wide * gain_ref[...]
+    filler = jnp.zeros((scaled_ref.shape[0] - scaled.shape[0], scaled.shape[1]), F32)
+    scaled_ref[...] = jnp.concatenate([scaled, filler], axis=0).astype(BF16)
+    depth = w_up_ref.shape[0]
+    part = scaled_ref[:, pl.ds(pl.multiple_of(turn_ref[0] * depth, LANES), depth)]
+    out_ref[...] = jnp.dot(part, w_up_ref[...], preferred_element_type=F32)
+
+
+def token_rows(turn, table, gain, w_up):
+    in_vmem = pl.BlockSpec(memory_space=pltpu.VMEM)
+    return pl.pallas_call(
+        token_kernel,
+        out_shape=jax.ShapeDtypeStruct((LANES // 2, w_up.shape[1]), F32),
+        in_specs=[pl.BlockSpec(memory_space=pltpu.SMEM)] + [in_vmem] * 3,
+        out_specs=in_vmem,
+        scratch_shapes=[pltpu.VMEM((LANES // 2, table.shape[1]), BF16)],
+        name="token_rows",
+    )(turn, table, gain, w_up)
 
 
 def message_kernel(
@@ -326,24 +349,17 @@
         base_ref, refs = refs[0], refs[1:]
         fetching = pltpu.make_async_copy(table_ref, table_raw, extra.at[0])
         fetching.start()
-    outs = refs[:-5]
-    buffer, inner, results, arrived, left = refs[-5:]
-    chunk = buffer.shape[2]
-    copies = [
-        pltpu.make_async_copy(
-            ref.at[:, first : first + chunk], buffer.at[place], arrived.at[place]
-        )
-        for place, (ref, first) in enumerate(zip(weights, columns))
-    ]
-    for copy in copies:
-        copy.start()
+    outs = refs[:-3]
+    inner, results, left = refs[-3:]
+    chunk = results.shape[2]
     rows = coded[0].shape[0]
     for place, ref in enumerate(coded):
         inner[place * rows : (place + 1) * rows, :] = gelu_rows(ref[...], up_ref[...])
     leaving = []
-    for place, copy in enumerate(copies):
-        copy.wait()
-        value = jnp.dot(inner[...], buffer[place], preferred_element_type=F32)
+    for place, (ref, first) in enumerate(zip(weights, columns)):
+        value = jnp.dot(
+            inner[...], ref[:, first : first + chunk], preferred_element_type=F32
+        )
         if table_columns:
             if place == 0:
                 fetching.wait()
@@ -395,14 +411,12 @@
         ),
         out_shape=[pltpu.HBM((rows, len(pieces) * chunk), F32)] * with_base
         + [pltpu.HBM((stop - start, len(pieces) * chunk), BF16) for start, stop in targets],
-        in_specs=[in_vmem] * (len(coded) + 1) + [pl.BlockSpec(memory_space=pl.ANY)] * len(pieces)
+        in_specs=[in_vmem] * (len(coded) + 1) + [in_vmem] * len(pieces)
         + [in_vmem, pl.BlockSpec(memory_space=pltpu.SMEM), hbm_spec] * with_base,
         out_specs=[hbm_spec] * (with_base + len(targets)),
         scratch_shapes=[
-            pltpu.VMEM((len(pieces), hidden, chunk), BF16),
             pltpu.VMEM((len(coded) * rows, hidden), BF16),
             pltpu.VMEM((len(pieces), kept * rows, chunk), BF16),
-            pltpu.SemaphoreType.DMA((len(pieces),)),
             pltpu.SemaphoreType.DMA((len(pieces) * len(targets),)),
         ]
         + (
@@ -463,7 +477,12 @@
     scalars = jnp.stack([block_index.astype(jnp.int32), counts[0], seq_index.astype(jnp.int32)])
 
     in_kernel = seq_count == 2 and w_up.shape[0] % LANES == 0
-    shown, coded, *token_up = messages(
+    if in_kernel:
+        token_up = token_rows(
+            seq_index.astype(jnp.int32)[None], embed_table, trunk_gain[None, :], w_up
+        )
+        token_up = (token_up + swap(token_up, "seq", 1)).astype(BF16)
+    shown, coded = messages(
         own,
         side,
         other,
@@ -475,11 +494,10 @@
         embed_table,
         scalars,
         (0, residues),
-        (trunk_gain[None, :], w_up) if in_kernel else (),
+        (),
     )
     if in_kernel:
-        token_up = (token_up[0] + swap(token_up[0], "seq", 1)).astype(BF16)
-        whole = in_hbm(w_down) + [swap(w_down, "seq", 1)]
+        whole = [w_down] + [swap(w_down, "seq", 1)]
     else:
         table_wide = embed_table.astype(F32)
         table_centred = table_wide - jnp.mean(table_wide, axis=1, keepdims=True)

time: 92.1 us -> 88.3 us (0.959)
  waiting for transfers between devices: 34.1 us -> 28.7 us
  other arithmetic: 3.07 us -> 4.05 us
    ppermute x6, waiting for transfers between devices: 8.88 us -> 4.04 us  [swap(): return lax.ppermute(value, axis, [(i, i ^ step) for i in range(count)])]
    pallas_call x0 -> x1, Pallas kernels: none -> 3.62 us  [token_rows(): pl.pallas_call(token_kernel, out_shape=jax.ShapeDtypeStruct((LANES // 2,...]
    pallas_call x3, Pallas kernels: 12.5 us -> 9.07 us  [trunk(): pl.pallas_call(functools.partial(trunk_kernel, len(coded), [column for _,...]
    ppermute x1, waiting for transfers between devices: 3.21 us -> 4.78 us  [on_device(): arrived_a = lax.ppermute(far_a, 'mp', inward)]
    ppermute x2, waiting for transfers between devices: 13.3 us -> 12.3 us  [on_device(): beyond = lax.ppermute(beyond, 'mp', skipping)]
    ppermute x1, waiting for transfers between devices: 8.63 us -> 7.59 us  [on_device(): arrived_b = lax.ppermute(far_b, 'mp', inward)]
    convert_element_type x1, other arithmetic: 0.03 us -> 1.01 us  [on_device(): token_up = (token_up + swap(token_up, 'seq', 1)).astype(BF16)]
  transfers between devices with their start and end apart: 15 -> 15, of which waited for: 6 -> 6; matrix products, arithmetic and copies ran while one was open for 3% -> 4% of each run, Pallas kernels for 29% -> 31%
where the time goes in v4:
time: 88.3 us; the launch traced here: 87.9 us
  waiting for transfers between devices  28.7 us (33%)
  Pallas kernels  27 us (31%)
  starting transfers between devices  26.5 us (30%)
  other arithmetic  4.05 us (5%)
  between operations  0.89 us (1%)
    ppermute x2, waiting for transfers between devices, on_device(): beyond = lax.ppermute(beyond, 'mp', skipping)  12.3 us
    pallas_call x1, Pallas kernels, messages(): pl.pallas_call(functools.partial(message_kernel, min(32, count), rows[0],...  11.7 us
    ppermute x6, starting transfers between devices, swap(): return lax.ppermute(value, axis, [(i, i ^ step) for i in range(count)])  9.89 us
    pallas_call x3, Pallas kernels, trunk(): pl.pallas_call(functools.partial(trunk_kernel, len(coded), [column for _,...  9.07 us
    ppermute x1, waiting for transfers between devices, on_device(): arrived_b = lax.ppermute(far_b, 'mp', inward)  7.59 us
    ppermute x1, waiting for transfers between devices, on_device(): arrived_a = lax.ppermute(far_a, 'mp', inward)  4.78 us
    ppermute x1, starting transfers between devices, on_device(): to_inner = lax.ppermute(near, 'mp', inward)  4.31 us
    ppermute x1, starting transfers between devices, on_device(): arrived_a = lax.ppermute(far_a, 'mp', inward)  4.1 us
  transfers between devices with their start and end apart: 15, of which 6 were waited for; matrix products, arithmetic and copies ran while one was open for 4% of the time, Pallas kernels for 31%

profile of v4, /device:TPU:0, one launch (start us, length us, event | category | flops | bytes accessed | tf_op | source)
XLA Modules:
  0.0 87.9 jit_solution(16641149024679164902)
XLA Ops:
  0.5 2.6 %near_rows.1.refs_0_ = bf16[144,1024]{1,0:T(8,128)(2,1)} custom-call(bf16[128,1024]{1,0:T(8,128)(2,1)} %bitcast.11, bf16[3,128]{1,0:T(4,128)(2,1)} %bitcast.13, bf16[1024,1024]{1,0:T(8,128)(2,1)} %w_near_ref.1), custom_call_target="tpu_custom_call" | custom-call | tf_op jit(solution)/shard_map/near_rows/pallas_call | solution.py:66
  3.1 2.6 %collective-permute-start = (bf16[144,1024]{1,0:T(8,128)(2,1)}, bf16[144,1024]{1,0:T(8,128)(2,1)}, u32[]{:S(2)}, u32[]{:S(2)}) collective-permute-start(bf16[144,1024]{1,0:T(8,128)(2,1)} %near_rows.1.refs_0_), channel_id=1, source_target_pairs={{0,1},{1,0},{2,3},{3,2},{4,5},{5,4},{6,7},{7,6},{8,9},{9,8},{10,11... | collective-permute-start | bytes 884744 | tf_op jit(solution)/shard_map/ppermute | solution.py:18
  5.7 1.4 %collective-permute-start.1 = (bf16[144,1024]{1,0:T(8,128)(2,1)}, bf16[144,1024]{1,0:T(8,128)(2,1)}, u32[]{:S(2)}, u32[]{:S(2)}) collective-permute-start(bf16[144,1024]{1,0:T(8,128)(2,1)} %near_rows.1.refs_0_), channel_id=1, source_target_pairs={{1,2},{2,1},{5,6},{6,5},{9,10},{10,9},{13,14},{14,13},{17,18},{18,... | collective-permute-start | bytes 884744 | tf_op jit(solution)/shard_map/ppermute | solution.py:475
  7.8 3.6 %token_rows.1 = f32[64,1280]{1,0:T(8,128)} custom-call(s32[1]{0:T(128)} %bitcast.7.turn_ref.refs_8_, bf16[33,2560]{1,0:T(8,128)(2,1)} %refs_9_.1, f32[1,2560]{1,0:T(1,128)} %broadcast_in_dim.12.gain_ref, bf16[1280,1280]{1,0:T(8,128)(2,1)} %w_up_ref.1), custom_call_target="tpu_custom_call" | custom-call | tf_op jit(solution)/shard_map/token_rows/pallas_call | solution.py:94
  12.3 1.4 %collective-permute-done.refs_1_ = bf16[144,1024]{1,0:T(8,128)(2,1)} collective-permute-done((bf16[144,1024]{1,0:T(8,128)(2,1)}, bf16[144,1024]{1,0:T(8,128)(2,1)}, u32[]{:S(2)}, u32[]{:S(2)}) %collective-permute-start) | collective-permute-done | bytes 294944 | tf_op jit(solution)/shard_map/ppermute | solution.py:18
  13.7 11.7 %messages.1 = (bf16[128,128]{1,0:T(8,128)(2,1)S(1)}, bf16[128,128]{1,0:T(8,128)(2,1)S(1)}) custom-call(bf16[144,1024]{1,0:T(8,128)(2,1)} %near_rows.1.refs_0_, bf16[144,1024]{1,0:T(8,128)(2,1)} %collective-permute-done.refs_1_, bf16[144,1024]{1,0:T(8,128)(2,1)} %collective-permute-done.1.refs_2_, bf16[128,1024]{1,0:T(8,128)(2,1)} %bitcast.12, ...), custom_call_target="tpu_custom_call" | custom-call | flops 12800000000 | bytes 5000000 | tf_op jit(solution)/shard_map/messages/pallas_call | solution.py:324
  25.5 3.8 %collective-permute-start.2 = (bf16[128,128]{1,0:T(8,128)(2,1)S(1)}, bf16[128,128]{1,0:T(8,128)(2,1)S(1)}, u32[]{:S(2)}, u32[]{:S(2)}) collective-permute-start(bf16[128,128]{1,0:T(8,128)(2,1)S(1)} %get-tuple-element.18.refs_1_), channel_id=1, source_target_pairs={{0,3},{1,2},{2,1},{3,0},{4,7},{5,6},{6,5},{7,4},{8,11},{9,10},{10,... | collective-permute-start | bytes 98312 | tf_op jit(solution)/shard_map/ppermute | solution.py:18
  29.3 2.5 %collective-permute-start.3 = (bf16[128,128]{1,0:T(8,128)(2,1)S(1)}, bf16[128,128]{1,0:T(8,128)(2,1)S(1)}, u32[]{:S(2)}, u32[]{:S(2)}) collective-permute-start(bf16[128,128]{1,0:T(8,128)(2,1)S(1)} %get-tuple-element.18.refs_1_), channel_id=1, source_target_pairs={{0,2},{1,3},{2,0},{3,1},{4,6},{5,7},{6,4},{7,5},{8,10},{9,11},{10,... | collective-permute-start | bytes 98312 | tf_op jit(solution)/shard_map/ppermute | solution.py:18
  33.1 1.2 %collective-permute-done.3.refs_1_ = bf16[128,128]{1,0:T(8,128)(2,1)S(1)} collective-permute-done((bf16[128,128]{1,0:T(8,128)(2,1)S(1)}, bf16[128,128]{1,0:T(8,128)(2,1)S(1)}, u32[]{:S(2)}, u32[]{:S(2)}) %collective-permute-start.3) | collective-permute-done | bytes 32800 | tf_op jit(solution)/shard_map/ppermute | solution.py:18
  34.2 1.5 %collective-permute-done.4.refs_0_ = bf16[128,128]{1,0:T(8,128)(2,1)S(1)} collective-permute-done((bf16[128,128]{1,0:T(8,128)(2,1)S(1)}, bf16[128,128]{1,0:T(8,128)(2,1)S(1)}, u32[]{:S(2)}, u32[]{:S(2)}) %collective-permute-start.4) | collective-permute-done | bytes 32800 | tf_op jit(solution)/shard_map/ppermute | solution.py:18
  35.7 2.2 %trunk.3 = bf16[256,1280]{1,0:T(8,128)(2,1)} custom-call(bf16[128,128]{1,0:T(8,128)(2,1)S(1)} %collective-permute-done.2.refs_0_, bf16[128,128]{1,0:T(8,128)(2,1)S(1)} %collective-permute-done.3.refs_1_, bf16[64,1280]{1,0:T(8,128)(2,1)S(1)} %add_convert_fusion.4.refs_2_, bf16[1280,1280]{1,0:T(8,128)(2,1)S(1)} %copy-done, bf16[1280,1280]{1,0:T(8,128)(2,1)S(1)} %copy-done), custom_call_target="tpu_custom_call" | custom-call | flops 838860800 | bytes 3276800 | tf_op jit(solution)/shard_map/trunk/pallas_call | solution.py:404
  37.9 4.1 %collective-permute-start.10 = (bf16[256,1280]{1,0:T(8,128)(2,1)}, bf16[256,1280]{1,0:T(8,128)(2,1)}, u32[]{:S(2)}, u32[]{:S(2)}) collective-permute-start(bf16[256,1280]{1,0:T(8,128)(2,1)} %trunk.3), channel_id=1, source_target_pairs={{0,1},{3,2},{4,5},{7,6},{8,9},{11,10},{12,13},{15,14},{16,17},{19,... | collective-permute-start | bytes 1966088 | tf_op jit(solution)/shard_map/ppermute | solution.py:540
  42.0 4.7 %trunk.4 = (f32[128,2560]{1,0:T(8,128)}, bf16[128,2560]{1,0:T(8,128)(2,1)}) custom-call(bf16[128,128]{1,0:T(8,128)(2,1)S(1)} %collective-permute-done.4.refs_0_, bf16[128,128]{1,0:T(8,128)(2,1)S(1)} %get-tuple-element.18.refs_1_, bf16[64,1280]{1,0:T(8,128)(2,1)S(1)} %add_convert_fusion.4.refs_2_, bf16[1280,1280]{1,0:T(8,128)(2,1)S(1)} %copy-done, ...), custom_call_target="tpu_custom_call" | custom-call | flops 1677721600 | bytes 6553600 | tf_op jit(solution)/shard_map/trunk/pallas_call | solution.py:404
  46.7 2.2 %trunk.5 = bf16[256,1280]{1,0:T(8,128)(2,1)} custom-call(bf16[128,128]{1,0:T(8,128)(2,1)S(1)} %collective-permute-done.2.refs_0_, bf16[128,128]{1,0:T(8,128)(2,1)S(1)} %collective-permute-done.3.refs_1_, bf16[64,1280]{1,0:T(8,128)(2,1)S(1)} %add_convert_fusion.4.refs_2_, bf16[1280,1280]{1,0:T(8,128)(2,1)S(1)} %collective-permute-done.6.refs_5_.refs_6_.refs_3_.refs_4_, ...), custom_call_target="tpu_custom_call" | custom-call | flops 838860800 | bytes 3276800 | tf_op jit(solution)/shard_map/trunk/pallas_call | solution.py:404
  48.9 1.5 %collective-permute-start.8 = (bf16[256,1280]{1,0:T(8,128)(2,1)}, bf16[256,1280]{1,0:T(8,128)(2,1)S(1)}, u32[]{:S(2)}, u32[]{:S(2)}) collective-permute-start(bf16[256,1280]{1,0:T(8,128)(2,1)} %trunk.5), channel_id=1, source_target_pairs={{0,1},{3,2},{4,5},{7,6},{8,9},{11,10},{12,13},{15,14},{16,17},{19,... | collective-permute-start | bytes 1966088 | tf_op jit(solution)/shard_map/ppermute | solution.py:542
  50.4 1.3 %collective-permute-start.7 = (bf16[128,2560]{1,0:T(8,128)(2,1)}, bf16[128,2560]{1,0:T(8,128)(2,1)S(1)}, u32[]{:S(2)}, u32[]{:S(2)}) collective-permute-start(bf16[128,2560]{1,0:T(8,128)(2,1)} %get-tuple-element.28), channel_id=1, source_target_pairs={{1,0},{2,3},{5,4},{6,7},{9,8},{10,11},{13,12},{14,15},{17,16},{18,... | collective-permute-start | bytes 1966088 | tf_op jit(solution)/shard_map/ppermute | solution.py:541
  51.7 4.8 %collective-permute-done.10 = bf16[256,1280]{1,0:T(8,128)(2,1)} collective-permute-done((bf16[256,1280]{1,0:T(8,128)(2,1)}, bf16[256,1280]{1,0:T(8,128)(2,1)}, u32[]{:S(2)}, u32[]{:S(2)}) %collective-permute-start.10) | collective-permute-done | bytes 655392 | tf_op jit(solution)/shard_map/ppermute | solution.py:540
  56.5 1.4 %add_convert_fusion.3 = (bf16[128,1280]{1,0:T(8,128)(2,1)S(1)}, bf16[128,1280]{1,0:T(8,128)(2,1)S(1)}) fusion(bf16[256,1280]{1,0:T(8,128)(2,1)} %collective-permute-done.10, bf16[256,1280]{1,0:T(8,128)(2,1)} %trunk.3), kind=kLoop, calls=%fused_computation.9 | loop fusion | flops 1310720 | bytes 1966080 | tf_op jit(solution)/shard_map/convert_element_type | solution.py:448
  58.6 1.3 %collective-permute-start.12 = (bf16[128,1280]{1,0:T(8,128)(2,1)S(1)}, bf16[128,1280]{1,0:T(8,128)(2,1)S(1)}, u32[]{:S(2)}, u32[]{:S(2)}) collective-permute-start(bf16[128,1280]{1,0:T(8,128)(2,1)S(1)} %get-tuple-element.32), channel_id=1, source_target_pairs={{1,3},{2,0},{5,7},{6,4},{9,11},{10,8},{13,15},{14,12},{17,19},{18,... | collective-permute-start | bytes 983048 | tf_op jit(solution)/shard_map/ppermute | solution.py:551
  59.9 7.6 %collective-permute-done.8 = bf16[256,1280]{1,0:T(8,128)(2,1)S(1)} collective-permute-done((bf16[256,1280]{1,0:T(8,128)(2,1)}, bf16[256,1280]{1,0:T(8,128)(2,1)S(1)}, u32[]{:S(2)}, u32[]{:S(2)}) %collective-permute-start.8) | collective-permute-done | bytes 655392 | tf_op jit(solution)/shard_map/ppermute | solution.py:542
  67.5 4.3 %collective-permute-start.9 = (bf16[128,2560]{1,0:T(8,128)(2,1)S(1)}, bf16[128,2560]{1,0:T(8,128)(2,1)S(1)}, u32[]{:S(2)}, u32[]{:S(2)}) collective-permute-start(bf16[128,2560]{1,0:T(8,128)(2,1)S(1)} %copy-done.5), channel_id=1, source_target_pairs={{0,1},{3,2},{4,5},{7,6},{8,9},{11,10},{12,13},{15,14},{16,17},{19,... | collective-permute-start | bytes 1966088 | tf_op jit(solution)/shard_map/ppermute | solution.py:545
  72.7 1.4 %collective-permute-start.14 = (bf16[128,1280]{1,0:T(8,128)(2,1)S(1)}, bf16[128,1280]{1,0:T(8,128)(2,1)S(1)}, u32[]{:S(2)}, u32[]{:S(2)}) collective-permute-start(bf16[128,1280]{1,0:T(8,128)(2,1)S(1)} %get-tuple-element.34), channel_id=1, source_target_pairs={{1,3},{2,0},{5,7},{6,4},{9,11},{10,8},{13,15},{14,12},{17,19},{18,... | collective-permute-start | bytes 983048 | tf_op jit(solution)/shard_map/ppermute | solution.py:551
  74.2 12.3 %collective-permute-done.14 = bf16[128,1280]{1,0:T(8,128)(2,1)S(1)} collective-permute-done((bf16[128,1280]{1,0:T(8,128)(2,1)S(1)}, bf16[128,1280]{1,0:T(8,128)(2,1)S(1)}, u32[]{:S(2)}, u32[]{:S(2)}) %collective-permute-start.14) | collective-permute-done | bytes 327712 | tf_op jit(solution)/shard_map/ppermute | solution.py:551
  86.9 1.0 %fusion.1 = bf16[1,128,2560]{2,1,0:T(8,128)(2,1)} fusion(bf16[128,2560]{1,0:T(8,128)(2,1)S(1)} %maximum_add_fusion, bf16[128,1280]{1,0:T(8,128)(2,1)S(1)} %get-tuple-element.36, bf16[128,1280]{1,0:T(8,128)(2,1)S(1)} %get-tuple-element.35, pred[]{:T(512)S(6)} %eq.3), kind=kLoop, calls=%fused_computation.3 | loop fusion | flops 1638400 | bytes 1966081 | tf_op jit(solution)/shard_map/broadcast_in_dim | solution.py:559
  (34 shorter events, 4.6 us)
Async XLA Ops:
  0.0 42.0 %collective-permute-start.6 = (bf16[1280,1280]{1,0:T(8,128)(2,1)}, bf16[1280,1280]{1,0:T(8,128)(2,1)S(1)}, u32[]{:S(2)}, u32[]{:S(2)}) collective-permute-start(bf16[1280,1280]{1,0:T(8,128)(2,1)} %refs_4_.3), channel_id=1, source_target_pairs={{0,4},{4,0},{1,5},{5,1},{2,6},{6,2},{3,7},{7,3},{8,12},{12,8},{9,1... | collective-permute-start | bytes 9830408 | tf_op jit(solution)/shard_map/ppermute | solution.py:18
  0.5 6.7 %copy-start.4 = (f32[2560]{0:T(1024)S(1)}, f32[2560]{0:T(1024)}, u32[]{:S(2)}) copy-start(f32[2560]{0:T(1024)} %param.21) | copy-start | bytes 30724
  3.1 10.6 %collective-permute-start = (bf16[144,1024]{1,0:T(8,128)(2,1)}, bf16[144,1024]{1,0:T(8,128)(2,1)}, u32[]{:S(2)}, u32[]{:S(2)}) collective-permute-start(bf16[144,1024]{1,0:T(8,128)(2,1)} %near_rows.1.refs_0_), channel_id=1, source_target_pairs={{0,1},{1,0},{2,3},{3,2},{4,5},{5,4},{6,7},{7,6},{8,9},{9,8},{10,11... | collective-permute-start | bytes 884744 | tf_op jit(solution)/shard_map/ppermute | solution.py:18
  5.7 8.0 %collective-permute-start.1 = (bf16[144,1024]{1,0:T(8,128)(2,1)}, bf16[144,1024]{1,0:T(8,128)(2,1)}, u32[]{:S(2)}, u32[]{:S(2)}) collective-permute-start(bf16[144,1024]{1,0:T(8,128)(2,1)} %near_rows.1.refs_0_), channel_id=1, source_target_pairs={{1,2},{2,1},{5,6},{6,5},{9,10},{10,9},{13,14},{14,13},{17,18},{18,... | collective-permute-start | bytes 884744 | tf_op jit(solution)/shard_map/ppermute | solution.py:475
  11.4 20.7 %collective-permute-start.5 = (f32[64,1280]{1,0:T(8,128)}, f32[64,1280]{1,0:T(8,128)}, u32[]{:S(2)}, u32[]{:S(2)}) collective-permute-start(f32[64,1280]{1,0:T(8,128)} %token_rows.1), channel_id=1, source_target_pairs={{0,4},{4,0},{1,5},{5,1},{2,6},{6,2},{3,7},{7,3},{8,12},{12,8},{9,1... | collective-permute-start | bytes 983048 | tf_op jit(solution)/shard_map/ppermute | solution.py:18
  13.7 18.3 %copy-start.2 = (f32[64,1280]{1,0:T(8,128)S(1)}, f32[64,1280]{1,0:T(8,128)}, u32[]{:S(2)}) copy-start(f32[64,1280]{1,0:T(8,128)} %token_rows.1) | copy-start | bytes 983044
  13.7 21.9 %copy-start = (bf16[1280,1280]{1,0:T(8,128)(2,1)S(1)}, bf16[1280,1280]{1,0:T(8,128)(2,1)}, u32[]{:S(2)}) copy-start(bf16[1280,1280]{1,0:T(8,128)(2,1)} %refs_4_.3) | copy-start | bytes 9830404
  25.5 7.6 %collective-permute-start.2 = (bf16[128,128]{1,0:T(8,128)(2,1)S(1)}, bf16[128,128]{1,0:T(8,128)(2,1)S(1)}, u32[]{:S(2)}, u32[]{:S(2)}) collective-permute-start(bf16[128,128]{1,0:T(8,128)(2,1)S(1)} %get-tuple-element.18.refs_1_), channel_id=1, source_target_pairs={{0,3},{1,2},{2,1},{3,0},{4,7},{5,6},{6,5},{7,4},{8,11},{9,10},{10,... | collective-permute-start | bytes 98312 | tf_op jit(solution)/shard_map/ppermute | solution.py:18
  29.3 4.9 %collective-permute-start.3 = (bf16[128,128]{1,0:T(8,128)(2,1)S(1)}, bf16[128,128]{1,0:T(8,128)(2,1)S(1)}, u32[]{:S(2)}, u32[]{:S(2)}) collective-permute-start(bf16[128,128]{1,0:T(8,128)(2,1)S(1)} %get-tuple-element.18.refs_1_), channel_id=1, source_target_pairs={{0,2},{1,3},{2,0},{3,1},{4,6},{5,7},{6,4},{7,5},{8,10},{9,11},{10,... | collective-permute-start | bytes 98312 | tf_op jit(solution)/shard_map/ppermute | solution.py:18
  31.8 3.9 %collective-permute-start.4 = (bf16[128,128]{1,0:T(8,128)(2,1)S(1)}, bf16[128,128]{1,0:T(8,128)(2,1)S(1)}, u32[]{:S(2)}, u32[]{:S(2)}) collective-permute-start(bf16[128,128]{1,0:T(8,128)(2,1)S(1)} %get-tuple-element.18.refs_1_), channel_id=1, source_target_pairs={{0,1},{1,0},{2,3},{3,2},{4,5},{5,4},{6,7},{7,6},{8,9},{9,8},{10,11... | collective-permute-start | bytes 98312 | tf_op jit(solution)/shard_map/ppermute | solution.py:18
  37.9 18.6 %collective-permute-start.10 = (bf16[256,1280]{1,0:T(8,128)(2,1)}, bf16[256,1280]{1,0:T(8,128)(2,1)}, u32[]{:S(2)}, u32[]{:S(2)}) collective-permute-start(bf16[256,1280]{1,0:T(8,128)(2,1)} %trunk.3), channel_id=1, source_target_pairs={{0,1},{3,2},{4,5},{7,6},{8,9},{11,10},{12,13},{15,14},{16,17},{19,... | collective-permute-start | bytes 1966088 | tf_op jit(solution)/shard_map/ppermute | solution.py:540
  48.9 18.6 %copy-start.5 = (bf16[128,2560]{1,0:T(8,128)(2,1)S(1)}, bf16[128,2560]{1,0:T(8,128)(2,1)}, u32[]{:S(2)}) copy-start(bf16[128,2560]{1,0:T(8,128)(2,1)} %get-tuple-element.28) | copy-start | bytes 1966084
  48.9 22.9 %copy-start.1 = (bf16[256,1280]{1,0:T(8,128)(2,1)S(1)}, bf16[256,1280]{1,0:T(8,128)(2,1)}, u32[]{:S(2)}) copy-start(bf16[256,1280]{1,0:T(8,128)(2,1)} %trunk.5) | copy-start | bytes 1966084
  48.9 18.6 %collective-permute-start.8 = (bf16[256,1280]{1,0:T(8,128)(2,1)}, bf16[256,1280]{1,0:T(8,128)(2,1)S(1)}, u32[]{:S(2)}, u32[]{:S(2)}) collective-permute-start(bf16[256,1280]{1,0:T(8,128)(2,1)} %trunk.5), channel_id=1, source_target_pairs={{0,1},{3,2},{4,5},{7,6},{8,9},{11,10},{12,13},{15,14},{16,17},{19,... | collective-permute-start | bytes 1966088 | tf_op jit(solution)/shard_map/ppermute | solution.py:542
  50.4 36.2 %collective-permute-start.7 = (bf16[128,2560]{1,0:T(8,128)(2,1)}, bf16[128,2560]{1,0:T(8,128)(2,1)S(1)}, u32[]{:S(2)}, u32[]{:S(2)}) collective-permute-start(bf16[128,2560]{1,0:T(8,128)(2,1)} %get-tuple-element.28), channel_id=1, source_target_pairs={{1,0},{2,3},{5,4},{6,7},{9,8},{10,11},{13,12},{14,15},{17,16},{18,... | collective-permute-start | bytes 1966088 | tf_op jit(solution)/shard_map/ppermute | solution.py:541
  57.9 14.8 %collective-permute-start.11 = (bf16[128,1280]{1,0:T(8,128)(2,1)S(1)}, bf16[128,1280]{1,0:T(8,128)(2,1)S(1)}, u32[]{:S(2)}, u32[]{:S(2)}) collective-permute-start(bf16[128,1280]{1,0:T(8,128)(2,1)S(1)} %get-tuple-element.31), channel_id=1, source_target_pairs={{1,2},{2,1},{5,6},{6,5},{9,10},{10,9},{13,14},{14,13},{17,18},{18,... | collective-permute-start | bytes 983048 | tf_op jit(solution)/shard_map/ppermute | solution.py:550
  58.6 15.5 %collective-permute-start.12 = (bf16[128,1280]{1,0:T(8,128)(2,1)S(1)}, bf16[128,1280]{1,0:T(8,128)(2,1)S(1)}, u32[]{:S(2)}, u32[]{:S(2)}) collective-permute-start(bf16[128,1280]{1,0:T(8,128)(2,1)S(1)} %get-tuple-element.32), channel_id=1, source_target_pairs={{1,3},{2,0},{5,7},{6,4},{9,11},{10,8},{13,15},{14,12},{17,19},{18,... | collective-permute-start | bytes 983048 | tf_op jit(solution)/shard_map/ppermute | solution.py:551
  67.5 19.1 %collective-permute-start.9 = (bf16[128,2560]{1,0:T(8,128)(2,1)S(1)}, bf16[128,2560]{1,0:T(8,128)(2,1)S(1)}, u32[]{:S(2)}, u32[]{:S(2)}) collective-permute-start(bf16[128,2560]{1,0:T(8,128)(2,1)S(1)} %copy-done.5), channel_id=1, source_target_pairs={{0,1},{3,2},{4,5},{7,6},{8,9},{11,10},{12,13},{15,14},{16,17},{19,... | collective-permute-start | bytes 1966088 | tf_op jit(solution)/shard_map/ppermute | solution.py:545
  72.0 2.2 %collective-permute-start.13 = (bf16[128,1280]{1,0:T(8,128)(2,1)S(1)}, bf16[128,1280]{1,0:T(8,128)(2,1)S(1)}, u32[]{:S(2)}, u32[]{:S(2)}) collective-permute-start(bf16[128,1280]{1,0:T(8,128)(2,1)S(1)} %get-tuple-element.33), channel_id=1, source_target_pairs={{1,2},{2,1},{5,6},{6,5},{9,10},{10,9},{13,14},{14,13},{17,18},{18,... | collective-permute-start | bytes 983048 | tf_op jit(solution)/shard_map/ppermute | solution.py:550
  72.7 13.9 %copy-start.3 = (f32[128,2560]{1,0:T(8,128)S(1)}, f32[128,2560]{1,0:T(8,128)}, u32[]{:S(2)}) copy-start(f32[128,2560]{1,0:T(8,128)} %get-tuple-element.25) | copy-start | bytes 3932164
  72.7 13.8 %collective-permute-start.14 = (bf16[128,1280]{1,0:T(8,128)(2,1)S(1)}, bf16[128,1280]{1,0:T(8,128)(2,1)S(1)}, u32[]{:S(2)}, u32[]{:S(2)}) collective-permute-start(bf16[128,1280]{1,0:T(8,128)(2,1)S(1)} %get-tuple-element.34), channel_id=1, source_target_pairs={{1,3},{2,0},{5,7},{6,4},{9,11},{10,8},{13,15},{14,12},{17,19},{18,... | collective-permute-start | bytes 983048 | tf_op jit(solution)/shard_map/ppermute | solution.py:551

commit v5 on v4

--- a/solution.py
+++ b/solution.py
@@ -161,7 +161,10 @@
         early.append(
             (ref.at[residues : residues + COORD_ROWS, 0:residues], position_ref.at[slot])
         )
-    early.append((w_rbf_ref, window_ref.at[window : window + bins, :]))
+    groups = LANES // bins
+    for group in range(groups):
+        place = window + group * bins
+        early.append((w_rbf_ref, window_ref.at[place : place + bins, :]))
     early.append((link_ref, link_buf))
     late = [
         (feats_ref, feats_buf),
@@ -178,9 +181,6 @@
     ]
     for copy in copies:
         copy.start()
-    window_ref[window + bins :, :] = jnp.zeros(
-        (window_ref.shape[0] - window - bins, feature_dim), BF16
-    )
     for copy in copies[: len(early)]:
         copy.wait()
 
@@ -196,7 +196,10 @@
         )
     )
     lane = lax.broadcasted_iota(jnp.int32, (rows_at_once, LANES), 1)
-    centres = 2.0 + (20.0 / (bins - 1)) * lane.astype(F32)
+    bin_of = jnp.bitwise_and(lane, bins - 1)
+    group_of = lax.shift_right_logical(lane, bins.bit_length() - 1)
+    group_short = group_of.astype(jnp.int16)
+    centres = 2.0 + (20.0 / (bins - 1)) * bin_of.astype(F32)
 
     lane_short = lane.astype(jnp.int16)
     one, zero = jnp.ones((), BF16), jnp.zeros((), BF16)
@@ -230,10 +233,11 @@
                 jnp.where(place_k == lane_short + jnp.int16(slot * residues), one, zero)
                 for slot in range(3)
             ]
-            distance_k = jnp.broadcast_to(distance[:, k : k + 1], (rows_at_once, LANES))
-            scaled = (distance_k - centres) * (1.0 / 1.25)
-            radial = jnp.where(lane < bins, jnp.exp(-scaled * scaled), 0.0)
-            parts.append(radial.astype(BF16))
+            if k % groups == 0:
+                spread_out = jnp.take_along_axis(distance, group_of + k, axis=1)
+                scaled = (spread_out - centres) * (1.0 / 1.25)
+                radial = jnp.exp(-scaled * scaled).astype(BF16)
+            parts.append(jnp.where(group_short == jnp.int16(k % groups), radial, zero))
             rows.append(jnp.concatenate(parts, axis=1))
         selector = jnp.concatenate(rows, axis=0)
         width = 256
@@ -294,7 +298,7 @@
     residues, feature_dim = feats.shape
     embed_dim = table.shape[1]
     bins = w_rbf.shape[0]
-    depth = -(-(3 * residues + bins) // 256) * 256
+    depth = 3 * residues + LANES
     count = rows[1] - rows[0]
     in_vmem = pl.BlockSpec(memory_space=pltpu.VMEM)
     in_hbm_spec = pl.BlockSpec(memory_space=pltpu.HBM)
@@ -311,7 +315,7 @@
         pltpu.VMEM((residues, LANES), jnp.int32),
         pltpu.VMEM((residues, LANES), F32),
         pltpu.VMEM((count, feature_dim), F32),
-        pltpu.SemaphoreType.DMA((16,)),
+        pltpu.SemaphoreType.DMA((12 + LANES // bins,)),
     ]
     if tokens:
         token_gain, w_up = tokens
@@ -547,9 +551,9 @@
     for far, arrived in ((far_a, arrived_a), (far_b, arrived_b)):
         across = rounded_sum(far[:residues], arrived[residues:])
         beyond = rounded_sum(far[residues:], arrived[:residues])
+        beyond = lax.ppermute(beyond, "mp", skipping)
         across = lax.ppermute(across, "mp", crossing)
-        beyond = lax.ppermute(beyond, "mp", skipping)
-        sums.append(across.astype(F32) + beyond.astype(F32))
+        sums.append(beyond.astype(F32) + across.astype(F32))
     total = base + to_edge.astype(F32) + to_inner.astype(F32)
     total = total + jnp.concatenate(sums, axis=1)
     if len(whole) == 2:

time: 88.3 us -> 87.5 us (level); the launches traced: 87.9 us -> 86 us
  waiting for transfers between devices: 28.7 us -> 27.2 us
    ppermute x2, waiting for transfers between devices: 12.3 us -> 10.5 us  [on_device(): beyond = lax.ppermute(beyond, 'mp', skipping)]
where the time goes in v5:
time: 87.5 us; the launch traced here: 86 us
  waiting for transfers between devices  27.2 us (31%)
  Pallas kernels  26.9 us (31%)
  starting transfers between devices  26.3 us (30%)
  other arithmetic  4.05 us (5%)
  between operations  0.89 us (1%)
    pallas_call x1, Pallas kernels, messages(): pl.pallas_call(functools.partial(message_kernel, min(32, count), rows[0],...  11.6 us
    ppermute x2, waiting for transfers between devices, on_device(): beyond = lax.ppermute(beyond, 'mp', skipping)  10.5 us
    ppermute x6, starting transfers between devices, swap(): return lax.ppermute(value, axis, [(i, i ^ step) for i in range(count)])  9.87 us
    pallas_call x3, Pallas kernels, trunk(): pl.pallas_call(functools.partial(trunk_kernel, len(coded), [column for _,...  9.07 us
    ppermute x1, waiting for transfers between devices, on_device(): arrived_b = lax.ppermute(far_b, 'mp', inward)  7.62 us
    ppermute x1, waiting for transfers between devices, on_device(): arrived_a = lax.ppermute(far_a, 'mp', inward)  4.96 us
    ppermute x1, starting transfers between devices, on_device(): to_inner = lax.ppermute(near, 'mp', inward)  4.31 us
    ppermute x6, waiting for transfers between devices, swap(): return lax.ppermute(value, axis, [(i, i ^ step) for i in range(count)])  4.06 us
  transfers between devices with their start and end apart: 15, of which 6 were waited for; matrix products, arithmetic and copies ran while one was open for 4% of the time, Pallas kernels for 31%

profile of v5, /device:TPU:0, one launch (start us, length us, event | category | flops | bytes accessed | tf_op | source)
XLA Modules:
  0.0 86.0 jit_solution(6166596164189649158)
XLA Ops:
  0.5 2.6 %near_rows.1.refs_0_ = bf16[144,1024]{1,0:T(8,128)(2,1)} custom-call(bf16[128,1024]{1,0:T(8,128)(2,1)} %bitcast.11, bf16[3,128]{1,0:T(4,128)(2,1)} %bitcast.13, bf16[1024,1024]{1,0:T(8,128)(2,1)} %w_near_ref.1), custom_call_target="tpu_custom_call" | custom-call | tf_op jit(solution)/shard_map/near_rows/pallas_call | solution.py:66
  3.1 2.6 %collective-permute-start = (bf16[144,1024]{1,0:T(8,128)(2,1)}, bf16[144,1024]{1,0:T(8,128)(2,1)}, u32[]{:S(2)}, u32[]{:S(2)}) collective-permute-start(bf16[144,1024]{1,0:T(8,128)(2,1)} %near_rows.1.refs_0_), channel_id=1, source_target_pairs={{0,1},{1,0},{2,3},{3,2},{4,5},{5,4},{6,7},{7,6},{8,9},{9,8},{10,11... | collective-permute-start | bytes 884744 | tf_op jit(solution)/shard_map/ppermute | solution.py:18
  5.7 1.4 %collective-permute-start.1 = (bf16[144,1024]{1,0:T(8,128)(2,1)}, bf16[144,1024]{1,0:T(8,128)(2,1)}, u32[]{:S(2)}, u32[]{:S(2)}) collective-permute-start(bf16[144,1024]{1,0:T(8,128)(2,1)} %near_rows.1.refs_0_), channel_id=1, source_target_pairs={{1,2},{2,1},{5,6},{6,5},{9,10},{10,9},{13,14},{14,13},{17,18},{18,... | collective-permute-start | bytes 884744 | tf_op jit(solution)/shard_map/ppermute | solution.py:479
  7.8 3.6 %token_rows.1 = f32[64,1280]{1,0:T(8,128)} custom-call(s32[1]{0:T(128)} %bitcast.7.turn_ref.refs_8_, bf16[33,2560]{1,0:T(8,128)(2,1)} %refs_9_.1, f32[1,2560]{1,0:T(1,128)} %broadcast_in_dim.12.gain_ref, bf16[1280,1280]{1,0:T(8,128)(2,1)} %w_up_ref.1), custom_call_target="tpu_custom_call" | custom-call | tf_op jit(solution)/shard_map/token_rows/pallas_call | solution.py:94
  12.3 1.4 %collective-permute-done.refs_1_ = bf16[144,1024]{1,0:T(8,128)(2,1)} collective-permute-done((bf16[144,1024]{1,0:T(8,128)(2,1)}, bf16[144,1024]{1,0:T(8,128)(2,1)}, u32[]{:S(2)}, u32[]{:S(2)}) %collective-permute-start) | collective-permute-done | bytes 294944 | tf_op jit(solution)/shard_map/ppermute | solution.py:18
  13.7 11.6 %messages.1 = (bf16[128,128]{1,0:T(8,128)(2,1)S(1)}, bf16[128,128]{1,0:T(8,128)(2,1)S(1)}) custom-call(bf16[144,1024]{1,0:T(8,128)(2,1)} %near_rows.1.refs_0_, bf16[144,1024]{1,0:T(8,128)(2,1)} %collective-permute-done.refs_1_, bf16[144,1024]{1,0:T(8,128)(2,1)} %collective-permute-done.1.refs_2_, bf16[128,1024]{1,0:T(8,128)(2,1)} %bitcast.12, ...), custom_call_target="tpu_custom_call" | custom-call | flops 12800000000 | bytes 5000000 | tf_op jit(solution)/shard_map/messages/pallas_call | solution.py:328
  25.3 3.8 %collective-permute-start.2 = (bf16[128,128]{1,0:T(8,128)(2,1)S(1)}, bf16[128,128]{1,0:T(8,128)(2,1)S(1)}, u32[]{:S(2)}, u32[]{:S(2)}) collective-permute-start(bf16[128,128]{1,0:T(8,128)(2,1)S(1)} %get-tuple-element.18.refs_1_), channel_id=1, source_target_pairs={{0,3},{1,2},{2,1},{3,0},{4,7},{5,6},{6,5},{7,4},{8,11},{9,10},{10,... | collective-permute-start | bytes 98312 | tf_op jit(solution)/shard_map/ppermute | solution.py:18
  29.2 2.5 %collective-permute-start.3 = (bf16[128,128]{1,0:T(8,128)(2,1)S(1)}, bf16[128,128]{1,0:T(8,128)(2,1)S(1)}, u32[]{:S(2)}, u32[]{:S(2)}) collective-permute-start(bf16[128,128]{1,0:T(8,128)(2,1)S(1)} %get-tuple-element.18.refs_1_), channel_id=1, source_target_pairs={{0,2},{1,3},{2,0},{3,1},{4,6},{5,7},{6,4},{7,5},{8,10},{9,11},{10,... | collective-permute-start | bytes 98312 | tf_op jit(solution)/shard_map/ppermute | solution.py:18
  32.9 1.2 %collective-permute-done.3.refs_1_ = bf16[128,128]{1,0:T(8,128)(2,1)S(1)} collective-permute-done((bf16[128,128]{1,0:T(8,128)(2,1)S(1)}, bf16[128,128]{1,0:T(8,128)(2,1)S(1)}, u32[]{:S(2)}, u32[]{:S(2)}) %collective-permute-start.3) | collective-permute-done | bytes 32800 | tf_op jit(solution)/shard_map/ppermute | solution.py:18
  34.1 1.5 %collective-permute-done.4.refs_0_ = bf16[128,128]{1,0:T(8,128)(2,1)S(1)} collective-permute-done((bf16[128,128]{1,0:T(8,128)(2,1)S(1)}, bf16[128,128]{1,0:T(8,128)(2,1)S(1)}, u32[]{:S(2)}, u32[]{:S(2)}) %collective-permute-start.4) | collective-permute-done | bytes 32800 | tf_op jit(solution)/shard_map/ppermute | solution.py:18
  35.6 2.2 %trunk.3 = bf16[256,1280]{1,0:T(8,128)(2,1)} custom-call(bf16[128,128]{1,0:T(8,128)(2,1)S(1)} %collective-permute-done.2.refs_0_, bf16[128,128]{1,0:T(8,128)(2,1)S(1)} %collective-permute-done.3.refs_1_, bf16[64,1280]{1,0:T(8,128)(2,1)S(1)} %add_convert_fusion.4.refs_2_, bf16[1280,1280]{1,0:T(8,128)(2,1)S(1)} %copy-done, bf16[1280,1280]{1,0:T(8,128)(2,1)S(1)} %copy-done), custom_call_target="tpu_custom_call" | custom-call | flops 838860800 | bytes 3276800 | tf_op jit(solution)/shard_map/trunk/pallas_call | solution.py:408
  37.8 3.9 %collective-permute-start.10 = (bf16[256,1280]{1,0:T(8,128)(2,1)}, bf16[256,1280]{1,0:T(8,128)(2,1)}, u32[]{:S(2)}, u32[]{:S(2)}) collective-permute-start(bf16[256,1280]{1,0:T(8,128)(2,1)} %trunk.3), channel_id=1, source_target_pairs={{0,1},{3,2},{4,5},{7,6},{8,9},{11,10},{12,13},{15,14},{16,17},{19,... | collective-permute-start | bytes 1966088 | tf_op jit(solution)/shard_map/ppermute | solution.py:544
  41.7 4.7 %trunk.4 = (f32[128,2560]{1,0:T(8,128)}, bf16[128,2560]{1,0:T(8,128)(2,1)}) custom-call(bf16[128,128]{1,0:T(8,128)(2,1)S(1)} %collective-permute-done.4.refs_0_, bf16[128,128]{1,0:T(8,128)(2,1)S(1)} %get-tuple-element.18.refs_1_, bf16[64,1280]{1,0:T(8,128)(2,1)S(1)} %add_convert_fusion.4.refs_2_, bf16[1280,1280]{1,0:T(8,128)(2,1)S(1)} %copy-done, ...), custom_call_target="tpu_custom_call" | custom-call | flops 1677721600 | bytes 6553600 | tf_op jit(solution)/shard_map/trunk/pallas_call | solution.py:408
  46.4 2.2 %trunk.5 = bf16[256,1280]{1,0:T(8,128)(2,1)} custom-call(bf16[128,128]{1,0:T(8,128)(2,1)S(1)} %collective-permute-done.2.refs_0_, bf16[128,128]{1,0:T(8,128)(2,1)S(1)} %collective-permute-done.3.refs_1_, bf16[64,1280]{1,0:T(8,128)(2,1)S(1)} %add_convert_fusion.4.refs_2_, bf16[1280,1280]{1,0:T(8,128)(2,1)S(1)} %collective-permute-done.6.refs_5_.refs_6_.refs_3_.refs_4_, ...), custom_call_target="tpu_custom_call" | custom-call | flops 838860800 | bytes 3276800 | tf_op jit(solution)/shard_map/trunk/pallas_call | solution.py:408
  48.6 1.5 %collective-permute-start.8 = (bf16[256,1280]{1,0:T(8,128)(2,1)}, bf16[256,1280]{1,0:T(8,128)(2,1)S(1)}, u32[]{:S(2)}, u32[]{:S(2)}) collective-permute-start(bf16[256,1280]{1,0:T(8,128)(2,1)} %trunk.5), channel_id=1, source_target_pairs={{0,1},{3,2},{4,5},{7,6},{8,9},{11,10},{12,13},{15,14},{16,17},{19,... | collective-permute-start | bytes 1966088 | tf_op jit(solution)/shard_map/ppermute | solution.py:546
  50.0 1.3 %collective-permute-start.7 = (bf16[128,2560]{1,0:T(8,128)(2,1)}, bf16[128,2560]{1,0:T(8,128)(2,1)S(1)}, u32[]{:S(2)}, u32[]{:S(2)}) collective-permute-start(bf16[128,2560]{1,0:T(8,128)(2,1)} %get-tuple-element.28), channel_id=1, source_target_pairs={{1,0},{2,3},{5,4},{6,7},{9,8},{10,11},{13,12},{14,15},{17,16},{18,... | collective-permute-start | bytes 1966088 | tf_op jit(solution)/shard_map/ppermute | solution.py:545
  51.3 5.0 %collective-permute-done.10 = bf16[256,1280]{1,0:T(8,128)(2,1)} collective-permute-done((bf16[256,1280]{1,0:T(8,128)(2,1)}, bf16[256,1280]{1,0:T(8,128)(2,1)}, u32[]{:S(2)}, u32[]{:S(2)}) %collective-permute-start.10) | collective-permute-done | bytes 655392 | tf_op jit(solution)/shard_map/ppermute | solution.py:544
  56.3 1.4 %add_convert_fusion.3 = (bf16[128,1280]{1,0:T(8,128)(2,1)S(1)}, bf16[128,1280]{1,0:T(8,128)(2,1)S(1)}) fusion(bf16[256,1280]{1,0:T(8,128)(2,1)} %collective-permute-done.10, bf16[256,1280]{1,0:T(8,128)(2,1)} %trunk.3), kind=kLoop, calls=%fused_computation.9 | loop fusion | flops 1310720 | bytes 1966080 | tf_op jit(solution)/shard_map/convert_element_type | solution.py:452
  57.7 1.3 %collective-permute-start.11 = (bf16[128,1280]{1,0:T(8,128)(2,1)S(1)}, bf16[128,1280]{1,0:T(8,128)(2,1)S(1)}, u32[]{:S(2)}, u32[]{:S(2)}) collective-permute-start(bf16[128,1280]{1,0:T(8,128)(2,1)S(1)} %get-tuple-element.31), channel_id=1, source_target_pairs={{1,3},{2,0},{5,7},{6,4},{9,11},{10,8},{13,15},{14,12},{17,19},{18,... | collective-permute-start | bytes 983048 | tf_op jit(solution)/shard_map/ppermute | solution.py:554
  59.7 7.6 %collective-permute-done.8 = bf16[256,1280]{1,0:T(8,128)(2,1)S(1)} collective-permute-done((bf16[256,1280]{1,0:T(8,128)(2,1)}, bf16[256,1280]{1,0:T(8,128)(2,1)S(1)}, u32[]{:S(2)}, u32[]{:S(2)}) %collective-permute-start.8) | collective-permute-done | bytes 655392 | tf_op jit(solution)/shard_map/ppermute | solution.py:546
  67.3 4.3 %collective-permute-start.9 = (bf16[128,2560]{1,0:T(8,128)(2,1)S(1)}, bf16[128,2560]{1,0:T(8,128)(2,1)S(1)}, u32[]{:S(2)}, u32[]{:S(2)}) collective-permute-start(bf16[128,2560]{1,0:T(8,128)(2,1)S(1)} %copy-done.5), channel_id=1, source_target_pairs={{0,1},{3,2},{4,5},{7,6},{8,9},{11,10},{12,13},{15,14},{16,17},{19,... | collective-permute-start | bytes 1966088 | tf_op jit(solution)/shard_map/ppermute | solution.py:549
  71.8 1.3 %collective-permute-start.13 = (bf16[128,1280]{1,0:T(8,128)(2,1)S(1)}, bf16[128,1280]{1,0:T(8,128)(2,1)S(1)}, u32[]{:S(2)}, u32[]{:S(2)}) collective-permute-start(bf16[128,1280]{1,0:T(8,128)(2,1)S(1)} %get-tuple-element.33), channel_id=1, source_target_pairs={{1,3},{2,0},{5,7},{6,4},{9,11},{10,8},{13,15},{14,12},{17,19},{18,... | collective-permute-start | bytes 983048 | tf_op jit(solution)/shard_map/ppermute | solution.py:554
  74.1 10.5 %collective-permute-done.13 = bf16[128,1280]{1,0:T(8,128)(2,1)S(1)} collective-permute-done((bf16[128,1280]{1,0:T(8,128)(2,1)S(1)}, bf16[128,1280]{1,0:T(8,128)(2,1)S(1)}, u32[]{:S(2)}, u32[]{:S(2)}) %collective-permute-start.13) | collective-permute-done | bytes 327712 | tf_op jit(solution)/shard_map/ppermute | solution.py:554
  85.0 1.0 %fusion.1 = bf16[1,128,2560]{2,1,0:T(8,128)(2,1)} fusion(bf16[128,2560]{1,0:T(8,128)(2,1)S(1)} %maximum_add_fusion, bf16[128,1280]{1,0:T(8,128)(2,1)S(1)} %get-tuple-element.36, bf16[128,1280]{1,0:T(8,128)(2,1)S(1)} %get-tuple-element.35, pred[]{:T(512)S(6)} %eq.3), kind=kLoop, calls=%fused_computation.3 | loop fusion | flops 1638400 | bytes 1966081 | tf_op jit(solution)/shard_map/broadcast_in_dim | solution.py:563
  (34 shorter events, 4.7 us)
Async XLA Ops:
  0.0 41.6 %collective-permute-start.6 = (bf16[1280,1280]{1,0:T(8,128)(2,1)}, bf16[1280,1280]{1,0:T(8,128)(2,1)S(1)}, u32[]{:S(2)}, u32[]{:S(2)}) collective-permute-start(bf16[1280,1280]{1,0:T(8,128)(2,1)} %refs_4_.3), channel_id=1, source_target_pairs={{0,4},{4,0},{1,5},{5,1},{2,6},{6,2},{3,7},{7,3},{8,12},{12,8},{9,1... | collective-permute-start | bytes 9830408 | tf_op jit(solution)/shard_map/ppermute | solution.py:18
  0.5 6.7 %copy-start.4 = (f32[2560]{0:T(1024)S(1)}, f32[2560]{0:T(1024)}, u32[]{:S(2)}) copy-start(f32[2560]{0:T(1024)} %param.21) | copy-start | bytes 30724
  3.1 10.6 %collective-permute-start = (bf16[144,1024]{1,0:T(8,128)(2,1)}, bf16[144,1024]{1,0:T(8,128)(2,1)}, u32[]{:S(2)}, u32[]{:S(2)}) collective-permute-start(bf16[144,1024]{1,0:T(8,128)(2,1)} %near_rows.1.refs_0_), channel_id=1, source_target_pairs={{0,1},{1,0},{2,3},{3,2},{4,5},{5,4},{6,7},{7,6},{8,9},{9,8},{10,11... | collective-permute-start | bytes 884744 | tf_op jit(solution)/shard_map/ppermute | solution.py:18
  5.7 8.0 %collective-permute-start.1 = (bf16[144,1024]{1,0:T(8,128)(2,1)}, bf16[144,1024]{1,0:T(8,128)(2,1)}, u32[]{:S(2)}, u32[]{:S(2)}) collective-permute-start(bf16[144,1024]{1,0:T(8,128)(2,1)} %near_rows.1.refs_0_), channel_id=1, source_target_pairs={{1,2},{2,1},{5,6},{6,5},{9,10},{10,9},{13,14},{14,13},{17,18},{18,... | collective-permute-start | bytes 884744 | tf_op jit(solution)/shard_map/ppermute | solution.py:479
  11.4 20.5 %collective-permute-start.5 = (f32[64,1280]{1,0:T(8,128)}, f32[64,1280]{1,0:T(8,128)}, u32[]{:S(2)}, u32[]{:S(2)}) collective-permute-start(f32[64,1280]{1,0:T(8,128)} %token_rows.1), channel_id=1, source_target_pairs={{0,4},{4,0},{1,5},{5,1},{2,6},{6,2},{3,7},{7,3},{8,12},{12,8},{9,1... | collective-permute-start | bytes 983048 | tf_op jit(solution)/shard_map/ppermute | solution.py:18
  13.7 18.1 %copy-start.2 = (f32[64,1280]{1,0:T(8,128)S(1)}, f32[64,1280]{1,0:T(8,128)}, u32[]{:S(2)}) copy-start(f32[64,1280]{1,0:T(8,128)} %token_rows.1) | copy-start | bytes 983044
  13.7 21.8 %copy-start = (bf16[1280,1280]{1,0:T(8,128)(2,1)S(1)}, bf16[1280,1280]{1,0:T(8,128)(2,1)}, u32[]{:S(2)}) copy-start(bf16[1280,1280]{1,0:T(8,128)(2,1)} %refs_4_.3) | copy-start | bytes 9830404
  25.3 7.6 %collective-permute-start.2 = (bf16[128,128]{1,0:T(8,128)(2,1)S(1)}, bf16[128,128]{1,0:T(8,128)(2,1)S(1)}, u32[]{:S(2)}, u32[]{:S(2)}) collective-permute-start(bf16[128,128]{1,0:T(8,128)(2,1)S(1)} %get-tuple-element.18.refs_1_), channel_id=1, source_target_pairs={{0,3},{1,2},{2,1},{3,0},{4,7},{5,6},{6,5},{7,4},{8,11},{9,10},{10,... | collective-permute-start | bytes 98312 | tf_op jit(solution)/shard_map/ppermute | solution.py:18
  29.2 4.9 %collective-permute-start.3 = (bf16[128,128]{1,0:T(8,128)(2,1)S(1)}, bf16[128,128]{1,0:T(8,128)(2,1)S(1)}, u32[]{:S(2)}, u32[]{:S(2)}) collective-permute-start(bf16[128,128]{1,0:T(8,128)(2,1)S(1)} %get-tuple-element.18.refs_1_), channel_id=1, source_target_pairs={{0,2},{1,3},{2,0},{3,1},{4,6},{5,7},{6,4},{7,5},{8,10},{9,11},{10,... | collective-permute-start | bytes 98312 | tf_op jit(solution)/shard_map/ppermute | solution.py:18
  31.6 3.9 %collective-permute-start.4 = (bf16[128,128]{1,0:T(8,128)(2,1)S(1)}, bf16[128,128]{1,0:T(8,128)(2,1)S(1)}, u32[]{:S(2)}, u32[]{:S(2)}) collective-permute-start(bf16[128,128]{1,0:T(8,128)(2,1)S(1)} %get-tuple-element.18.refs_1_), channel_id=1, source_target_pairs={{0,1},{1,0},{2,3},{3,2},{4,5},{5,4},{6,7},{7,6},{8,9},{9,8},{10,11... | collective-permute-start | bytes 98312 | tf_op jit(solution)/shard_map/ppermute | solution.py:18
  37.8 18.5 %collective-permute-start.10 = (bf16[256,1280]{1,0:T(8,128)(2,1)}, bf16[256,1280]{1,0:T(8,128)(2,1)}, u32[]{:S(2)}, u32[]{:S(2)}) collective-permute-start(bf16[256,1280]{1,0:T(8,128)(2,1)} %trunk.3), channel_id=1, source_target_pairs={{0,1},{3,2},{4,5},{7,6},{8,9},{11,10},{12,13},{15,14},{16,17},{19,... | collective-permute-start | bytes 1966088 | tf_op jit(solution)/shard_map/ppermute | solution.py:544
  48.5 18.8 %copy-start.5 = (bf16[128,2560]{1,0:T(8,128)(2,1)S(1)}, bf16[128,2560]{1,0:T(8,128)(2,1)}, u32[]{:S(2)}) copy-start(bf16[128,2560]{1,0:T(8,128)(2,1)} %get-tuple-element.28) | copy-start | bytes 1966084
  48.5 23.1 %copy-start.1 = (bf16[256,1280]{1,0:T(8,128)(2,1)S(1)}, bf16[256,1280]{1,0:T(8,128)(2,1)}, u32[]{:S(2)}) copy-start(bf16[256,1280]{1,0:T(8,128)(2,1)} %trunk.5) | copy-start | bytes 1966084
  48.6 18.8 %collective-permute-start.8 = (bf16[256,1280]{1,0:T(8,128)(2,1)}, bf16[256,1280]{1,0:T(8,128)(2,1)S(1)}, u32[]{:S(2)}, u32[]{:S(2)}) collective-permute-start(bf16[256,1280]{1,0:T(8,128)(2,1)} %trunk.5), channel_id=1, source_target_pairs={{0,1},{3,2},{4,5},{7,6},{8,9},{11,10},{12,13},{15,14},{16,17},{19,... | collective-permute-start | bytes 1966088 | tf_op jit(solution)/shard_map/ppermute | solution.py:546
  50.0 34.6 %collective-permute-start.7 = (bf16[128,2560]{1,0:T(8,128)(2,1)}, bf16[128,2560]{1,0:T(8,128)(2,1)S(1)}, u32[]{:S(2)}, u32[]{:S(2)}) collective-permute-start(bf16[128,2560]{1,0:T(8,128)(2,1)} %get-tuple-element.28), channel_id=1, source_target_pairs={{1,0},{2,3},{5,4},{6,7},{9,8},{10,11},{13,12},{14,15},{17,16},{18,... | collective-permute-start | bytes 1966088 | tf_op jit(solution)/shard_map/ppermute | solution.py:545
  57.7 15.4 %collective-permute-start.11 = (bf16[128,1280]{1,0:T(8,128)(2,1)S(1)}, bf16[128,1280]{1,0:T(8,128)(2,1)S(1)}, u32[]{:S(2)}, u32[]{:S(2)}) collective-permute-start(bf16[128,1280]{1,0:T(8,128)(2,1)S(1)} %get-tuple-element.31), channel_id=1, source_target_pairs={{1,3},{2,0},{5,7},{6,4},{9,11},{10,8},{13,15},{14,12},{17,19},{18,... | collective-permute-start | bytes 983048 | tf_op jit(solution)/shard_map/ppermute | solution.py:554
  59.0 14.9 %collective-permute-start.12 = (bf16[128,1280]{1,0:T(8,128)(2,1)S(1)}, bf16[128,1280]{1,0:T(8,128)(2,1)S(1)}, u32[]{:S(2)}, u32[]{:S(2)}) collective-permute-start(bf16[128,1280]{1,0:T(8,128)(2,1)S(1)} %get-tuple-element.32), channel_id=1, source_target_pairs={{1,2},{2,1},{5,6},{6,5},{9,10},{10,9},{13,14},{14,13},{17,18},{18,... | collective-permute-start | bytes 983048 | tf_op jit(solution)/shard_map/ppermute | solution.py:555
  67.3 17.3 %collective-permute-start.9 = (bf16[128,2560]{1,0:T(8,128)(2,1)S(1)}, bf16[128,2560]{1,0:T(8,128)(2,1)S(1)}, u32[]{:S(2)}, u32[]{:S(2)}) collective-permute-start(bf16[128,2560]{1,0:T(8,128)(2,1)S(1)} %copy-done.5), channel_id=1, source_target_pairs={{0,1},{3,2},{4,5},{7,6},{8,9},{11,10},{12,13},{15,14},{16,17},{19,... | collective-permute-start | bytes 1966088 | tf_op jit(solution)/shard_map/ppermute | solution.py:549
  71.8 12.7 %collective-permute-start.13 = (bf16[128,1280]{1,0:T(8,128)(2,1)S(1)}, bf16[128,1280]{1,0:T(8,128)(2,1)S(1)}, u32[]{:S(2)}, u32[]{:S(2)}) collective-permute-start(bf16[128,1280]{1,0:T(8,128)(2,1)S(1)} %get-tuple-element.33), channel_id=1, source_target_pairs={{1,3},{2,0},{5,7},{6,4},{9,11},{10,8},{13,15},{14,12},{17,19},{18,... | collective-permute-start | bytes 983048 | tf_op jit(solution)/shard_map/ppermute | solution.py:554
  73.1 11.5 %copy-start.3 = (f32[128,2560]{1,0:T(8,128)S(1)}, f32[128,2560]{1,0:T(8,128)}, u32[]{:S(2)}) copy-start(f32[128,2560]{1,0:T(8,128)} %get-tuple-element.25) | copy-start | bytes 3932164
  73.1 11.4 %collective-permute-start.14 = (bf16[128,1280]{1,0:T(8,128)(2,1)S(1)}, bf16[128,1280]{1,0:T(8,128)(2,1)S(1)}, u32[]{:S(2)}, u32[]{:S(2)}) collective-permute-start(bf16[128,1280]{1,0:T(8,128)(2,1)S(1)} %get-tuple-element.34), channel_id=1, source_target_pairs={{1,2},{2,1},{5,6},{6,5},{9,10},{10,9},{13,14},{14,13},{17,18},{18,... | collective-permute-start | bytes 983048 | tf_op jit(solution)/shard_map/ppermute | solution.py:555
